TPU v7x, 512 devices: a whole 4x8x8 slice. The times are simulated.
512 devices in a mesh: mem: 32 (over x, z), lat: 4 (over y_lo, core), lon: 4 (over y_hi).
Axes of the slice: x: 4, y: 8 (y_hi: 4, y_lo: 2; y = y_hi * 2 + y_lo), z: 8, core: 2. Of those that a mesh axis runs over, the one named last changes fastest.
Arguments:
- perturb: float32 [64, 1536, 2048], P('mem', 'lat', 'lon'), may hold values from -6 to 6
- loc_lat: float32 [384], replicated, may hold values from 1 to 96
- loc_lon: float32 [512], replicated, may hold values from 1 to 128
- obs_cell: int32 [4, 4, 2048], P('lat', 'lon'), may hold values from 0 to 196607
- obs_count: int32 [4, 4], P('lat', 'lon'), may hold values from 512 to 2048, as said below
- obs_innov: float32 [4, 4, 2048], P('lat', 'lon'), may hold values from -8 to 8
- obs_error: float32 [4, 4, 2048], P('lat', 'lon'), may hold values from 0.5 to 4
Outputs:
- analysis: float32 [64, 384, 512], P('mem', 'lat', 'lon')
- increment: float32 [1536, 2048], P('lat', 'lon')
Inputs may be any that keep to these rules, and one draw needn't show every extreme that they name: `obs_cell`: cells may repeat within a tile. `obs_count`: in every draw at least one tile uses all 2048 slots.
All inputs are finite; a program needn't handle non-finite values.
Results may differ from a plain program's by a relative error of at most 0.0001.
Values sent between devices are 32-bit elements; how exact they have to be, the bound alone decides.
No kernel may reach another device: no remote copies, remote signals or barrier semaphores. Data moves between devices by JAX's collectives and lax.ppermute only.
A program may use at most 64 MiB of HBM per device.

v0:
```python
import math

import jax
import jax.numpy as jnp
from jax import lax
from jax.sharding import Mesh
from jax.sharding import PartitionSpec as P

ITERS = 2
MEM = ("mem_0", "mem_1")
LAT = ("lat_0", "lat_1")
MEM_LAT_LON = ("mem_0", "mem_1", "lat_0", "lat_1", "lon")
LAT_LON = ("lat_0", "lat_1", "lon")


huber_width = 1.0
tiny_floor = 1e-06
highest = lax.Precision.HIGHEST


def sent_to_all(x, axis):
    copies = jnp.broadcast_to(x, (lax.axis_size(axis), *x.shape))
    return lax.all_to_all(copies, axis, split_axis=0, concat_axis=0, tiled=True)


def in_order(pieces, dim):
    pieces = jnp.moveaxis(pieces, 0, dim)
    lengths = pieces.shape
    return pieces.reshape(*lengths[:dim], lengths[dim] * lengths[dim + 1], *lengths[dim + 2 :])


def collect(x, axis, dim):
    pieces = sent_to_all(x, axis)
    return in_order(pieces, dim)


def split_up(x, dim, size):
    lengths = x.shape
    pieces = x.reshape(*lengths[:dim], size, lengths[dim] // size, *lengths[dim + 1 :])
    return jnp.moveaxis(pieces, dim, 0)


def summed_on_arrival(x, axis, dim):
    size = lax.axis_size(axis)
    pieces = lax.all_to_all(split_up(x, dim, size), axis, 0, 0, tiled=True)
    return jnp.sum(pieces, axis=0)


def by_axis(x, axes):
    for axis in axes:
        x = lax.psum(x, axis)
    return x


def taken_together(x, axis):
    everything = sent_to_all(x, axis)
    return jnp.sum(everything, axis=0)


def rows_for(lines, size):
    spare = -lines.shape[0] % size
    if not spare:
        return lines
    return jnp.concatenate([lines, jnp.zeros((spare, *lines.shape[1:]), lines.dtype)])


def nested_sum(x, axes):
    lines = x.reshape(-1, x.shape[-1])
    padded = rows_for(lines, lax.axis_size(axes))
    whole = collect(summed_on_arrival(padded, axes, 0), axes, 0)
    return lax.slice_in_dim(whole, 0, len(lines)).reshape(x.shape)


def kernel_rows(scales, first_row, row_count):
    total_rows = scales.shape[0]
    row_index = first_row + jnp.arange(row_count, dtype=jnp.int32)
    inside = (row_index >= 0) & (row_index < total_rows)
    row_scale = scales[jnp.clip(row_index, 0, total_rows - 1)]
    col_index = jnp.arange(total_rows, dtype=jnp.int32)
    offset = (row_index[:, None] - col_index[None, :]).astype(jnp.float32)
    spread = row_scale[:, None] ** 2 + scales[None, :] ** 2
    weight = jnp.where(inside, (jnp.sqrt(jnp.pi) * row_scale) ** (-0.5), jnp.zeros_like(row_scale))
    return weight[:, None] * jnp.exp(-offset * offset / spread)


def refine_axis(coarse, along):
    coarse_count = coarse.shape[along] - 2
    lower_cells = lax.slice_in_dim(coarse, 0, coarse_count, axis=along)
    middle = lax.slice_in_dim(coarse, 1, coarse_count + 1, axis=along)
    upper_cells = lax.slice_in_dim(coarse, 2, coarse_count + 2, axis=along)
    pieces = (
        0.375 * lower_cells + 0.625 * middle,
        0.125 * lower_cells + 0.875 * middle,
        0.875 * middle + 0.125 * upper_cells,
        0.625 * middle + 0.375 * upper_cells,
    )
    stacked = jnp.stack(pieces, axis=along + 1)
    new_shape = list(coarse.shape)
    new_shape[along] = 4 * coarse_count
    return stacked.reshape(new_shape)


def refine_members(coarse):
    return refine_axis(refine_axis(coarse, 1), 2)


def per_device(perturb, loc_lat, loc_lon, obs_cell, obs_count, obs_innov, obs_error):
    members, fine_lat, fine_lon = perturb.shape
    coarse_lat = fine_lat // 4
    coarse_lon = fine_lon // 4
    member_scale = 1.0 / math.sqrt(members * lax.axis_size(MEM) - 1)
    lat_kernel = kernel_rows(loc_lat, lax.axis_index(LAT) * coarse_lat - 1, coarse_lat + 2)
    lon_kernel = kernel_rows(loc_lon, lax.axis_index("lon") * coarse_lon - 1, coarse_lon + 2)
    cell_index = obs_cell.reshape(-1)
    innovation = obs_innov.reshape(-1)
    deviation = obs_error.reshape(-1)
    usable = (jnp.arange(cell_index.shape[0], dtype=jnp.int32) < obs_count.reshape(-1)[0]).astype(
        jnp.float32
    )
    ext_shape = (members, coarse_lat + 2, coarse_lon + 2)
    analysis = jnp.zeros((members, coarse_lat, coarse_lon), jnp.float32)
    observed = jnp.zeros_like(innovation)
    increment = jnp.zeros((fine_lat, fine_lon), jnp.float32)
    for iteration in range(ITERS):
        residual = (observed - innovation) / deviation
        weights = usable * residual / jnp.sqrt(1.0 + (residual / huber_width) ** 2) / deviation
        spread = (
            jnp.zeros((fine_lat * fine_lon,), jnp.float32)
            .at[cell_index]
            .add(weights)
            .reshape(fine_lat, fine_lon)
        )
        _, pullback = jax.vjp(refine_members, jnp.zeros(ext_shape, jnp.float32))
        coarse_grad = pullback(perturb * (member_scale * spread))[0]
        along_lon = summed_on_arrival(
            jnp.einsum("cj,mac->jma", lon_kernel, coarse_grad, precision=highest).reshape(
                coarse_lon * lax.axis_size("lon"), -1
            ),
            "lon",
            0,
        )
        along_lon = along_lon.reshape(coarse_lon, members, coarse_lat + 2)
        along_lat = summed_on_arrival(
            jnp.einsum("ai,jma->imj", lat_kernel, along_lon, precision=highest), LAT, 0
        )
        gradient = analysis + jnp.transpose(along_lat, (1, 0, 2))
        grad_part = jnp.sum(gradient * gradient)
        grad_total = by_axis(grad_part, MEM_LAT_LON)
        localize_along_lat = jnp.einsum(
            "ab,mbq->maq", lat_kernel, collect(gradient, LAT, 1), precision=highest
        )
        partial_value = member_scale * jnp.sum(
            refine_members(
                jnp.einsum(
                    "mab,cb->mac",
                    collect(localize_along_lat, "lon", 2),
                    lon_kernel,
                    precision=highest,
                )
            )
            * perturb,
            axis=0,
        )
        image_obs = taken_together(partial_value.reshape(-1)[cell_index], MEM)
        curve_part = jnp.sum(usable * (image_obs / deviation) ** 2)
        curvature = taken_together(curve_part, LAT_LON)
        length = grad_total / (grad_total + curvature + tiny_floor)
        analysis = analysis - length * gradient
        observed = observed - length * image_obs
        increment = increment - length * partial_value
    increment = nested_sum(increment, MEM)
    return (analysis, increment)


def solution(mesh):
    torus = Mesh(
        mesh.devices.reshape(4, 8, 2, 2, mesh.shape["lon"]),
        ("mem_0", "mem_1", "lat_0", "lat_1", "lon"),
    )
    return jax.shard_map(
        per_device,
        mesh=torus,
        in_specs=(
            P(MEM, LAT, "lon"),
            P(),
            P(),
            P(LAT, "lon", None),
            P(LAT, "lon"),
            P(LAT, "lon", None),
            P(LAT, "lon", None),
        ),
        out_specs=(P(MEM, LAT, "lon"), P(LAT, "lon")),
        check_vma=False,
    )
```

profile of v0, /device:TPU:1, one launch (start us, length us, event | category | flops | bytes accessed | tf_op | source)
XLA Modules:
  0.0 421.3 jit_solution(4102132424249863213)
XLA Ops:
  2.8 11.4 %scatter_custom_fusion = f32[196608]{0:T(1024)S(1)} fusion(s32[2048]{0:T(1024)S(1)} %bitcast.187, f32[2048]{0:T(1024)S(1)} %multiply_divide_fusion.1, f32[]{:T(128)} %constant.23.clone.1), kind=kCustom, calls=%fused_computation.52 | custom fusion | flops 2048 | bytes 786436 | tf_op jit(solution)/shard_map/scatter-add | solution.py:130
  15.6 1.4 broadcast_multiply_fusion.1
  17.0 2.8 copy.299
  19.8 1.4 fusion.69
  26.2 1.6 gather_fusion
  30.2 7.6 %all-to-all-start = ((f32[4,128,196]{1,2,0:T(8,128)}), f32[4,128,196]{1,2,0:T(8,128)S(1)}, u32[]{:S(2)}, u32[]{:S(2)}) async-start(f32[4,128,196]{1,2,0:T(8,128)} %copy.312), calls=%async_computation | async-start | bytes 819200 | tf_op jit(solution)/shard_map/all_to_all | solution.py:45
  37.8 1.3 gather_fusion.1
  39.1 9.9 %all-to-all-done = f32[4,128,196]{1,2,0:T(8,128)S(1)} async-done(((f32[4,128,196]{1,2,0:T(8,128)}), f32[4,128,196]{1,2,0:T(8,128)S(1)}, u32[]{:S(2)}, u32[]{:S(2)}) %all-to-all-start) | async-done | bytes 401440 | tf_op jit(solution)/shard_map/all_to_all | solution.py:45
  49.9 12.0 %all_to_all.74 = f32[4,96,2,128]{3,1,2,0:T(8,128)S(1)} all-to-all(f32[4,96,2,128]{3,1,2,0:T(8,128)S(1)} %copy.314), channel_id=1, replica_groups=mesh['mem_0'=4,'mem_1'=8,'lat_0'=2,'lat_1'=2,'lon'=4] {'lat_0','lat_1'}, dimensions={0} | all-to-all | bytes 786432 | tf_op jit(solution)/shard_map/all_to_all | solution.py:45
  62.0 9.8 %all_to_all.75 = f32[4,2,96,128]{3,2,1,0:T(8,128)S(1)} all-to-all(f32[4,2,96,128]{3,2,1,0:T(8,128)S(1)} %broadcast_in_dim.64), channel_id=1, replica_groups=mesh['mem_0'=4,'mem_1'=8,'lat_0'=2,'lat_1'=2,'lon'=4] {'lat_0','lat_1'}, dimensions={0} | all-to-all | bytes 786432 | tf_op jit(solution)/shard_map/all_to_all | solution.py:23
  73.2 4.3 %all-to-all-start.3 = ((f32[4,2,98,128]{3,1,2,0:T(2,128)}), f32[4,2,98,128]{3,1,2,0:T(2,128)}, u32[]{:S(2)}, u32[]{:S(2)}) async-start(f32[4,2,98,128]{3,1,2,0:T(2,128)} %broadcast_in_dim.65), calls=%async_computation.3 | async-start | bytes 802816 | tf_op jit(solution)/shard_map/all_to_all | solution.py:23
  78.7 9.7 %all-to-all-done.3 = f32[4,2,98,128]{3,1,2,0:T(2,128)} async-done(((f32[4,2,98,128]{3,1,2,0:T(2,128)}), f32[4,2,98,128]{3,1,2,0:T(2,128)}, u32[]{:S(2)}, u32[]{:S(2)}) %all-to-all-start.3) | async-done | bytes 401440 | tf_op jit(solution)/shard_map/all_to_all | solution.py:23
  88.4 1.9 copy.355
  90.3 1.9 reshape.366
  92.2 1.7 fusion.21
  94.9 2.1 copy.319
  97.0 2.5 add_bitcast_fusion.8
  99.5 1.7 pad_maximum_fusion
  101.2 3.9 copy.322
  105.2 3.9 fusion.1
  110.6 11.8 %gather_fusion.2 = f32[2048]{0:T(1024)S(1)} fusion(f32[196608]{0:T(1024)S(1)} %bitcast.164, s32[2048]{0:T(1024)S(1)} %broadcast_clamp_fusion), kind=kCustom, calls=%fused_computation.2 | custom fusion | bytes 24576 | tf_op jit(solution)/shard_map/gather | solution.py:164
  123.2 12.4 %all-to-all-start.4 = ((f32[32,1,2048]{2,1,0:T(1,128)}), f32[32,1,2048]{2,1,0:T(1,128)S(1)}, u32[]{:S(2)}, u32[]{:S(2)}) async-start(f32[32,1,2048]{2,1,0:T(1,128)} %broadcast_in_dim.66), calls=%async_computation.4 | async-start | bytes 524288 | tf_op jit(solution)/shard_map/all_to_all | solution.py:23
  136.2 9.4 %psum.70 = f32[]{:T(128)} all-reduce(f32[]{:T(128)} %multiply_reduce_fusion.1), channel_id=1, replica_groups=mesh['mem_0'=4,'mem_1'=8,'lat_0'=2,'lat_1'=2,'lon'=4] {'mem_0'}, use_global_device_ids=true, to_apply=%region_4.5 | all-reduce | flops 1 | bytes 8 | tf_op jit(solution)/shard_map/psum | solution.py:51
  145.6 14.1 %psum.71 = f32[]{:T(128)} all-reduce(f32[]{:T(128)} %psum.70), channel_id=1, replica_groups=mesh['mem_0'=4,'mem_1'=8,'lat_0'=2,'lat_1'=2,'lon'=4] {'mem_1'}, use_global_device_ids=true, to_apply=%region_5.6 | all-reduce | flops 1 | bytes 8 | tf_op jit(solution)/shard_map/psum | solution.py:51
  159.7 4.7 %psum.72 = f32[]{:T(128)} all-reduce(f32[]{:T(128)} %psum.71), channel_id=1, replica_groups=mesh['mem_0'=4,'mem_1'=8,'lat_0'=2,'lat_1'=2,'lon'=4] {'lat_0'}, use_global_device_ids=true, to_apply=%region_6.7 | all-reduce | flops 1 | bytes 8 | tf_op jit(solution)/shard_map/psum | solution.py:51
  166.5 13.2 %all-to-all-start.5 = ((f32[16,1,1]{2,1,0:T(1,128)}), f32[16,1,1]{2,1,0:T(1,128)S(1)}, u32[]{:S(2)}, u32[]{:S(2)}) async-start(f32[16,1,1]{2,1,0:T(1,128)} %broadcast_in_dim.67), calls=%async_computation.5 | async-start | bytes 16384 | tf_op jit(solution)/shard_map/all_to_all | solution.py:23
  179.6 3.0 psum.73
  182.6 11.0 %psum.74 = f32[]{:T(128)} all-reduce(f32[]{:T(128)} %psum.73), channel_id=1, replica_groups=mesh['mem_0'=4,'mem_1'=8,'lat_0'=2,'lat_1'=2,'lon'=4] {'lon'}, use_global_device_ids=true, to_apply=%region_8.9 | all-reduce | flops 1 | bytes 8 | tf_op jit(solution)/shard_map/psum | solution.py:51
  196.2 11.7 %scatter_custom_fusion.1 = f32[196608]{0:T(1024)S(1)} fusion(s32[2048]{0:T(1024)S(1)} %bitcast.189, f32[2048]{0:T(1024)S(1)} %multiply_divide_fusion, f32[]{:T(128)} %constant.23.clone.1), kind=kCustom, calls=%fused_computation.50 | custom fusion | flops 2048 | bytes 786436 | tf_op jit(solution)/shard_map/scatter-add | solution.py:130
  209.0 1.4 broadcast_multiply_fusion
  216.6 13.7 %all_to_all.76 = f32[4,128,196]{1,2,0:T(8,128)S(1)} all-to-all(f32[4,128,196]{1,2,0:T(8,128)S(1)} %copy.341), channel_id=1, replica_groups=mesh['mem_0'=4,'mem_1'=8,'lat_0'=2,'lat_1'=2,'lon'=4] {'lon'}, dimensions={0} | all-to-all | bytes 802816 | tf_op jit(solution)/shard_map/all_to_all | solution.py:45
  231.1 14.2 %all_to_all.77 = f32[4,96,2,128]{3,1,2,0:T(8,128)S(1)} all-to-all(f32[4,96,2,128]{3,1,2,0:T(8,128)S(1)} %copy.343), channel_id=1, replica_groups=mesh['mem_0'=4,'mem_1'=8,'lat_0'=2,'lat_1'=2,'lon'=4] {'lat_0','lat_1'}, dimensions={0} | all-to-all | bytes 786432 | tf_op jit(solution)/shard_map/all_to_all | solution.py:45
  246.0 9.8 %all_to_all.78 = f32[4,2,96,128]{3,2,1,0:T(8,128)S(1)} all-to-all(f32[4,2,96,128]{3,2,1,0:T(8,128)S(1)} %broadcast_in_dim.68), channel_id=1, replica_groups=mesh['mem_0'=4,'mem_1'=8,'lat_0'=2,'lat_1'=2,'lon'=4] {'lat_0','lat_1'}, dimensions={0} | all-to-all | bytes 786432 | tf_op jit(solution)/shard_map/all_to_all | solution.py:23
  256.5 15.0 %all_to_all.79 = f32[4,2,98,128]{3,1,2,0:T(2,128)S(1)} all-to-all(f32[4,2,98,128]{3,1,2,0:T(2,128)S(1)} %broadcast_in_dim.69), channel_id=1, replica_groups=mesh['mem_0'=4,'mem_1'=8,'lat_0'=2,'lat_1'=2,'lon'=4] {'lon'}, dimensions={0} | all-to-all | bytes 802816 | tf_op jit(solution)/shard_map/all_to_all | solution.py:23
  274.1 1.7 pad_maximum_fusion.1
  275.9 4.1 copy.349
  280.0 3.8 fusion
  284.4 11.8 %gather_fusion.3 = f32[2048]{0:T(1024)S(1)} fusion(f32[196608]{0:T(1024)S(1)} %bitcast.163, s32[2048]{0:T(1024)S(1)} %broadcast_clamp_fusion), kind=kCustom, calls=%fused_computation.3 | custom fusion | bytes 24576 | tf_op jit(solution)/shard_map/gather | solution.py:164
  297.0 4.9 %all-to-all-start.10 = ((f32[32,1,2048]{2,1,0:T(1,128)}), f32[32,1,2048]{2,1,0:T(1,128)S(1)}, u32[]{:S(2)}, u32[]{:S(2)}) async-start(f32[32,1,2048]{2,1,0:T(1,128)} %broadcast_in_dim.70), calls=%async_computation.10 | async-start | bytes 524288 | tf_op jit(solution)/shard_map/all_to_all | solution.py:23
  302.0 9.4 %psum.75 = f32[]{:T(128)} all-reduce(f32[]{:T(128)} %get-tuple-element.2), channel_id=1, replica_groups=mesh['mem_0'=4,'mem_1'=8,'lat_0'=2,'lat_1'=2,'lon'=4] {'mem_0'}, use_global_device_ids=true, to_apply=%region_17.18 | all-reduce | flops 1 | bytes 8 | tf_op jit(solution)/shard_map/psum | solution.py:51
  311.4 14.0 %psum.76 = f32[]{:T(128)} all-reduce(f32[]{:T(128)} %psum.75), channel_id=1, replica_groups=mesh['mem_0'=4,'mem_1'=8,'lat_0'=2,'lat_1'=2,'lon'=4] {'mem_1'}, use_global_device_ids=true, to_apply=%region_18.19 | all-reduce | flops 1 | bytes 8 | tf_op jit(solution)/shard_map/psum | solution.py:51
  325.4 4.5 %psum.77 = f32[]{:T(128)} all-reduce(f32[]{:T(128)} %psum.76), channel_id=1, replica_groups=mesh['mem_0'=4,'mem_1'=8,'lat_0'=2,'lat_1'=2,'lon'=4] {'lat_0'}, use_global_device_ids=true, to_apply=%region_19.20 | all-reduce | flops 1 | bytes 8 | tf_op jit(solution)/shard_map/psum | solution.py:51
  329.9 12.1 %psum.78 = f32[]{:T(128)} all-reduce(f32[]{:T(128)} %psum.77), channel_id=1, replica_groups=mesh['mem_0'=4,'mem_1'=8,'lat_0'=2,'lat_1'=2,'lon'=4] {'lat_1'}, use_global_device_ids=true, to_apply=%region_20.21 | all-reduce | flops 1 | bytes 8 | tf_op jit(solution)/shard_map/psum | solution.py:51
  344.1 3.6 all-to-all-start.11
  347.7 10.9 %psum.79 = f32[]{:T(128)} all-reduce(f32[]{:T(128)} %psum.78), channel_id=1, replica_groups=mesh['mem_0'=4,'mem_1'=8,'lat_0'=2,'lat_1'=2,'lon'=4] {'lon'}, use_global_device_ids=true, to_apply=%region_21.22 | all-reduce | flops 1 | bytes 8 | tf_op jit(solution)/shard_map/psum | solution.py:51
  361.6 28.9 %all_to_all.80 = f32[32,12,512]{2,1,0:T(8,128)S(1)} all-to-all(f32[32,12,512]{2,1,0:T(8,128)S(1)} %sub.74), channel_id=1, replica_groups=mesh['mem_0'=4,'mem_1'=8,'lat_0'=2,'lat_1'=2,'lon'=4] {'mem_0','mem_1'}, dimensions={0} | all-to-all | bytes 1572864 | tf_op jit(solution)/shard_map/all_to_all | solution.py:45
  391.7 7.0 %all-to-all-start.13 = ((f32[32,12,512]{2,1,0:T(8,128)}), f32[32,12,512]{2,1,0:T(8,128)S(1)}, u32[]{:S(2)}, u32[]{:S(2)}) async-start(f32[32,12,512]{2,1,0:T(8,128)} %broadcast_in_dim.73), calls=%async_computation.13 | async-start | bytes 2097152 | tf_op jit(solution)/shard_map/all_to_all | solution.py:23
  399.4 21.0 %all-to-all-done.13 = f32[32,12,512]{2,1,0:T(8,128)S(1)} async-done(((f32[32,12,512]{2,1,0:T(8,128)}), f32[32,12,512]{2,1,0:T(8,128)S(1)}, u32[]{:S(2)}, u32[]{:S(2)}) %all-to-all-start.13) | async-done | bytes 786464 | tf_op jit(solution)/shard_map/all_to_all | solution.py:23
  (136 shorter events, 39.2 us)
Async XLA Ops:
  14.2 1.4 copy-start.2
  21.2 2.4 copy-start.7
  25.2 0.9 copy-start
  29.2 8.6 %copy-start.1 = (f32[384]{0:T(512)S(1)}, f32[384]{0:T(512)}, u32[]{:S(2)}) copy-start(f32[384]{0:T(512)} %param.8) | copy-start | bytes 4612
  30.2 18.9 %all-to-all-start = ((f32[4,128,196]{1,2,0:T(8,128)}), f32[4,128,196]{1,2,0:T(8,128)S(1)}, u32[]{:S(2)}, u32[]{:S(2)}) async-start(f32[4,128,196]{1,2,0:T(8,128)} %copy.312), calls=%async_computation | async-start | bytes 819200 | tf_op jit(solution)/shard_map/all_to_all | solution.py:45
  73.2 15.2 %all-to-all-start.3 = ((f32[4,2,98,128]{3,1,2,0:T(2,128)}), f32[4,2,98,128]{3,1,2,0:T(2,128)}, u32[]{:S(2)}, u32[]{:S(2)}) async-start(f32[4,2,98,128]{3,1,2,0:T(2,128)} %broadcast_in_dim.65), calls=%async_computation.3 | async-start | bytes 802816 | tf_op jit(solution)/shard_map/all_to_all | solution.py:23
  78.7 26.5 %copy-start.3 = (f32[2,384,512]{1,0,2:T(2,128)}, f32[2,384,512]{1,0,2:T(2,128)S(1)}, u32[]{:S(2)}) copy-start(f32[2,384,512]{1,0,2:T(2,128)S(1)} %copy.323) | copy-start | bytes 4718596
  109.1 0.9 copy-start.5
  110.6 54.0 %copy-start.8 = (f32[1,1,2048]{2,1,0:T(1,128)S(1)}, f32[1,1,2048]{2,1,0:T(1,128)}, u32[]{:S(2)}) copy-start(f32[1,1,2048]{2,1,0:T(1,128)} %param.13) | copy-start | bytes 24580
  110.6 85.6 %copy-start.9 = (f32[1,1,2048]{2,1,0:T(1,128)S(1)}, f32[1,1,2048]{2,1,0:T(1,128)}, u32[]{:S(2)}) copy-start(f32[1,1,2048]{2,1,0:T(1,128)} %param.12) | copy-start | bytes 24580
  123.2 41.2 %all-to-all-start.4 = ((f32[32,1,2048]{2,1,0:T(1,128)}), f32[32,1,2048]{2,1,0:T(1,128)S(1)}, u32[]{:S(2)}, u32[]{:S(2)}) async-start(f32[32,1,2048]{2,1,0:T(1,128)} %broadcast_in_dim.66), calls=%async_computation.4 | async-start | bytes 524288 | tf_op jit(solution)/shard_map/all_to_all | solution.py:23
  166.5 27.2 %all-to-all-start.5 = ((f32[16,1,1]{2,1,0:T(1,128)}), f32[16,1,1]{2,1,0:T(1,128)S(1)}, u32[]{:S(2)}, u32[]{:S(2)}) async-start(f32[16,1,1]{2,1,0:T(1,128)} %broadcast_in_dim.67), calls=%async_computation.5 | async-start | bytes 16384 | tf_op jit(solution)/shard_map/all_to_all | solution.py:23
  275.9 4.2 copy-start.4
  296.2 65.0 %copy-start.6 = (f32[384,512]{0,1:T(8,128)S(1)}, f32[384,512]{0,1:T(8,128)}, u32[]{:S(2)}) copy-start(f32[384,512]{0,1:T(8,128)} %copy-done.5) | copy-start | bytes 2359300
  297.0 45.0 %all-to-all-start.10 = ((f32[32,1,2048]{2,1,0:T(1,128)}), f32[32,1,2048]{2,1,0:T(1,128)S(1)}, u32[]{:S(2)}, u32[]{:S(2)}) async-start(f32[32,1,2048]{2,1,0:T(1,128)} %broadcast_in_dim.70), calls=%async_computation.10 | async-start | bytes 524288 | tf_op jit(solution)/shard_map/all_to_all | solution.py:23
  344.1 14.5 %all-to-all-start.11 = ((f32[16,1,1]{2,1,0:T(1,128)}), f32[16,1,1]{2,1,0:T(1,128)S(1)}, u32[]{:S(2)}, u32[]{:S(2)}) async-start(f32[16,1,1]{2,1,0:T(1,128)} %broadcast_in_dim.71), calls=%async_computation.11 | async-start | bytes 16384 | tf_op jit(solution)/shard_map/all_to_all | solution.py:23
  391.7 28.7 %all-to-all-start.13 = ((f32[32,12,512]{2,1,0:T(8,128)}), f32[32,12,512]{2,1,0:T(8,128)S(1)}, u32[]{:S(2)}, u32[]{:S(2)}) async-start(f32[32,12,512]{2,1,0:T(8,128)} %broadcast_in_dim.73), calls=%async_computation.13 | async-start | bytes 2097152 | tf_op jit(solution)/shard_map/all_to_all | solution.py:23
where the time goes:
time: 429 us; the launch traced here: 421 us
  blocking collectives  197 us (46%)
  local copies, waits for them, and re-layouts  68.3 us (16%)
  starting transfers between devices  53.1 us (12%)
  other arithmetic  50.9 us (12%)
  waiting for transfers between devices  40.6 us (9%)
  between operations  6.07 us (1%)
  matrix products  5.9 us (1%)
    psum x10, blocking collectives, by_axis(): x = lax.psum(x, axis)  93.1 us
    all_to_all x4, blocking collectives, summed_on_arrival(): pieces = lax.all_to_all(split_up(x, dim, size), axis, 0, 0, tiled=True)  68.8 us
    all_to_all x6, starting transfers between devices, sent_to_all(): return lax.all_to_all(copies, axis, split_axis=0, concat_axis=0, tiled=True)  45.4 us
    all_to_all x3, blocking collectives, sent_to_all(): return lax.all_to_all(copies, axis, split_axis=0, concat_axis=0, tiled=True)  34.6 us
    all_to_all x6, waiting for transfers between devices, sent_to_all(): return lax.all_to_all(copies, axis, split_axis=0, concat_axis=0, tiled=True)  30.7 us
    gather x2, local copies, waits for them, and re-layouts, per_device(): image_obs = taken_together(partial_value.reshape(-1)[cell_index], MEM)  23.6 us
    scatter-add x2, other arithmetic, per_device(): spread = jnp.zeros((fine_lat * fine_lon,), jnp.float32).at[cell_index].ad...  23.1 us
    another operation x8, local copies, waits for them, and re-layouts, refine_axis(): stacked = jnp.stack(pieces, axis=along + 1)  13.2 us
  transfers between devices with their start and end apart: 7, of which 3 were waited for; matrix products, arithmetic and copies ran while one was open for 1% of the time, Pallas kernels for 0%

commit v1 on v0

v1 whole, which is shorter than its diff:
```python
import functools
import math

import jax
import jax.numpy as jnp
from jax import lax
from jax.experimental import pallas as pl
from jax.experimental.pallas import tpu as pltpu
from jax.sharding import Mesh
from jax.sharding import PartitionSpec as P

MEM = ("mem_0", "mem_1")
LAT = ("lat_0", "lat_1")
TILES = ("lat_0", "lat_1", "lon")

tiny_floor = 1e-06
highest = lax.Precision.HIGHEST
f32 = jnp.float32
bf16 = jnp.bfloat16

ROWS = 112
COLS = 144
EDGE = 128


def sent_to_all(x, axis):
    copies = jnp.broadcast_to(x, (lax.axis_size(axis), *x.shape))
    return lax.all_to_all(copies, axis, split_axis=0, concat_axis=0, tiled=True)


def scale_run(scales, first, count):
    padded = jnp.pad(scales, (8, 248), constant_values=1.0)
    return lax.dynamic_slice(padded, (first + 8,), (count,))


def kernel_block(scales, first_row, row_count, first_col, col_count):
    total = scales.shape[0]
    rows = first_row + jnp.arange(row_count, dtype=jnp.int32)
    cols = first_col + jnp.arange(col_count, dtype=jnp.int32)
    row_scale = scale_run(scales, first_row, row_count)
    col_scale = scale_run(scales, first_col, col_count)
    inside = (rows >= 0) & (rows < total)
    weight = jnp.where(inside, (jnp.sqrt(jnp.pi) * row_scale) ** (-0.5), jnp.zeros_like(row_scale))
    offset = (rows[:, None] - cols[None, :]).astype(f32)
    spread = row_scale[:, None] ** 2 + col_scale[None, :] ** 2
    return weight[:, None] * jnp.exp(-offset * offset / spread)


def split_two(x):
    high = x.astype(bf16)
    low = (x - high.astype(f32)).astype(bf16)
    return high, low


def hat(position, count):
    cell = lax.broadcasted_iota(jnp.int32, (count, position.shape[-1]), 0).astype(f32)
    return jnp.maximum(1.0 - jnp.abs(position - cell), 0.0)


def nt_dot(a, b):
    return lax.dot_general(a, b, (((1,), (1,)), ((), ())), preferred_element_type=f32)


def picked_kernel(perturb_ref, cell_ref, out_ref):
    members, fine_lat, fine_lon = perturb_ref.shape
    slots = cell_ref.shape[-1]
    step = 512
    blocks = []
    for k in range(members):
        high, low = split_two(perturb_ref[k])
        blocks.append(jnp.concatenate([high, low], axis=1))
    field = jnp.concatenate(blocks, axis=0)
    for start in range(0, slots, step):
        cell = cell_ref[:, start : start + step]
        row = cell // fine_lon
        col = cell - row * fine_lon
        at_col = lax.broadcasted_iota(jnp.int32, (fine_lon, step), 0) == col
        one = jnp.where(at_col, 1.0, 0.0).astype(bf16)
        values = jnp.dot(field, jnp.concatenate([one, one], axis=0), preferred_element_type=f32)
        at_row = lax.broadcasted_iota(jnp.int32, (fine_lat, step), 0) == row
        for k in range(members):
            mine = values[k * fine_lat : (k + 1) * fine_lat]
            out_ref[k : k + 1, start : start + step] = jnp.sum(
                jnp.where(at_row, mine, 0.0), axis=0, keepdims=True
            )


def picked(perturb, cell):
    return pl.pallas_call(
        picked_kernel,
        out_shape=jax.ShapeDtypeStruct((perturb.shape[0], cell.shape[-1]), f32),
        compiler_params=pltpu.CompilerParams(vmem_limit_bytes=56 * 1024 * 1024),
        name="picked",
    )(perturb, cell)


def weights_of(observed, innovation, inverse):
    residual = (observed - innovation) * inverse
    return residual / jnp.sqrt(1.0 + residual * residual) * inverse


def length_of(grad_total, curvature):
    return grad_total / (grad_total + curvature + tiny_floor)


def sweep_kernel(first, scale, lon_tiles, *refs):
    if first:
        tile_ref, known_ref, left_ref, right_ref, left_own_ref, right_own_ref = refs[:6]
        refs = refs[6:]
    else:
        tile_ref, known_ref, seen_ref, left_ref, right_ref, left_own_ref, right_own_ref = refs[:7]
        refs = refs[7:]
    if first:
        part_ref, coarse_ref, grad_ref, total_ref, q_ref, at_row_ref, at_col_ref = refs
    else:
        part_ref, coarse_ref, grad_ref, length_ref, total_ref, q_ref, at_row_ref, at_col_ref = refs
    tiles = known_ref.shape[0]
    slots = known_ref.shape[2] // 5
    members = grad_ref.shape[0]

    def known(n):
        return known_ref[:, 0, n * slots : (n + 1) * slots]

    cell = known(0)
    innovation = known(1)
    inverse = known(2)
    row = jnp.floor(cell * (1.0 / 512.0))
    at_row_ref[...] = (row + 2.5) * 0.25
    at_col_ref[...] = (cell - row * 512.0 + 2.5) * 0.25
    force = weights_of(0.0, innovation, inverse)
    if not first:
        image = seen_ref[:, 0, :slots]
        grad_total = jnp.sum(seen_ref[:, 0, slots:])
        curvature = jnp.sum((image * inverse) ** 2)
        length = length_of(grad_total, curvature)
        force = weights_of(-length * image, innovation, inverse) - length * force
        length_ref[...] = jnp.broadcast_to(length, length_ref.shape)
    for k in range(members):
        q_ref[k] = known(3 + k) * force * scale
    total_ref[...] = jnp.zeros_like(total_ref)

    def one_tile(t, carry):
        lat = t // lon_tiles
        lon = t - lat * lon_tiles
        rows = hat(at_row_ref[pl.ds(t, 1), :], ROWS)
        cols = hat(at_col_ref[pl.ds(t, 1), :], COLS).astype(bf16)
        blocks = []
        for k in range(members):
            blocks.extend(split_two(rows * q_ref[k, pl.ds(t, 1), :]))
        made = nt_dot(jnp.concatenate(blocks, axis=0), cols)
        at = pl.ds(pl.multiple_of(lat * 96, 8), ROWS)
        for k in range(members):
            both = made[2 * k * ROWS : (2 * k + 1) * ROWS] + made[(2 * k + 1) * ROWS : (2 * k + 2) * ROWS]
            total_ref[k, at, pl.ds(pl.multiple_of(lon * 128, 128), 128)] += both[:, :128]
            total_ref[k, at, pl.ds(pl.multiple_of(lon * 128 + 128, 128), COLS - 128)] += both[:, 128:]
        return carry

    lax.fori_loop(0, tiles, one_tile, 0)

    own = tile_ref[0]
    rows = hat(at_row_ref[pl.ds(own, 1), :], ROWS)
    cols = hat(at_col_ref[pl.ds(own, 1), :], COLS).astype(bf16)
    left = jnp.concatenate([left_ref[...], left_own_ref[...]], axis=0)
    image = jnp.zeros((1, slots), f32)
    squares = jnp.zeros((1, EDGE), f32)
    for k in range(members):
        half = jnp.dot(left, total_ref[k], precision=highest, preferred_element_type=f32)
        coarse = jnp.dot(half[:ROWS], right_ref[...], precision=highest, preferred_element_type=f32)
        grad = jnp.dot(half[ROWS:], right_own_ref[...], precision=highest, preferred_element_type=f32)
        coarse_ref[k] = coarse
        grad_ref[k] = grad
        squares = squares + jnp.sum(grad * grad, axis=0, keepdims=True)
        made = jnp.dot(jnp.concatenate(split_two(coarse), axis=0), cols, preferred_element_type=f32)
        value = jnp.sum((made[:ROWS] + made[ROWS:]) * rows, axis=0, keepdims=True)
        image = image + value * known_ref[own, :, (3 + k) * slots : (4 + k) * slots]
    part_ref[:, :slots] = image * scale
    part_ref[:, slots:] = squares


def sweep(tile, known, seen, kernels, scale, lon_tiles, members):
    left, right, left_own, right_own = kernels
    slots = known.shape[2] // 5
    tiles = known.shape[0]
    first = seen is None
    out_shape = [
        jax.ShapeDtypeStruct((1, slots + EDGE), f32),
        jax.ShapeDtypeStruct((members, ROWS, COLS), f32),
        jax.ShapeDtypeStruct((members, left_own.shape[0], right_own.shape[1]), f32),
    ]
    if not first:
        out_shape.append(jax.ShapeDtypeStruct((1, EDGE), f32))
    arrays = [known] if first else [known, seen]
    arrays += [left, right, left_own, right_own]
    whole = pl.BlockSpec(memory_space=pltpu.VMEM)
    return pl.pallas_call(
        functools.partial(sweep_kernel, first, scale, lon_tiles),
        out_shape=out_shape,
        in_specs=[pl.BlockSpec(memory_space=pltpu.SMEM)] + [whole] * len(arrays),
        out_specs=[whole] * len(out_shape),
        scratch_shapes=[
            pltpu.VMEM((members, left.shape[1], right.shape[0]), f32),
            pltpu.VMEM((members, tiles, slots), f32),
            pltpu.VMEM((tiles, slots), f32),
            pltpu.VMEM((tiles, slots), f32),
        ],
        compiler_params=pltpu.CompilerParams(vmem_limit_bytes=56 * 1024 * 1024),
        name="sweep_first" if first else "sweep_second",
    )(tile, *arrays)


def field_kernel(scale, perturb_ref, length_ref, ends_ref, c1_ref, c2_ref, g1_ref, g2_ref, out_ref, analysis_ref):
    members, fine_lat, fine_lon = perturb_ref.shape
    pieces, piece_rows, piece_cols = out_ref.shape
    across = fine_lon // piece_cols
    one = length_ref[0, 0]
    two = length_of(jnp.sum(ends_ref[:, 0, EDGE:]), jnp.sum(ends_ref[:, 0, :EDGE]))

    def refined(count, cells, axis):
        shape = (count, cells) if axis == 0 else (cells, count)
        fine = lax.broadcasted_iota(jnp.int32, shape, axis).astype(f32)
        cell = lax.broadcasted_iota(jnp.int32, shape, 1 - axis).astype(f32)
        return jnp.maximum(1.0 - jnp.abs((fine + 2.5) * 0.25 - cell), 0.0).astype(bf16)

    to_rows = refined(fine_lat, ROWS, 0)
    to_cols = refined(fine_lon, COLS, 1)
    field = jnp.zeros((fine_lat, fine_lon), f32)
    for k in range(members):
        coarse = one * c1_ref[k] + two * c2_ref[k]
        high, low = split_two(coarse)
        tall = jnp.dot(to_rows, high, preferred_element_type=f32) + jnp.dot(to_rows, low, preferred_element_type=f32)
        high, low = split_two(tall)
        fine = jnp.dot(high, to_cols, preferred_element_type=f32) + jnp.dot(low, to_cols, preferred_element_type=f32)
        field = field + fine * perturb_ref[k]
        analysis_ref[k] = -(one * g1_ref[k] + two * g2_ref[k])
    field = -scale * field
    for n in range(pieces):
        i = n // across * piece_rows
        j = n % across * piece_cols
        out_ref[n] = field[i : i + piece_rows, j : j + piece_cols]


def per_device(perturb, loc_lat, loc_lon, obs_cell, obs_count, obs_innov, obs_error):
    members, fine_lat, fine_lon = perturb.shape
    coarse_lat, coarse_lon = fine_lat // 4, fine_lon // 4
    groups = lax.axis_size(MEM)
    scale = 1.0 / math.sqrt(members * groups - 1)
    lat, lon = lax.axis_index(LAT), lax.axis_index("lon")
    lat_tiles, lon_tiles = lax.axis_size(LAT), lax.axis_size("lon")
    slots = obs_cell.shape[-1]
    total_lat, total_lon = lat_tiles * coarse_lat, lon_tiles * coarse_lon
    padded_lat, padded_lon = total_lat + 16, total_lon + 128
    tile = (lat * lon_tiles + lon).astype(jnp.int32).reshape(1)

    cell = obs_cell.reshape(1, slots)
    innovation = obs_innov.reshape(1, slots)
    usable = jnp.arange(slots, dtype=jnp.int32)[None, :] < obs_count.reshape(1, 1)
    inverse = jnp.where(usable, 1.0 / obs_error.reshape(1, slots), 0.0)
    near = picked(perturb, cell)
    message = jnp.concatenate([cell.astype(f32), innovation, inverse, near[:1], near[1:]], axis=1)
    known = sent_to_all(message, TILES)

    first_lat, first_lon = lat * coarse_lat, lon * coarse_lon
    lat_all = kernel_block(loc_lat, -1, padded_lat, 0, total_lat)
    lon_all = kernel_block(loc_lon, -1, padded_lon, 0, total_lon)
    lat_tile = kernel_block(loc_lat, first_lat - 1, ROWS, 0, total_lat)
    lon_tile = kernel_block(loc_lon, first_lon - 1, COLS, 0, total_lon)
    left = jnp.einsum("ab,cb->ac", lat_tile, lat_all, precision=highest)
    right = jnp.einsum("ab,cb->ac", lon_all, lon_tile, precision=highest)
    left_own = kernel_block(loc_lat, -1, padded_lat, first_lat, coarse_lat).T
    right_own = kernel_block(loc_lon, -1, padded_lon, first_lon, coarse_lon)
    kernels = (left, right, left_own, right_own)

    part, coarse_1, grad_1 = sweep(tile, known, None, kernels, scale, lon_tiles, members)
    mine = jnp.sum(sent_to_all(part, MEM), axis=0)
    seen = sent_to_all(mine, TILES)
    part, coarse_2, grad_2, length_1 = sweep(tile, known, seen, kernels, scale, lon_tiles, members)
    mine = jnp.sum(sent_to_all(part, MEM), axis=0)
    bent = (mine[:, :slots] * inverse) ** 2
    bent = jnp.sum(bent.reshape(slots // EDGE, EDGE), axis=0, keepdims=True)
    ends = sent_to_all(jnp.concatenate([bent, mine[:, slots:]], axis=1), TILES)

    whole = pl.BlockSpec(memory_space=pltpu.VMEM)
    piece_cols = 128
    piece_rows = fine_lat * fine_lon // groups // piece_cols
    pieces, analysis = pl.pallas_call(
        functools.partial(field_kernel, scale),
        out_shape=[
            jax.ShapeDtypeStruct((groups, piece_rows, piece_cols), f32),
            jax.ShapeDtypeStruct((members, coarse_lat, coarse_lon), f32),
        ],
        in_specs=[whole] * 7,
        out_specs=[whole] * 2,
        compiler_params=pltpu.CompilerParams(vmem_limit_bytes=56 * 1024 * 1024),
        name="field",
    )(perturb, length_1, ends, coarse_1, coarse_2, grad_1, grad_2)
    summed = jnp.sum(lax.all_to_all(pieces, MEM, 0, 0, tiled=True), axis=0)
    everything = sent_to_all(summed, MEM)
    across = fine_lon // piece_cols
    increment = jnp.transpose(
        everything.reshape(fine_lat // piece_rows, across, piece_rows, piece_cols), (0, 2, 1, 3)
    ).reshape(fine_lat, fine_lon)
    return analysis, increment


def solution(mesh):
    torus = Mesh(
        mesh.devices.reshape(4, -1, 2, mesh.shape["lat"] // 2, mesh.shape["lon"]),
        ("mem_0", "mem_1", "lat_0", "lat_1", "lon"),
    )
    return jax.shard_map(
        per_device,
        mesh=torus,
        in_specs=(
            P(MEM, LAT, "lon"),
            P(),
            P(),
            P(LAT, "lon", None),
            P(LAT, "lon"),
            P(LAT, "lon", None),
            P(LAT, "lon", None),
        ),
        out_specs=(P(MEM, LAT, "lon"), P(LAT, "lon")),
        check_vma=False,
    )
```

time: 429 us -> 205 us (0.48); the launches traced: 421 us -> 202 us
  blocking collectives: 197 us -> 116 us
  local copies, waits for them, and re-layouts: 68.3 us -> 5.17 us
  Pallas kernels: 0 us -> 46.6 us
  other arithmetic: 50.9 us -> 5.03 us
  starting transfers between devices: 53.1 us -> 10.2 us
  waiting for transfers between devices: 40.6 us -> 12.7 us
  between operations: 6.07 us -> 1.47 us
    psum x10 -> x0, blocking collectives: 93.1 us -> none  [by_axis(): x = lax.psum(x, axis)]
    all_to_all x3 -> x5, blocking collectives: 34.6 us -> 92.3 us  [sent_to_all(): return lax.all_to_all(copies, axis, split_axis=0, concat_axis=0, tiled=True)]
    pallas_call x0 -> x4, Pallas kernels: none -> 46.6 us  [the longest x2 37 us: sweep(): pl.pallas_call(functools.partial(sweep_kernel, first, scale, lon_tiles),...]
    all_to_all x4 -> x1, blocking collectives: 68.8 us -> 24 us  [per_device(): summed = jnp.sum(lax.all_to_all(pieces, MEM, 0, 0, tiled=True), axis=0)]
    all_to_all x6 -> x1, starting transfers between devices: 45.4 us -> 10.2 us  [sent_to_all(): return lax.all_to_all(copies, axis, split_axis=0, concat_axis=0, tiled=True)]
    gather x4 -> x0, local copies, waits for them, and re-layouts: 26.4 us -> none  [the longest x2 23.6 us: per_device(): image_obs = taken_together(partial_value.reshape(-1)[cell_index], MEM)]
    scatter-add x2 -> x0, other arithmetic: 23.1 us -> none  [per_device(): spread = jnp.zeros((fine_lat * fine_lon,), jnp.float32).at[cell_index].ad...]
    all_to_all x6 -> x1, waiting for transfers between devices: 30.7 us -> 12.7 us  [sent_to_all(): return lax.all_to_all(copies, axis, split_axis=0, concat_axis=0, tiled=True)]
  transfers between devices with their start and end apart: 7 -> 1, of which waited for: 3 -> 1; matrix products, arithmetic and copies ran while one was open for 1% -> 3% of each run, Pallas kernels for 0% -> 0%
where the time goes in v1:
time: 205 us; the launch traced here: 202 us
  blocking collectives  116 us (57%)
  Pallas kernels  46.6 us (23%)
  waiting for transfers between devices  12.7 us (6%)
  starting transfers between devices  10.2 us (5%)
  local copies, waits for them, and re-layouts  5.17 us (3%)
  other arithmetic  5.03 us (2%)
  matrix products  4.31 us (2%)
    all_to_all x5, blocking collectives, sent_to_all(): return lax.all_to_all(copies, axis, split_axis=0, concat_axis=0, tiled=True)  92.3 us
    pallas_call x2, Pallas kernels, sweep(): pl.pallas_call(functools.partial(sweep_kernel, first, scale, lon_tiles),...  37 us
    all_to_all x1, blocking collectives, per_device(): summed = jnp.sum(lax.all_to_all(pieces, MEM, 0, 0, tiled=True), axis=0)  24 us
    all_to_all x1, waiting for transfers between devices, sent_to_all(): return lax.all_to_all(copies, axis, split_axis=0, concat_axis=0, tiled=True)  12.7 us
    all_to_all x1, starting transfers between devices, sent_to_all(): return lax.all_to_all(copies, axis, split_axis=0, concat_axis=0, tiled=True)  10.2 us
    pallas_call x1, Pallas kernels, picked(): pl.pallas_call(picked_kernel, out_shape=jax.ShapeDtypeStruct((perturb.sha...  5.94 us
  transfers between devices with their start and end apart: 1, of which 1 were waited for; matrix products, arithmetic and copies ran while one was open for 3% of the time, Pallas kernels for 0%

profile of v1, /device:TPU:1, one launch (start us, length us, event | category | flops | bytes accessed | tf_op | source)
XLA Modules:
  0.0 201.8 jit_solution(12275099868161848589)
XLA Ops:
  0.6 0.0 copy-start.4
  0.6 0.0 copy-start.3
  1.3 0.7 constant_dynamic-update-slice_fusion.4
  2.0 5.9 %picked.1 = f32[2,2048]{1,0:T(2,128)} custom-call(f32[2,384,512]{2,1,0:T(8,128)} %perturb_ref.3, s32[1,2048]{1,0:T(1,128)} %bitcast.26), custom_call_target="tpu_custom_call" | custom-call | tf_op jit(solution)/shard_map/picked/pallas_call | solution.py:89
  8.0 0.0 copy-done.4
  8.0 0.0 copy-start.1
  8.0 0.0 copy-start.2
  8.0 0.0 copy-done.3
  8.0 0.7 constant_dynamic-update-slice_fusion.1
  8.7 0.7 constant_dynamic-update-slice_fusion
  9.5 1.2 broadcast_in_dim.23
  10.7 10.2 %all-to-all-start = ((f32[16,1,10240]{2,1,0:T(1,128)}), f32[16,1,10240]{2,1,0:T(1,128)S(1)}, u32[]{:S(2)}, u32[]{:S(2)}) async-start(f32[16,1,10240]{2,1,0:T(1,128)} %broadcast_in_dim.23), calls=%async_computation | async-start | bytes 1310720 | tf_op jit(solution)/shard_map/all_to_all | solution.py:28
  20.9 0.0 copy-done.1
  21.0 0.1 power_select_fusion.1
  21.0 0.1 fusion.51
  21.1 0.1 and_select_fusion.1
  21.2 0.0 copy-done.2
  21.2 0.1 and_select_fusion
  21.3 0.1 fusion.52
  21.4 0.1 power_select_fusion
  21.5 0.8 fusion.31.refs_4_.refs_5_
  22.3 1.7 fusion.12.refs_2_.refs_3_
  24.1 1.0 fusion.16.refs_5_.refs_6_
  25.1 2.6 %fusion.3.refs_3_.refs_4_ = f32[640,144]{1,0:T(8,128)} fusion(f32[512]{0:T(512)S(1)} %integer_pow.43, f32[640]{0:T(1024)S(1)} %get-tuple-element.25, s32[640]{0:T(1024)S(1)} %iota_add_fusion, f32[640]{0:T(1024)S(1)} %get-tuple-element.24, f32[144]{0:T(256)S(1)} %get-tuple-element.23, s32[144]{0:T(256)S(1)} %iota_add_fusion.2, f32[144]{0:T(256)S(1)} %get-tuple-element.22), kind=kOutput, calls=%fused_computation.4 | convolution fusion | flops 569040896 | bytes 380096 | tf_op jit(solution)/shard_map/ab,cb->ac/dot_general | solution.py:268
  27.7 12.7 %all-to-all-done.refs_1_ = f32[16,1,10240]{2,1,0:T(1,128)S(1)} async-done(((f32[16,1,10240]{2,1,0:T(1,128)}), f32[16,1,10240]{2,1,0:T(1,128)S(1)}, u32[]{:S(2)}, u32[]{:S(2)}) %all-to-all-start) | async-done | bytes 655392 | tf_op jit(solution)/shard_map/all_to_all | solution.py:28
  40.4 0.0 copy-start
  40.4 0.8 copy-done
  41.2 18.4 %sweep_first.1 = (f32[1,2176]{1,0:T(1,128)}, f32[2,112,144]{2,1,0:T(8,128)}, f32[2,96,128]{2,1,0:T(8,128)}) custom-call(s32[1]{0:T(128)} %bitcast.refs_0_, f32[16,1,10240]{2,1,0:T(1,128)} %copy-done, f32[112,400]{1,0:T(8,128)} %fusion.12.refs_2_.refs_3_, f32[640,144]{1,0:T(8,128)} %fusion.3.refs_3_.refs_4_, f32[96,400]{1,0:T(8,128)} %fusion.31.refs_4_.refs_5_, ...), custom_call_target="tpu_custom_call" | custom-call | tf_op jit(solution)/shard_map/sweep_first/pallas_call | solution.py:195
  59.6 0.7 reduce.2
  60.3 0.1 broadcast_in_dim.26
  60.5 23.0 %all_to_all.35 = f32[32,1,2176]{2,1,0:T(1,128)S(1)} all-to-all(f32[32,1,2176]{2,1,0:T(1,128)S(1)} %broadcast_in_dim.26), channel_id=1, replica_groups=mesh['mem_0'=4,'mem_1'=8,'lat_0'=2,'lat_1'=2,'lon'=4] {'mem_0','mem_1'}, dimensions={0} | all-to-all | bytes 557056 | tf_op jit(solution)/shard_map/all_to_all | solution.py:28
  83.5 0.2 reduce_sum.38
  83.7 0.1 broadcast_in_dim.27
  83.8 13.7 %all_to_all.36.refs_2_ = f32[16,1,2176]{2,1,0:T(1,128)} all-to-all(f32[16,1,2176]{2,1,0:T(1,128)S(1)} %broadcast_in_dim.27), channel_id=1, replica_groups=mesh['mem_0'=4,'mem_1'=8,'lat_0'=2,'lat_1'=2,'lon'=4] {'lat_0','lat_1','..., dimensions={0} | all-to-all | bytes 278528 | tf_op jit(solution)/shard_map/all_to_all | solution.py:28
  97.4 18.6 %sweep_second.1 = (f32[1,2176]{1,0:T(1,128)}, f32[2,112,144]{2,1,0:T(8,128)}, f32[2,96,128]{2,1,0:T(8,128)}, f32[1,128]{1,0:T(1,128)}) custom-call(s32[1]{0:T(128)} %bitcast.refs_0_, f32[16,1,10240]{2,1,0:T(1,128)} %copy-done, f32[16,1,2176]{2,1,0:T(1,128)} %all_to_all.36.refs_2_, f32[112,400]{1,0:T(8,128)} %fusion.12.refs_2_.refs_3_, ...), custom_call_target="tpu_custom_call" | custom-call | tf_op jit(solution)/shard_map/sweep_second/pallas_call | solution.py:195
  116.0 0.7 reduce.3
  116.7 0.1 broadcast_in_dim.28
  116.9 14.9 %all_to_all.37 = f32[32,1,2176]{2,1,0:T(1,128)S(1)} all-to-all(f32[32,1,2176]{2,1,0:T(1,128)S(1)} %broadcast_in_dim.28), channel_id=1, replica_groups=mesh['mem_0'=4,'mem_1'=8,'lat_0'=2,'lat_1'=2,'lon'=4] {'mem_0','mem_1'}, dimensions={0} | all-to-all | bytes 557056 | tf_op jit(solution)/shard_map/all_to_all | solution.py:28
  131.8 0.2 reduce_sum.39
  132.0 12.3 %all_to_all.38.ends_ref = f32[16,1,256]{2,1,0:T(1,128)} all-to-all(f32[16,1,256]{2,1,0:T(1,128)S(1)} %broadcast_in_dim.30), channel_id=1, replica_groups=mesh['mem_0'=4,'mem_1'=8,'lat_0'=2,'lat_1'=2,'lon'=4] {'lat_0','lat_1','..., dimensions={0} | all-to-all | bytes 32768 | tf_op jit(solution)/shard_map/all_to_all | solution.py:28
  144.3 3.7 %field.1 = (f32[32,48,128]{2,1,0:T(8,128)}, f32[2,96,128]{2,1,0:T(8,128)}) custom-call(f32[2,384,512]{2,1,0:T(8,128)} %perturb_ref.3, f32[1,128]{1,0:T(1,128)} %get-tuple-element.12.length_ref, f32[16,1,256]{2,1,0:T(1,128)} %all_to_all.38.ends_ref, f32[2,112,144]{2,1,0:T(8,128)} %get-tuple-element.14.c1_ref, f32[2,112,144]{2,1,0:T(8,128)} %get-tuple-element.15.c2_ref, ...), custom_call_target="tpu_custom_call" | custom-call | tf_op jit(solution)/shard_map/field/pallas_call | solution.py:285
  148.0 24.0 %all_to_all.39 = f32[32,48,128]{2,1,0:T(8,128)S(1)} all-to-all(f32[32,48,128]{2,1,0:T(8,128)} %get-tuple-element.19), channel_id=1, replica_groups=mesh['mem_0'=4,'mem_1'=8,'lat_0'=2,'lat_1'=2,'lon'=4] {'mem_0','mem_1'}, dimensions={0} | all-to-all | bytes 1572864 | tf_op jit(solution)/shard_map/all_to_all | solution.py:296
  172.0 0.1 reduce_sum.42
  172.1 0.1 broadcast_in_dim.31
  172.1 28.4 %all_to_all.40 = f32[32,48,128]{2,1,0:T(8,128)S(1)} all-to-all(f32[32,48,128]{2,1,0:T(8,128)S(1)} %broadcast_in_dim.31), channel_id=1, replica_groups=mesh['mem_0'=4,'mem_1'=8,'lat_0'=2,'lat_1'=2,'lon'=4] {'mem_0','mem_1'}, dimensions={0} | all-to-all | bytes 1572864 | tf_op jit(solution)/shard_map/all_to_all | solution.py:28
  200.6 0.3 copy.33
  200.9 0.9 copy.40
  (16 shorter events, 0.1 us)
Async XLA Ops:
  0.6 7.3 %copy-start.4 = (f32[1,1,2048]{2,1,0:T(1,128)S(1)}, f32[1,1,2048]{2,1,0:T(1,128)}, u32[]{:S(2)}) copy-start(f32[1,1,2048]{2,1,0:T(1,128)} %param.12) | copy-start | bytes 24580
  0.6 7.3 %copy-start.3 = (f32[1,1,2048]{2,1,0:T(1,128)S(1)}, f32[1,1,2048]{2,1,0:T(1,128)}, u32[]{:S(2)}) copy-start(f32[1,1,2048]{2,1,0:T(1,128)} %param.13) | copy-start | bytes 24580
  8.0 13.0 %copy-start.1 = (f32[384]{0:T(512)S(1)}, f32[384]{0:T(512)}, u32[]{:S(2)}) copy-start(f32[384]{0:T(512)} %param.8) | copy-start | bytes 4612
  8.0 13.3 %copy-start.2 = (f32[512]{0:T(512)S(1)}, f32[512]{0:T(512)}, u32[]{:S(2)}) copy-start(f32[512]{0:T(512)} %param.9) | copy-start | bytes 6148
  10.7 29.7 %all-to-all-start = ((f32[16,1,10240]{2,1,0:T(1,128)}), f32[16,1,10240]{2,1,0:T(1,128)S(1)}, u32[]{:S(2)}, u32[]{:S(2)}) async-start(f32[16,1,10240]{2,1,0:T(1,128)} %broadcast_in_dim.23), calls=%async_computation | async-start | bytes 1310720 | tf_op jit(solution)/shard_map/all_to_all | solution.py:28
  40.4 0.8 copy-start

commit v2 on v1

v2 whole, which is shorter than its diff:
```python
import functools
import math

import jax
import jax.numpy as jnp
from jax import lax
from jax.experimental import pallas as pl
from jax.experimental.pallas import tpu as pltpu
from jax.sharding import Mesh
from jax.sharding import PartitionSpec as P

MEM = ("mem_0", "mem_1")
LAT = ("lat_0", "lat_1")
TILES = ("lat_0", "lat_1", "lon")

tiny_floor = 1e-06
highest = lax.Precision.HIGHEST
f32 = jnp.float32
bf16 = jnp.bfloat16

ROWS = 112
COLS = 144
EDGE = 128


def sent_to_all(x, axis):
    copies = jnp.broadcast_to(x, (lax.axis_size(axis), *x.shape))
    return lax.all_to_all(copies, axis, split_axis=0, concat_axis=0, tiled=True)


def scale_run(scales, first, count):
    padded = jnp.pad(scales, (8, 248), constant_values=1.0)
    return lax.dynamic_slice(padded, (first + 8,), (count,))


def kernel_block(scales, first_row, row_count, first_col, col_count):
    total = scales.shape[0]
    rows = first_row + jnp.arange(row_count, dtype=jnp.int32)
    cols = first_col + jnp.arange(col_count, dtype=jnp.int32)
    row_scale = scale_run(scales, first_row, row_count)
    col_scale = scale_run(scales, first_col, col_count)
    inside = (rows >= 0) & (rows < total)
    weight = jnp.where(inside, (jnp.sqrt(jnp.pi) * row_scale) ** (-0.5), jnp.zeros_like(row_scale))
    offset = (rows[:, None] - cols[None, :]).astype(f32)
    spread = row_scale[:, None] ** 2 + col_scale[None, :] ** 2
    return weight[:, None] * jnp.exp(-offset * offset / spread)


def split_two(x):
    high = x.astype(bf16)
    low = (x - high.astype(f32)).astype(bf16)
    return high, low


def nt_dot(a, b):
    return lax.dot_general(a, b, (((1,), (1,)), ((), ())), preferred_element_type=f32)


def dot(a, b):
    return jnp.dot(a, b, preferred_element_type=f32)


def picked_kernel(count_ref, perturb_ref, cell_ref, innov_ref, error_ref, out_ref):
    members, fine_lat, fine_lon = perturb_ref.shape
    slots = cell_ref.shape[-1]
    step = 512
    slot = lax.broadcasted_iota(jnp.int32, (1, slots), 1)
    out_ref[:, :slots] = cell_ref[...].astype(f32)
    out_ref[:, slots : 2 * slots] = innov_ref[...]
    out_ref[:, 2 * slots : 3 * slots] = jnp.where(slot < count_ref[0], 1.0 / error_ref[...], 0.0)
    blocks = []
    for k in range(members):
        blocks.append(jnp.concatenate(split_two(perturb_ref[k]), axis=1))
    field = jnp.concatenate(blocks, axis=0)
    for start in range(0, slots, step):
        cell = cell_ref[:, start : start + step]
        row = cell // fine_lon
        col = cell - row * fine_lon
        at_col = lax.broadcasted_iota(jnp.int32, (fine_lon, step), 0) == col
        one = jnp.where(at_col, 1.0, 0.0).astype(bf16)
        values = dot(field, jnp.concatenate([one, one], axis=0))
        at_row = lax.broadcasted_iota(jnp.int32, (fine_lat, step), 0) == row
        for k in range(members):
            mine = values[k * fine_lat : (k + 1) * fine_lat]
            at = (3 + k) * slots + start
            out_ref[:, at : at + step] = jnp.sum(jnp.where(at_row, mine, 0.0), axis=0, keepdims=True)


def picked(count, perturb, cell, innovation, error):
    whole = pl.BlockSpec(memory_space=pltpu.VMEM)
    fields = 3 + perturb.shape[0]
    return pl.pallas_call(
        picked_kernel,
        out_shape=jax.ShapeDtypeStruct((1, fields * cell.shape[-1]), f32),
        in_specs=[pl.BlockSpec(memory_space=pltpu.SMEM)] + [whole] * 4,
        out_specs=whole,
        compiler_params=pltpu.CompilerParams(vmem_limit_bytes=24 * 1024 * 1024),
        name="picked",
    )(count, perturb, cell, innovation, error)


def weights_of(observed, innovation, inverse):
    residual = (observed - innovation) * inverse
    return residual / jnp.sqrt(1.0 + residual * residual) * inverse


def length_of(grad_total, curvature):
    return grad_total / (grad_total + curvature + tiny_floor)


def hat(below, lower, upper, count):
    groups = []
    wide = (16, below.shape[-1])
    below, lower, upper = (jnp.broadcast_to(x, wide).astype(bf16) for x in (below, lower, upper))
    zero = jnp.zeros(wide, bf16)
    cell = lax.broadcasted_iota(jnp.int32, wide, 0).astype(f32)
    for start in range(0, count, 16):
        at = (cell + start).astype(bf16)
        before = (cell + (start - 1)).astype(bf16)
        groups.append(jnp.where(below == at, lower, jnp.where(below == before, upper, zero)))
    return jnp.concatenate(groups, axis=0)


def sweep_kernel(first, scale, lon_tiles, members, *refs):
    tile_ref, known_ref = refs[:2]
    refs = refs[2:]
    if not first:
        seen_ref = refs[0]
        refs = refs[1:]
    left_ref, left_low_ref, right_ref, right_low_ref, part_ref, coarse_ref, total_ref = refs[:7]
    refs = refs[7:]
    if not first:
        length_ref, force_ref = refs[:2]
        refs = refs[2:]
    hold = refs[0]
    tiles = known_ref.shape[0]
    slots = known_ref.shape[2] // (3 + members)
    width = total_ref.shape[2]

    def known(n):
        return known_ref[:, 0, n * slots : (n + 1) * slots]

    cell = known(0)
    innovation = known(1)
    inverse = known(2)
    row = jnp.floor(cell * (1.0 / 512.0))
    col = (cell - row * 512.0 + 2.5) * 0.25
    row = (row + 2.5) * 0.25
    row_cell, col_cell = jnp.floor(row), jnp.floor(col)
    row_up, col_up = row - row_cell, col - col_cell
    hold[0], hold[1], hold[2], hold[3] = row_cell, col_cell, 1.0 - col_up, col_up
    hold[4], hold[5] = 1.0 - row_up, row_up
    force = weights_of(0.0, innovation, inverse)
    if not first:
        image = seen_ref[:, 0, :slots]
        length = length_of(jnp.sum(force * image), jnp.sum((image * inverse) ** 2))
        force = weights_of(-length * image, innovation, inverse) - length * force
        length_ref[...] = jnp.broadcast_to(length, length_ref.shape)
    hold[6] = force
    n = 7
    for k in range(members):
        q = known(3 + k) * force * scale
        for share in (1.0 - row_up, row_up):
            whole = share * q
            high = whole.astype(bf16).astype(f32)
            hold[n] = high
            hold[n + 1] = whole - high
            n += 2
    total_ref[...] = jnp.zeros_like(total_ref)

    def one_tile(t, carry):
        lat = t // lon_tiles
        lon = t - lat * lon_tiles

        def line(i):
            return hold[i, pl.ds(t, 1), :]

        cols = hat(line(1), line(2), line(3), COLS)
        blocks = []
        for k in range(members):
            for term in range(2):
                at = 7 + 4 * k + term
                blocks.append(hat(line(0), line(at), line(at + 2), ROWS))
        made = nt_dot(jnp.concatenate(blocks, axis=0), cols)
        at = pl.ds(pl.multiple_of(lat * 96, 8), ROWS)
        for k in range(members):
            both = made[2 * k * ROWS : (2 * k + 1) * ROWS] + made[(2 * k + 1) * ROWS : (2 * k + 2) * ROWS]
            total_ref[k, at, pl.ds(pl.multiple_of(lon * 128, 128), 128)] += both[:, :128]
            total_ref[k, at, pl.ds(pl.multiple_of(lon * 128 + 128, 128), COLS - 128)] += both[:, 128:]
        return carry

    lax.fori_loop(0, tiles, one_tile, 0)

    own = tile_ref[0]

    def own_line(i):
        return hold[i, pl.ds(own, 1), :]

    rows = hat(own_line(0), own_line(4), own_line(5), ROWS).astype(f32)
    cols = hat(own_line(1), own_line(2), own_line(3), COLS)
    high, low = zip(*(split_two(total_ref[k]) for k in range(members)))
    high, low = jnp.concatenate(high, axis=1), jnp.concatenate(low, axis=1)
    half = dot(left_ref[...], high) + (dot(left_ref[...], low) + dot(left_low_ref[...], high))
    half = jnp.concatenate([half[:, k * width : (k + 1) * width] for k in range(members)], axis=0)
    high, low = split_two(half)
    coarse = dot(high, right_ref[...]) + (dot(low, right_ref[...]) + dot(high, right_low_ref[...]))
    image = jnp.zeros((1, slots), f32)
    for k in range(members):
        mine = coarse[k * ROWS : (k + 1) * ROWS]
        coarse_ref[k] = mine
        high, low = split_two(mine)
        made = dot(high, cols) + dot(low, cols)
        value = jnp.sum(made * rows, axis=0, keepdims=True)
        image = image + value * known_ref[own, :, (3 + k) * slots : (4 + k) * slots]
    image = image * scale
    if not first:
        force_ref[...] = own_line(6)
    for n in range(part_ref.shape[0]):
        part_ref[n, :, :slots] = image


def sweep(tile, known, seen, kernels, scale, lon_tiles, members, groups):
    slots = known.shape[2] // (3 + members)
    tiles = known.shape[0]
    first = seen is None
    left, _, right, _ = kernels
    out_shape = [
        jax.ShapeDtypeStruct((groups, 1, slots), f32),
        jax.ShapeDtypeStruct((members, ROWS, COLS), f32),
        jax.ShapeDtypeStruct((members, left.shape[1], right.shape[0]), f32),
    ]
    if not first:
        out_shape.append(jax.ShapeDtypeStruct((1, EDGE), f32))
        out_shape.append(jax.ShapeDtypeStruct((1, slots), f32))
    arrays = [known] if first else [known, seen]
    arrays += kernels
    whole = pl.BlockSpec(memory_space=pltpu.VMEM)
    return pl.pallas_call(
        functools.partial(sweep_kernel, first, scale, lon_tiles, members),
        out_shape=out_shape,
        in_specs=[pl.BlockSpec(memory_space=pltpu.SMEM)] + [whole] * len(arrays),
        out_specs=[whole] * len(out_shape),
        scratch_shapes=[pltpu.VMEM((7 + 4 * members, tiles, slots), f32)],
        compiler_params=pltpu.CompilerParams(vmem_limit_bytes=32 * 1024 * 1024),
        name="sweep_first" if first else "sweep_second",
    )(tile, *arrays)


def ends_length(ends_ref):
    return length_of(jnp.sum(ends_ref[:, 0, EDGE:]), jnp.sum(ends_ref[:, 0, :EDGE]))


def field_kernel(scale, perturb_ref, length_ref, ends_ref, c1_ref, c2_ref, out_ref):
    members, fine_lat, fine_lon = perturb_ref.shape
    pieces, piece_rows, piece_cols = out_ref.shape
    across = fine_lon // piece_cols
    one = length_ref[0, 0]
    two = ends_length(ends_ref)

    def refined(count, cells, axis):
        shape = (count, cells) if axis == 0 else (cells, count)
        fine = lax.broadcasted_iota(jnp.int32, shape, axis).astype(f32)
        cell = lax.broadcasted_iota(jnp.int32, shape, 1 - axis).astype(f32)
        return jnp.maximum(1.0 - jnp.abs((fine + 2.5) * 0.25 - cell), 0.0).astype(bf16)

    to_rows = refined(fine_lat, ROWS, 0)
    to_cols = refined(fine_lon, COLS, 1)
    field = jnp.zeros((fine_lat, fine_lon), f32)
    for k in range(members):
        coarse = one * c1_ref[k] + two * c2_ref[k]
        high, low = split_two(coarse)
        tall = dot(to_rows, high) + dot(to_rows, low)
        high, low = split_two(tall)
        field = field + (dot(high, to_cols) + dot(low, to_cols)) * perturb_ref[k]
    field = -scale * field
    for n in range(pieces):
        i = n // across * piece_rows
        j = n % across * piece_cols
        out_ref[n] = field[i : i + piece_rows, j : j + piece_cols]


def analysis_kernel(length_ref, ends_ref, total_1_ref, total_2_ref, left_ref, right_ref, out_ref):
    one = length_ref[0, 0]
    two = ends_length(ends_ref)
    for k in range(out_ref.shape[0]):
        total = one * total_1_ref[k] + two * total_2_ref[k]
        half = jnp.dot(left_ref[...], total, precision=highest, preferred_element_type=f32)
        out_ref[k] = -jnp.dot(half, right_ref[...], precision=highest, preferred_element_type=f32)


def per_device(perturb, loc_lat, loc_lon, obs_cell, obs_count, obs_innov, obs_error):
    members, fine_lat, fine_lon = perturb.shape
    coarse_lat, coarse_lon = fine_lat // 4, fine_lon // 4
    groups = lax.axis_size(MEM)
    scale = 1.0 / math.sqrt(members * groups - 1)
    lat, lon = lax.axis_index(LAT), lax.axis_index("lon")
    lat_tiles, lon_tiles = lax.axis_size(LAT), lax.axis_size("lon")
    slots = obs_cell.shape[-1]
    total_lat, total_lon = lat_tiles * coarse_lat, lon_tiles * coarse_lon
    padded_lat, padded_lon = total_lat + 16, total_lon + 128
    tile = (lat * lon_tiles + lon).astype(jnp.int32).reshape(1)

    cell = obs_cell.reshape(1, slots)
    innovation = obs_innov.reshape(1, slots)
    error = obs_error.reshape(1, slots)
    message = picked(obs_count.reshape(1), perturb, cell, innovation, error)
    known = sent_to_all(message, TILES)

    first_lat, first_lon = lat * coarse_lat, lon * coarse_lon
    lat_all = kernel_block(loc_lat, -1, padded_lat, 0, total_lat)
    lon_all = kernel_block(loc_lon, -1, padded_lon, 0, total_lon)
    lat_tile = kernel_block(loc_lat, first_lat - 1, ROWS, 0, total_lat)
    lon_tile = kernel_block(loc_lon, first_lon - 1, COLS, 0, total_lon)
    left = jnp.einsum("ab,cb->ac", lat_tile, lat_all, precision=highest)
    right = jnp.einsum("ab,cb->ac", lon_all, lon_tile, precision=highest)
    left_own = kernel_block(loc_lat, -1, padded_lat, first_lat, coarse_lat).T
    right_own = kernel_block(loc_lon, -1, padded_lon, first_lon, coarse_lon)
    kernels = [*split_two(left), *split_two(right)]

    part, coarse_1, total_1 = sweep(tile, known, None, kernels, scale, lon_tiles, members, groups)
    mine = jnp.sum(lax.all_to_all(part, MEM, 0, 0, tiled=True), axis=0)
    seen = sent_to_all(mine, TILES)
    part, coarse_2, total_2, length_1, force = sweep(
        tile, known, seen, kernels, scale, lon_tiles, members, groups
    )
    mine = jnp.sum(lax.all_to_all(part, MEM, 0, 0, tiled=True), axis=0)
    inverse = known[tile[0], :, 2 * slots : 3 * slots]
    bent = jnp.stack([(mine * inverse) ** 2, mine * force])
    bent = jnp.sum(bent.reshape(2, slots // EDGE, EDGE), axis=1).reshape(1, 2 * EDGE)
    ends = sent_to_all(bent, TILES)

    whole = pl.BlockSpec(memory_space=pltpu.VMEM)
    piece_cols = 128
    piece_rows = fine_lat * fine_lon // groups // piece_cols
    pieces = pl.pallas_call(
        functools.partial(field_kernel, scale),
        out_shape=jax.ShapeDtypeStruct((groups, piece_rows, piece_cols), f32),
        in_specs=[whole] * 5,
        out_specs=whole,
        compiler_params=pltpu.CompilerParams(vmem_limit_bytes=24 * 1024 * 1024),
        name="field",
    )(perturb, length_1, ends, coarse_1, coarse_2)
    analysis = pl.pallas_call(
        analysis_kernel,
        out_shape=jax.ShapeDtypeStruct((members, coarse_lat, coarse_lon), f32),
        in_specs=[whole] * 6,
        out_specs=whole,
        compiler_params=pltpu.CompilerParams(vmem_limit_bytes=24 * 1024 * 1024),
        cost_estimate=pl.CostEstimate(flops=2 * 10**9, bytes_accessed=5 * 10**6, transcendentals=0),
        name="analysis",
    )(length_1, ends, total_1, total_2, left_own, right_own)
    summed = jnp.sum(lax.all_to_all(pieces, MEM, 0, 0, tiled=True), axis=0)
    everything = sent_to_all(summed, MEM)
    across = fine_lon // piece_cols
    increment = jnp.transpose(
        everything.reshape(fine_lat // piece_rows, across, piece_rows, piece_cols), (0, 2, 1, 3)
    ).reshape(fine_lat, fine_lon)
    return analysis, increment


def solution(mesh):
    torus = Mesh(
        mesh.devices.reshape(4, -1, 2, mesh.shape["lat"] // 2, mesh.shape["lon"]),
        ("mem_0", "mem_1", "lat_0", "lat_1", "lon"),
    )
    return jax.shard_map(
        per_device,
        mesh=torus,
        in_specs=(
            P(MEM, LAT, "lon"),
            P(),
            P(),
            P(LAT, "lon", None),
            P(LAT, "lon"),
            P(LAT, "lon", None),
            P(LAT, "lon", None),
        ),
        out_specs=(P(MEM, LAT, "lon"), P(LAT, "lon")),
        check_vma=False,
    )
```

time: 205 us -> 196 us (0.956)
  blocking collectives: 116 us -> 71.3 us
  waiting for transfers between devices: 12.7 us -> 39 us
  starting transfers between devices: 10.2 us -> 23.2 us
  local copies, waits for them, and re-layouts: 5.17 us -> 15.2 us
  Pallas kernels: 46.6 us -> 37.8 us
  other arithmetic: 5.03 us -> 1.52 us
    all_to_all x5 -> x2, blocking collectives: 92.3 us -> 25.5 us  [sent_to_all(): return lax.all_to_all(copies, axis, split_axis=0, concat_axis=0, tiled=True)]
    all_to_all x0 -> x1, blocking collectives: none -> 22.6 us  [per_device(): mine = jnp.sum(lax.all_to_all(part, MEM, 0, 0, tiled=True), axis=0)]
    all_to_all x1 -> x2, waiting for transfers between devices: 12.7 us -> 28.4 us  [sent_to_all(): return lax.all_to_all(copies, axis, split_axis=0, concat_axis=0, tiled=True)]
    all_to_all x0 -> x1, waiting for transfers between devices: none -> 10.5 us  [per_device(): mine = jnp.sum(lax.all_to_all(part, MEM, 0, 0, tiled=True), axis=0)]
    unnamed x13 -> x27, local copies, waits for them, and re-layouts: 2.52 us -> 12.1 us
    all_to_all x1 -> x2, starting transfers between devices: 10.2 us -> 19.1 us  [sent_to_all(): return lax.all_to_all(copies, axis, split_axis=0, concat_axis=0, tiled=True)]
    pallas_call x4 -> x5, Pallas kernels: 46.6 us -> 37.8 us  [the longest x2 29.9 us: sweep(): pl.pallas_call(functools.partial(sweep_kernel, first, scale, lon_tiles, m...]
    all_to_all x0 -> x1, starting transfers between devices: none -> 4.15 us  [per_device(): mine = jnp.sum(lax.all_to_all(part, MEM, 0, 0, tiled=True), axis=0)]
  transfers between devices with their start and end apart: 1 -> 3, of which waited for: 1 -> 3; matrix products, arithmetic and copies ran while one was open for 3% -> 2% of each run, Pallas kernels for 0% -> 1%
where the time goes in v2:
time: 196 us; the launch traced here: 192 us
  blocking collectives  71.3 us (36%)
  waiting for transfers between devices  39 us (20%)
  Pallas kernels  37.8 us (19%)
  starting transfers between devices  23.2 us (12%)
  local copies, waits for them, and re-layouts  15.2 us (8%)
  matrix products  2.96 us (2%)
    pallas_call x2, Pallas kernels, sweep(): pl.pallas_call(functools.partial(sweep_kernel, first, scale, lon_tiles, m...  29.9 us
    all_to_all x2, waiting for transfers between devices, sent_to_all(): return lax.all_to_all(copies, axis, split_axis=0, concat_axis=0, tiled=True)  28.4 us
    all_to_all x2, blocking collectives, sent_to_all(): return lax.all_to_all(copies, axis, split_axis=0, concat_axis=0, tiled=True)  25.5 us
    all_to_all x1, blocking collectives, per_device(): summed = jnp.sum(lax.all_to_all(pieces, MEM, 0, 0, tiled=True), axis=0)  23.2 us
    all_to_all x1, blocking collectives, per_device(): mine = jnp.sum(lax.all_to_all(part, MEM, 0, 0, tiled=True), axis=0)  22.6 us
    all_to_all x2, starting transfers between devices, sent_to_all(): return lax.all_to_all(copies, axis, split_axis=0, concat_axis=0, tiled=True)  19.1 us
    unnamed x27, local copies, waits for them, and re-layouts  12.1 us
    all_to_all x1, waiting for transfers between devices, per_device(): mine = jnp.sum(lax.all_to_all(part, MEM, 0, 0, tiled=True), axis=0)  10.5 us
  transfers between devices with their start and end apart: 3, of which 3 were waited for; matrix products, arithmetic and copies ran while one was open for 2% of the time, Pallas kernels for 1%

profile of v2, /device:TPU:1, one launch (start us, length us, event | category | flops | bytes accessed | tf_op | source)
XLA Modules:
  0.0 192.5 jit_solution(7846743244244852990)
XLA Ops:
  1.3 1.4 copy-done
  2.7 0.7 copy-done.4
  3.4 0.7 copy-done.5
  4.1 0.7 copy-done.6
  4.8 4.0 %picked.1 = f32[1,10240]{1,0:T(1,128)S(1)} custom-call(s32[1]{0:T(128)} %bitcast.19.count_ref, f32[2,384,512]{2,1,0:T(8,128)S(1)} %copy-done, s32[1,2048]{1,0:T(1,128)S(1)} %bitcast.21, f32[1,2048]{1,0:T(1,128)S(1)} %bitcast.22, f32[1,2048]{1,0:T(1,128)S(1)} %bitcast.23), custom_call_target="tpu_custom_call" | custom-call | tf_op jit(solution)/shard_map/picked/pallas_call | solution.py:92
  8.8 1.2 broadcast_in_dim.12
  9.9 10.2 %all-to-all-start = ((f32[16,1,10240]{2,1,0:T(1,128)}), f32[16,1,10240]{2,1,0:T(1,128)S(1)}, u32[]{:S(2)}, u32[]{:S(2)}) async-start(f32[16,1,10240]{2,1,0:T(1,128)} %broadcast_in_dim.12), calls=%async_computation | async-start | bytes 1310720 | tf_op jit(solution)/shard_map/all_to_all | solution.py:28
  20.2 0.1 power_select_fusion
  20.3 0.1 and_select_fusion
  20.4 2.0 %fusion.55 = (bf16[640,144]{0,1:T(8,128)(2,1)S(1)}, f32[640,144]{0,1:T(8,128)S(1)}) fusion(f32[512]{0:T(512)S(1)} %integer_pow.46, f32[144]{0:T(256)S(1)} %get-tuple-element.19, s32[144]{0:T(256)S(1)} %iota_add_fusion.2, f32[144]{0:T(256)S(1)} %get-tuple-element.18, f32[640]{0:T(1024)S(1)} %get-tuple-element.21, s32[640]{0:T(1024)S(1)} %iota_add_fusion, ...), kind=kOutput, calls=%fused_computation.78 | convolution fusion | flops 569133056 | bytes 564416 | tf_op jit(solution)/shard_map/ab,cb->ac/dot_general | solution.py:315
  22.4 0.2 copy.27.refs_4_.refs_5_
  22.6 0.2 copy.25
  22.8 0.2 copy-done.11
  23.1 0.1 and_select_fusion.1
  23.2 0.1 power_select_fusion.1
  23.3 1.0 fusion.54
  24.2 0.1 copy.26.refs_2_.refs_3_
  24.3 0.1 copy.23
  24.5 0.1 subtract_convert_fusion.refs_5_.refs_6_
  24.6 15.2 %all-to-all-done.refs_1_ = f32[16,1,10240]{2,1,0:T(1,128)S(1)} async-done(((f32[16,1,10240]{2,1,0:T(1,128)}), f32[16,1,10240]{2,1,0:T(1,128)S(1)}, u32[]{:S(2)}, u32[]{:S(2)}) %all-to-all-start) | async-done | bytes 655392 | tf_op jit(solution)/shard_map/all_to_all | solution.py:28
  39.8 14.2 %sweep_first.1 = (f32[32,1,2048]{2,1,0:T(1,128)S(1)}, f32[2,112,144]{2,1,0:T(8,128)S(1)}, f32[2,400,640]{2,1,0:T(8,128)S(1)}) custom-call(s32[1]{0:T(128)} %bitcast.refs_0_, f32[16,1,10240]{2,1,0:T(1,128)S(1)} %all-to-all-done.refs_1_, bf16[112,400]{1,0:T(8,128)(2,1)S(1)} %copy.26.refs_2_.refs_3_, ...), custom_call_target="tpu_custom_call" | custom-call | tf_op jit(solution)/shard_map/sweep_first/pallas_call | solution.py:238
  54.0 1.3 copy-done.7
  55.4 22.6 %all_to_all.35 = f32[32,1,2048]{2,1,0:T(1,128)S(1)} all-to-all(f32[32,1,2048]{2,1,0:T(1,128)S(1)} %get-tuple-element.10), channel_id=1, replica_groups=mesh['mem_0'=4,'mem_1'=8,'lat_0'=2,'lat_1'=2,'lon'=4] {'mem_0','mem_1'}, dimensions={0} | all-to-all | bytes 524288 | tf_op jit(solution)/shard_map/all_to_all | solution.py:321
  78.0 0.2 reduce_sum.40
  78.1 0.1 broadcast_in_dim.15
  78.2 13.3 %all_to_all.36.refs_2_ = f32[16,1,2048]{2,1,0:T(1,128)S(1)} all-to-all(f32[16,1,2048]{2,1,0:T(1,128)S(1)} %broadcast_in_dim.15), channel_id=1, replica_groups=mesh['mem_0'=4,'mem_1'=8,'lat_0'=2,'lat_1'=2,'lon'=4] {'lat_0','lat_1','..., dimensions={0} | all-to-all | bytes 262144 | tf_op jit(solution)/shard_map/all_to_all | solution.py:28
  91.5 15.7 %sweep_second.1 = (f32[32,1,2048]{2,1,0:T(1,128)}, f32[2,112,144]{2,1,0:T(8,128)S(1)}, f32[2,400,640]{2,1,0:T(8,128)S(1)}, f32[1,128]{1,0:T(1,128)S(1)}, f32[1,2048]{1,0:T(1,128)S(1)}) custom-call(s32[1]{0:T(128)} %bitcast.refs_0_, f32[16,1,10240]{2,1,0:T(1,128)S(1)} %all-to-all-done.refs_1_, f32[16,1,2048]{2,1,0:T(1,128)S(1)} %all_to_all.36.refs_2_, ...), custom_call_target="tpu_custom_call" | custom-call | tf_op jit(solution)/shard_map/sweep_second/pallas_call | solution.py:238
  107.2 0.7 copy-done.2
  107.9 1.3 copy-done.9
  109.2 4.2 %all-to-all-start.3 = ((f32[32,1,2048]{2,1,0:T(1,128)}), f32[32,1,2048]{2,1,0:T(1,128)S(1)}, u32[]{:S(2)}, u32[]{:S(2)}) async-start(f32[32,1,2048]{2,1,0:T(1,128)} %get-tuple-element.12), calls=%async_computation.3 | async-start | bytes 524288 | tf_op jit(solution)/shard_map/all_to_all | solution.py:326
  113.3 10.5 %all-to-all-done.3 = f32[32,1,2048]{2,1,0:T(1,128)S(1)} async-done(((f32[32,1,2048]{2,1,0:T(1,128)}), f32[32,1,2048]{2,1,0:T(1,128)S(1)}, u32[]{:S(2)}, u32[]{:S(2)}) %all-to-all-start.3) | async-done | bytes 262176 | tf_op jit(solution)/shard_map/all_to_all | solution.py:326
  123.9 0.2 reduce_sum.41
  124.1 12.2 %all_to_all.37.ends_ref = f32[16,1,256]{2,1,0:T(1,128)S(1)} all-to-all(f32[16,1,256]{2,1,0:T(1,128)S(1)} %broadcast_in_dim.16), channel_id=1, replica_groups=mesh['mem_0'=4,'mem_1'=8,'lat_0'=2,'lat_1'=2,'lon'=4] {'lat_0','lat_1','..., dimensions={0} | all-to-all | bytes 32768 | tf_op jit(solution)/shard_map/all_to_all | solution.py:28
  136.3 0.9 copy-done.3
  137.2 1.2 field.1
  138.4 23.2 %all_to_all.38 = f32[32,48,128]{2,1,0:T(8,128)S(1)} all-to-all(f32[32,48,128]{2,1,0:T(8,128)S(1)} %field.1), channel_id=1, replica_groups=mesh['mem_0'=4,'mem_1'=8,'lat_0'=2,'lat_1'=2,'lon'=4] {'mem_0','mem_1'}, dimensions={0} | all-to-all | bytes 1572864 | tf_op jit(solution)/shard_map/all_to_all | solution.py:352
  161.7 0.9 broadcast_in_dim.17
  162.6 8.9 %all-to-all-start.6 = ((f32[32,48,128]{2,1,0:T(8,128)}), f32[32,48,128]{2,1,0:T(8,128)S(1)}, u32[]{:S(2)}, u32[]{:S(2)}) async-start(f32[32,48,128]{2,1,0:T(8,128)} %broadcast_in_dim.17), calls=%async_computation.6 | async-start | bytes 1572864 | tf_op jit(solution)/shard_map/all_to_all | solution.py:28
  171.5 0.1 fusion.50
  171.6 0.1 fusion.51
  171.6 0.1 fusion.31.left_ref
  171.8 0.3 fusion.16.right_ref
  172.1 1.6 copy-done.8
  173.7 1.6 copy-done.10
  175.3 2.8 %analysis.1 = f32[2,96,128]{2,1,0:T(8,128)} custom-call(f32[1,128]{1,0:T(1,128)S(1)} %get-tuple-element.11.length_ref, f32[16,1,256]{2,1,0:T(1,128)S(1)} %all_to_all.37.ends_ref, f32[2,400,640]{2,1,0:T(8,128)S(1)} %copy-done.8, f32[2,400,640]{2,1,0:T(8,128)S(1)} %copy-done.10, f32[96,400]{1,0:T(8,128)S(1)} %fusion.31.left_ref, f32[640,128]{1,0:T(8,128)S(1)} %fusion.16.right_ref), custom_call_target="tpu_custom_call" | custom-call | flops 2000000000 | bytes 5000000 | tf_op jit(solution)/shard_map/analysis/pallas_call | solution.py:343
  178.1 13.2 %all-to-all-done.6 = f32[32,48,128]{2,1,0:T(8,128)S(1)} async-done(((f32[32,48,128]{2,1,0:T(8,128)}), f32[32,48,128]{2,1,0:T(8,128)S(1)}, u32[]{:S(2)}, u32[]{:S(2)}) %all-to-all-start.6) | async-done | bytes 786464 | tf_op jit(solution)/shard_map/all_to_all | solution.py:28
  191.2 0.3 copy.30
  191.6 0.9 copy.33
  (29 shorter events, 0.2 us)
Async XLA Ops:
  1.3 1.4 copy-start
  2.7 0.7 copy-start.4
  3.4 0.7 copy-start.5
  4.1 0.7 copy-start.6
  8.7 11.4 %copy-start.12 = (f32[512]{0:T(512)S(1)}, f32[512]{0:T(512)}, u32[]{:S(2)}) copy-start(f32[512]{0:T(512)} %param.9) | copy-start | bytes 6148
  9.9 29.9 %all-to-all-start = ((f32[16,1,10240]{2,1,0:T(1,128)}), f32[16,1,10240]{2,1,0:T(1,128)S(1)}, u32[]{:S(2)}, u32[]{:S(2)}) async-start(f32[16,1,10240]{2,1,0:T(1,128)} %broadcast_in_dim.12), calls=%async_computation | async-start | bytes 1310720 | tf_op jit(solution)/shard_map/all_to_all | solution.py:28
  22.4 0.7 copy-start.11
  54.0 1.3 copy-start.7
  91.5 44.8 %copy-start.1 = (f32[2,384,512]{2,1,0:T(8,128)S(1)}, f32[2,384,512]{2,1,0:T(8,128)}, u32[]{:S(2)}) copy-start(f32[2,384,512]{2,1,0:T(8,128)} %perturb_ref.3) | copy-start | bytes 4718596
  107.2 0.7 copy-start.2
  107.9 1.3 copy-start.9
  109.2 14.7 %all-to-all-start.3 = ((f32[32,1,2048]{2,1,0:T(1,128)}), f32[32,1,2048]{2,1,0:T(1,128)S(1)}, u32[]{:S(2)}, u32[]{:S(2)}) async-start(f32[32,1,2048]{2,1,0:T(1,128)} %get-tuple-element.12), calls=%async_computation.3 | async-start | bytes 524288 | tf_op jit(solution)/shard_map/all_to_all | solution.py:326
  136.3 0.9 copy-start.3
  162.6 28.7 %all-to-all-start.6 = ((f32[32,48,128]{2,1,0:T(8,128)}), f32[32,48,128]{2,1,0:T(8,128)S(1)}, u32[]{:S(2)}, u32[]{:S(2)}) async-start(f32[32,48,128]{2,1,0:T(8,128)} %broadcast_in_dim.17), calls=%async_computation.6 | async-start | bytes 1572864 | tf_op jit(solution)/shard_map/all_to_all | solution.py:28
  172.1 1.6 copy-start.8
  173.7 1.6 copy-start.10

commit v3 on v2

--- a/solution.py
+++ b/solution.py
@@ -20,7 +20,8 @@
 
 ROWS = 112
 COLS = 144
-EDGE = 128
+LANES = 128
+TOGETHER = 2
 
 
 def sent_to_all(x, axis):
@@ -60,20 +61,27 @@
     return jnp.dot(a, b, preferred_element_type=f32)
 
 
+def lane_rows(read, count):
+    return jnp.concatenate([read(r) for r in range(count)], axis=1)
+
+
 def picked_kernel(count_ref, perturb_ref, cell_ref, innov_ref, error_ref, out_ref):
     members, fine_lat, fine_lon = perturb_ref.shape
-    slots = cell_ref.shape[-1]
+    lines = cell_ref.shape[0]
     step = 512
-    slot = lax.broadcasted_iota(jnp.int32, (1, slots), 1)
-    out_ref[:, :slots] = cell_ref[...].astype(f32)
-    out_ref[:, slots : 2 * slots] = innov_ref[...]
-    out_ref[:, 2 * slots : 3 * slots] = jnp.where(slot < count_ref[0], 1.0 / error_ref[...], 0.0)
+    per_step = step // LANES
+    slot = lax.broadcasted_iota(jnp.int32, cell_ref.shape, 0) * LANES + lax.broadcasted_iota(
+        jnp.int32, cell_ref.shape, 1
+    )
+    out_ref[:lines] = cell_ref[...].astype(f32)
+    out_ref[lines : 2 * lines] = innov_ref[...]
+    out_ref[2 * lines : 3 * lines] = jnp.where(slot < count_ref[0], 1.0 / error_ref[...], 0.0)
     blocks = []
     for k in range(members):
         blocks.append(jnp.concatenate(split_two(perturb_ref[k]), axis=1))
     field = jnp.concatenate(blocks, axis=0)
-    for start in range(0, slots, step):
-        cell = cell_ref[:, start : start + step]
+    for start in range(0, lines, per_step):
+        cell = lane_rows(lambda r: cell_ref[start + r : start + r + 1, :], per_step)
         row = cell // fine_lon
         col = cell - row * fine_lon
         at_col = lax.broadcasted_iota(jnp.int32, (fine_lon, step), 0) == col
@@ -82,8 +90,10 @@
         at_row = lax.broadcasted_iota(jnp.int32, (fine_lat, step), 0) == row
         for k in range(members):
             mine = values[k * fine_lat : (k + 1) * fine_lat]
-            at = (3 + k) * slots + start
-            out_ref[:, at : at + step] = jnp.sum(jnp.where(at_row, mine, 0.0), axis=0, keepdims=True)
+            found = jnp.sum(jnp.where(at_row, mine, 0.0), axis=0, keepdims=True)
+            for r in range(per_step):
+                at = (3 + k) * lines + start + r
+                out_ref[at : at + 1, :] = found[:, r * LANES : (r + 1) * LANES]
 
 
 def picked(count, perturb, cell, innovation, error):
@@ -91,10 +101,10 @@
     fields = 3 + perturb.shape[0]
     return pl.pallas_call(
         picked_kernel,
-        out_shape=jax.ShapeDtypeStruct((1, fields * cell.shape[-1]), f32),
+        out_shape=jax.ShapeDtypeStruct((fields * cell.shape[0], LANES), f32),
         in_specs=[pl.BlockSpec(memory_space=pltpu.SMEM)] + [whole] * 4,
         out_specs=whole,
-        compiler_params=pltpu.CompilerParams(vmem_limit_bytes=24 * 1024 * 1024),
+        compiler_params=pltpu.CompilerParams(vmem_limit_bytes=60 * 1024 * 1024),
         name="picked",
     )(count, perturb, cell, innovation, error)
 
@@ -108,17 +118,19 @@
     return grad_total / (grad_total + curvature + tiny_floor)
 
 
-def hat(below, lower, upper, count):
-    groups = []
-    wide = (16, below.shape[-1])
-    below, lower, upper = (jnp.broadcast_to(x, wide).astype(bf16) for x in (below, lower, upper))
-    zero = jnp.zeros(wide, bf16)
-    cell = lax.broadcasted_iota(jnp.int32, wide, 0).astype(f32)
+def masks(below, count):
+    cell = lax.broadcasted_iota(jnp.int32, below.shape, 0).astype(f32)
+    found = []
     for start in range(0, count, 16):
         at = (cell + start).astype(bf16)
         before = (cell + (start - 1)).astype(bf16)
-        groups.append(jnp.where(below == at, lower, jnp.where(below == before, upper, zero)))
-    return jnp.concatenate(groups, axis=0)
+        found.append((below == at, below == before))
+    return found
+
+
+def hat(where, lower, upper):
+    zero = jnp.zeros_like(lower)
+    return jnp.concatenate([jnp.where(at, lower, jnp.where(before, upper, zero)) for at, before in where], axis=0)
 
 
 def sweep_kernel(first, scale, lon_tiles, members, *refs):
@@ -127,18 +139,18 @@
     if not first:
         seen_ref = refs[0]
         refs = refs[1:]
-    left_ref, left_low_ref, right_ref, right_low_ref, part_ref, coarse_ref, total_ref = refs[:7]
+    left_ref, left_low_ref, right_ref, right_low_ref, part_ref, coarse_ref, total_out_ref = refs[:7]
     refs = refs[7:]
     if not first:
-        length_ref, force_ref = refs[:2]
+        length_ref, own_ref = refs[:2]
         refs = refs[2:]
-    hold = refs[0]
+    hold, total_ref, coarse_own_ref, image_ref, sems = refs
     tiles = known_ref.shape[0]
-    slots = known_ref.shape[2] // (3 + members)
+    lines = known_ref.shape[1] // (3 + members)
     width = total_ref.shape[2]
 
     def known(n):
-        return known_ref[:, 0, n * slots : (n + 1) * slots]
+        return known_ref[:, n * lines : (n + 1) * lines, :]
 
     cell = known(0)
     innovation = known(1)
@@ -152,7 +164,7 @@
     hold[4], hold[5] = 1.0 - row_up, row_up
     force = weights_of(0.0, innovation, inverse)
     if not first:
-        image = seen_ref[:, 0, :slots]
+        image = seen_ref[...]
         length = length_of(jnp.sum(force * image), jnp.sum((image * inverse) ** 2))
         force = weights_of(-length * image, innovation, inverse) - length * force
         length_ref[...] = jnp.broadcast_to(length, length_ref.shape)
@@ -168,89 +180,120 @@
             n += 2
     total_ref[...] = jnp.zeros_like(total_ref)
 
-    def one_tile(t, carry):
+    def line(i, t):
+        return lane_rows(
+            lambda r: jnp.broadcast_to(hold[i, t, r : r + 1, :], (16, LANES)).astype(bf16), lines
+        )
+
+    def add_tile(t):
         lat = t // lon_tiles
         lon = t - lat * lon_tiles
-
-        def line(i):
-            return hold[i, pl.ds(t, 1), :]
-
-        cols = hat(line(1), line(2), line(3), COLS)
+        cols = hat(masks(line(1, t), COLS), line(2, t), line(3, t))
+        where = masks(line(0, t), ROWS)
         blocks = []
         for k in range(members):
             for term in range(2):
                 at = 7 + 4 * k + term
-                blocks.append(hat(line(0), line(at), line(at + 2), ROWS))
+                blocks.append(hat(where, line(at, t), line(at + 2, t)))
         made = nt_dot(jnp.concatenate(blocks, axis=0), cols)
         at = pl.ds(pl.multiple_of(lat * 96, 8), ROWS)
         for k in range(members):
             both = made[2 * k * ROWS : (2 * k + 1) * ROWS] + made[(2 * k + 1) * ROWS : (2 * k + 2) * ROWS]
             total_ref[k, at, pl.ds(pl.multiple_of(lon * 128, 128), 128)] += both[:, :128]
             total_ref[k, at, pl.ds(pl.multiple_of(lon * 128 + 128, 128), COLS - 128)] += both[:, 128:]
+
+    def some_tiles(t, carry):
+        for n in range(TOGETHER):
+            add_tile(t * TOGETHER + n)
         return carry
 
-    lax.fori_loop(0, tiles, one_tile, 0)
+    lax.fori_loop(0, tiles // TOGETHER, some_tiles, 0)
+    total_copy = pltpu.make_async_copy(total_ref, total_out_ref, sems.at[0])
+    total_copy.start()
 
     own = tile_ref[0]
-
-    def own_line(i):
-        return hold[i, pl.ds(own, 1), :]
-
-    rows = hat(own_line(0), own_line(4), own_line(5), ROWS).astype(f32)
-    cols = hat(own_line(1), own_line(2), own_line(3), COLS)
+    rows = hat(masks(line(0, own), ROWS), line(4, own), line(5, own)).astype(f32)
+    cols = hat(masks(line(1, own), COLS), line(2, own), line(3, own))
     high, low = zip(*(split_two(total_ref[k]) for k in range(members)))
     high, low = jnp.concatenate(high, axis=1), jnp.concatenate(low, axis=1)
-    half = dot(left_ref[...], high) + (dot(left_ref[...], low) + dot(left_low_ref[...], high))
+    half = dot(jnp.concatenate([left_ref[...], left_low_ref[...]], axis=0), high)
+    half = half[:ROWS] + (half[ROWS:] + dot(left_ref[...], low))
     half = jnp.concatenate([half[:, k * width : (k + 1) * width] for k in range(members)], axis=0)
     high, low = split_two(half)
-    coarse = dot(high, right_ref[...]) + (dot(low, right_ref[...]) + dot(high, right_low_ref[...]))
-    image = jnp.zeros((1, slots), f32)
-    for k in range(members):
-        mine = coarse[k * ROWS : (k + 1) * ROWS]
-        coarse_ref[k] = mine
-        high, low = split_two(mine)
-        made = dot(high, cols) + dot(low, cols)
-        value = jnp.sum(made * rows, axis=0, keepdims=True)
-        image = image + value * known_ref[own, :, (3 + k) * slots : (4 + k) * slots]
+    count = high.shape[0]
+    coarse = dot(jnp.concatenate([high, low], axis=0), right_ref[...])
+    coarse = coarse[:count] + (coarse[count:] + dot(high, right_low_ref[...]))
+    for k in range(members):
+        coarse_own_ref[k] = coarse[k * ROWS : (k + 1) * ROWS]
+    coarse_copy = pltpu.make_async_copy(coarse_own_ref, coarse_ref, sems.at[1])
+    coarse_copy.start()
+    made = dot(jnp.concatenate(split_two(coarse), axis=0), cols)
+    for k in range(members):
+        mine = made[k * ROWS : (k + 1) * ROWS] + made[count + k * ROWS : count + (k + 1) * ROWS]
+        value = jnp.sum(mine * rows, axis=0, keepdims=True)
+        for r in range(lines):
+            image_ref[k, r : r + 1, :] = value[:, r * LANES : (r + 1) * LANES]
+    image = jnp.zeros((lines, LANES), f32)
+    for k in range(members):
+        image = image + image_ref[k] * known_ref[own, (3 + k) * lines : (4 + k) * lines, :]
     image = image * scale
     if not first:
-        force_ref[...] = own_line(6)
+        own_ref[0] = known_ref[own, 2 * lines : 3 * lines, :]
+        own_ref[1] = hold[6, own]
     for n in range(part_ref.shape[0]):
-        part_ref[n, :, :slots] = image
+        part_ref[n] = image
+    coarse_copy.wait()
+    total_copy.wait()
 
 
 def sweep(tile, known, seen, kernels, scale, lon_tiles, members, groups):
-    slots = known.shape[2] // (3 + members)
     tiles = known.shape[0]
+    lines = known.shape[1] // (3 + members)
     first = seen is None
     left, _, right, _ = kernels
+    total = (members, left.shape[1], right.shape[0])
+    whole = pl.BlockSpec(memory_space=pltpu.VMEM)
     out_shape = [
-        jax.ShapeDtypeStruct((groups, 1, slots), f32),
-        jax.ShapeDtypeStruct((members, ROWS, COLS), f32),
-        jax.ShapeDtypeStruct((members, left.shape[1], right.shape[0]), f32),
+        jax.ShapeDtypeStruct((groups, lines, LANES), f32),
+        pltpu.HBM((members, ROWS, COLS), f32),
+        pltpu.HBM(total, f32),
     ]
+    far = pl.BlockSpec(memory_space=pltpu.HBM)
+    out_specs = [whole, far, far]
     if not first:
-        out_shape.append(jax.ShapeDtypeStruct((1, EDGE), f32))
-        out_shape.append(jax.ShapeDtypeStruct((1, slots), f32))
+        out_shape.append(jax.ShapeDtypeStruct((1, LANES), f32))
+        out_shape.append(jax.ShapeDtypeStruct((2, lines, LANES), f32))
+        out_specs += [whole, whole]
     arrays = [known] if first else [known, seen]
     arrays += kernels
-    whole = pl.BlockSpec(memory_space=pltpu.VMEM)
     return pl.pallas_call(
         functools.partial(sweep_kernel, first, scale, lon_tiles, members),
         out_shape=out_shape,
         in_specs=[pl.BlockSpec(memory_space=pltpu.SMEM)] + [whole] * len(arrays),
-        out_specs=[whole] * len(out_shape),
-        scratch_shapes=[pltpu.VMEM((7 + 4 * members, tiles, slots), f32)],
-        compiler_params=pltpu.CompilerParams(vmem_limit_bytes=32 * 1024 * 1024),
+        out_specs=out_specs,
+        scratch_shapes=[
+            pltpu.VMEM((7 + 4 * members, tiles, lines, LANES), f32),
+            pltpu.VMEM(total, f32),
+            pltpu.VMEM((members, ROWS, COLS), f32),
+            pltpu.VMEM((members, lines, LANES), f32),
+            pltpu.SemaphoreType.DMA((2,)),
+        ],
+        compiler_params=pltpu.CompilerParams(vmem_limit_bytes=24 * 1024 * 1024),
         name="sweep_first" if first else "sweep_second",
     )(tile, *arrays)
 
 
 def ends_length(ends_ref):
-    return length_of(jnp.sum(ends_ref[:, 0, EDGE:]), jnp.sum(ends_ref[:, 0, :EDGE]))
-
-
-def field_kernel(scale, perturb_ref, length_ref, ends_ref, c1_ref, c2_ref, out_ref):
+    return length_of(jnp.sum(ends_ref[:, 1, :]), jnp.sum(ends_ref[:, 0, :]))
+
+
+def field_kernel(scale, perturb_ref, length_ref, ends_ref, c1_far, c2_far, out_ref, c1_ref, c2_ref, sems):
+    copies = [
+        pltpu.make_async_copy(c1_far, c1_ref, sems.at[0]),
+        pltpu.make_async_copy(c2_far, c2_ref, sems.at[1]),
+    ]
+    for copy in copies:
+        copy.start()
     members, fine_lat, fine_lon = perturb_ref.shape
     pieces, piece_rows, piece_cols = out_ref.shape
     across = fine_lon // piece_cols
@@ -266,6 +309,8 @@
     to_rows = refined(fine_lat, ROWS, 0)
     to_cols = refined(fine_lon, COLS, 1)
     field = jnp.zeros((fine_lat, fine_lon), f32)
+    for copy in copies:
+        copy.wait()
     for k in range(members):
         coarse = one * c1_ref[k] + two * c2_ref[k]
         high, low = split_two(coarse)
@@ -273,10 +318,11 @@
         high, low = split_two(tall)
         field = field + (dot(high, to_cols) + dot(low, to_cols)) * perturb_ref[k]
     field = -scale * field
-    for n in range(pieces):
-        i = n // across * piece_rows
+    for n in range(pieces * piece_rows // 8):
+        i = n // across * 8
         j = n % across * piece_cols
-        out_ref[n] = field[i : i + piece_rows, j : j + piece_cols]
+        at = n * 8 % piece_rows
+        out_ref[n * 8 // piece_rows, at : at + 8, :] = field[i : i + 8, j : j + piece_cols]
 
 
 def analysis_kernel(length_ref, ends_ref, total_1_ref, total_2_ref, left_ref, right_ref, out_ref):
@@ -300,9 +346,10 @@
     padded_lat, padded_lon = total_lat + 16, total_lon + 128
     tile = (lat * lon_tiles + lon).astype(jnp.int32).reshape(1)
 
-    cell = obs_cell.reshape(1, slots)
-    innovation = obs_innov.reshape(1, slots)
-    error = obs_error.reshape(1, slots)
+    lines = slots // LANES
+    cell = obs_cell.reshape(lines, LANES)
+    innovation = obs_innov.reshape(lines, LANES)
+    error = obs_error.reshape(lines, LANES)
     message = picked(obs_count.reshape(1), perturb, cell, innovation, error)
     known = sent_to_all(message, TILES)
 
@@ -320,13 +367,11 @@
     part, coarse_1, total_1 = sweep(tile, known, None, kernels, scale, lon_tiles, members, groups)
     mine = jnp.sum(lax.all_to_all(part, MEM, 0, 0, tiled=True), axis=0)
     seen = sent_to_all(mine, TILES)
-    part, coarse_2, total_2, length_1, force = sweep(
+    part, coarse_2, total_2, length_1, own = sweep(
         tile, known, seen, kernels, scale, lon_tiles, members, groups
     )
     mine = jnp.sum(lax.all_to_all(part, MEM, 0, 0, tiled=True), axis=0)
-    inverse = known[tile[0], :, 2 * slots : 3 * slots]
-    bent = jnp.stack([(mine * inverse) ** 2, mine * force])
-    bent = jnp.sum(bent.reshape(2, slots // EDGE, EDGE), axis=1).reshape(1, 2 * EDGE)
+    bent = jnp.sum(jnp.stack([(mine * own[0]) ** 2, mine * own[1]]), axis=1)
     ends = sent_to_all(bent, TILES)
 
     whole = pl.BlockSpec(memory_space=pltpu.VMEM)
@@ -335,8 +380,13 @@
     pieces = pl.pallas_call(
         functools.partial(field_kernel, scale),
         out_shape=jax.ShapeDtypeStruct((groups, piece_rows, piece_cols), f32),
-        in_specs=[whole] * 5,
+        in_specs=[whole] * 3 + [pl.BlockSpec(memory_space=pltpu.HBM)] * 2,
         out_specs=whole,
+        scratch_shapes=[
+            pltpu.VMEM((members, ROWS, COLS), f32),
+            pltpu.VMEM((members, ROWS, COLS), f32),
+            pltpu.SemaphoreType.DMA((2,)),
+        ],
         compiler_params=pltpu.CompilerParams(vmem_limit_bytes=24 * 1024 * 1024),
         name="field",
     )(perturb, length_1, ends, coarse_1, coarse_2)
@@ -353,7 +403,7 @@
     everything = sent_to_all(summed, MEM)
     across = fine_lon // piece_cols
     increment = jnp.transpose(
-        everything.reshape(fine_lat // piece_rows, across, piece_rows, piece_cols), (0, 2, 1, 3)
+        everything.reshape(fine_lat // 8, across, 8, piece_cols), (0, 2, 1, 3)
     ).reshape(fine_lat, fine_lon)
     return analysis, increment
 

time: 196 us -> 186 us (0.949)
  blocking collectives: 71.3 us -> 85.7 us
  waiting for transfers between devices: 39 us -> 28.4 us
  local copies, waits for them, and re-layouts: 15.2 us -> 8.48 us
  starting transfers between devices: 23.2 us -> 19.1 us
  Pallas kernels: 37.8 us -> 35.4 us
    all_to_all x1 -> x2, blocking collectives: 22.6 us -> 37 us  [per_device(): mine = jnp.sum(lax.all_to_all(part, MEM, 0, 0, tiled=True), axis=0)]
    all_to_all x1 -> x0, waiting for transfers between devices: 10.5 us -> none  [per_device(): mine = jnp.sum(lax.all_to_all(part, MEM, 0, 0, tiled=True), axis=0)]
    unnamed x27 -> x15, local copies, waits for them, and re-layouts: 12.1 us -> 5.21 us
    pallas_call x2, Pallas kernels: 29.9 us -> 24.9 us  [sweep(): pl.pallas_call(functools.partial(sweep_kernel, first, scale, lon_tiles, m...]
    all_to_all x1 -> x0, starting transfers between devices: 4.15 us -> none  [per_device(): mine = jnp.sum(lax.all_to_all(part, MEM, 0, 0, tiled=True), axis=0)]
    pallas_call x1, Pallas kernels: 3.96 us -> 5.94 us  [picked(): pl.pallas_call(picked_kernel, out_shape=jax.ShapeDtypeStruct((fields * ce...]
  transfers between devices with their start and end apart: 3 -> 2, of which waited for: 3 -> 2; matrix products, arithmetic and copies ran while one was open for 2% -> 3% of each run, Pallas kernels for 1% -> 2%
where the time goes in v3:
time: 186 us; the launch traced here: 183 us
  blocking collectives  85.7 us (46%)
  Pallas kernels  35.4 us (19%)
  waiting for transfers between devices  28.4 us (15%)
  starting transfers between devices  19.1 us (10%)
  local copies, waits for them, and re-layouts  8.48 us (5%)
  matrix products  2.96 us (2%)
    all_to_all x2, blocking collectives, per_device(): mine = jnp.sum(lax.all_to_all(part, MEM, 0, 0, tiled=True), axis=0)  37 us
    all_to_all x2, waiting for transfers between devices, sent_to_all(): return lax.all_to_all(copies, axis, split_axis=0, concat_axis=0, tiled=True)  28.4 us
    all_to_all x2, blocking collectives, sent_to_all(): return lax.all_to_all(copies, axis, split_axis=0, concat_axis=0, tiled=True)  25.6 us
    pallas_call x2, Pallas kernels, sweep(): pl.pallas_call(functools.partial(sweep_kernel, first, scale, lon_tiles, m...  24.9 us
    all_to_all x1, blocking collectives, per_device(): summed = jnp.sum(lax.all_to_all(pieces, MEM, 0, 0, tiled=True), axis=0)  23.2 us
    all_to_all x2, starting transfers between devices, sent_to_all(): return lax.all_to_all(copies, axis, split_axis=0, concat_axis=0, tiled=True)  19.1 us
    pallas_call x1, Pallas kernels, picked(): pl.pallas_call(picked_kernel, out_shape=jax.ShapeDtypeStruct((fields * ce...  5.94 us
    unnamed x15, local copies, waits for them, and re-layouts  5.21 us
  transfers between devices with their start and end apart: 2, of which 2 were waited for; matrix products, arithmetic and copies ran while one was open for 3% of the time, Pallas kernels for 2%

profile of v3, /device:TPU:1, one launch (start us, length us, event | category | flops | bytes accessed | tf_op | source)
XLA Modules:
  0.0 182.8 jit_solution(4152845697308451729)
XLA Ops:
  1.3 5.9 %picked.1 = f32[80,128]{1,0:T(8,128)} custom-call(s32[1]{0:T(128)} %bitcast.15.count_ref, f32[2,384,512]{2,1,0:T(8,128)} %perturb_ref.3, s32[16,128]{1,0:T(8,128)} %bitcast.17, f32[16,128]{1,0:T(8,128)} %bitcast.18, f32[16,128]{1,0:T(8,128)} %bitcast.19), custom_call_target="tpu_custom_call" | custom-call | tf_op jit(solution)/shard_map/picked/pallas_call | solution.py:102
  7.2 0.0 copy-start.6
  7.2 1.7 broadcast_in_dim.12
  8.9 10.2 %all-to-all-start = ((f32[16,80,128]{2,1,0:T(8,128)}), f32[16,80,128]{2,1,0:T(8,128)S(1)}, u32[]{:S(2)}, u32[]{:S(2)}) async-start(f32[16,80,128]{2,1,0:T(8,128)} %broadcast_in_dim.12), calls=%async_computation | async-start | bytes 1310720 | tf_op jit(solution)/shard_map/all_to_all | solution.py:29
  19.1 0.0 copy-done.6
  19.1 0.1 power_select_fusion
  19.2 0.1 and_select_fusion
  19.3 2.0 %fusion.56 = (bf16[640,144]{0,1:T(8,128)(2,1)S(1)}, f32[640,144]{0,1:T(8,128)S(1)}) fusion(f32[512]{0:T(512)S(1)} %integer_pow.44, f32[144]{0:T(256)S(1)} %get-tuple-element.21, s32[144]{0:T(256)S(1)} %iota_add_fusion.2, f32[144]{0:T(256)S(1)} %get-tuple-element.20, f32[640]{0:T(1024)S(1)} %get-tuple-element.23, s32[640]{0:T(1024)S(1)} %iota_add_fusion, ...), kind=kOutput, calls=%fused_computation.79 | convolution fusion | flops 569133056 | bytes 564416 | tf_op jit(solution)/shard_map/ab,cb->ac/dot_general | solution.py:362
  21.4 0.0 copy-start.5
  21.4 0.2 copy.18.refs_4_.refs_5_
  21.6 0.2 copy.16
  21.8 0.2 copy-done.5
  22.0 0.1 and_select_fusion.1
  22.1 0.1 power_select_fusion.1
  22.2 1.0 fusion.55
  23.2 0.1 copy.17.refs_2_.refs_3_
  23.3 0.1 copy.14
  23.5 0.1 subtract_convert_fusion.refs_5_.refs_6_
  23.5 15.2 %all-to-all-done.refs_1_ = f32[16,80,128]{2,1,0:T(8,128)S(1)} async-done(((f32[16,80,128]{2,1,0:T(8,128)}), f32[16,80,128]{2,1,0:T(8,128)S(1)}, u32[]{:S(2)}, u32[]{:S(2)}) %all-to-all-start) | async-done | bytes 655392 | tf_op jit(solution)/shard_map/all_to_all | solution.py:29
  38.8 12.9 %sweep_first.1 = (f32[32,16,128]{2,1,0:T(8,128)S(1)}, f32[2,112,144]{2,1,0:T(8,128)}, f32[2,400,640]{2,1,0:T(8,128)}) custom-call(s32[1]{0:T(128)} %bitcast.refs_0_, f32[16,80,128]{2,1,0:T(8,128)S(1)} %all-to-all-done.refs_1_, bf16[112,400]{1,0:T(8,128)(2,1)S(1)} %copy.17.refs_2_.refs_3_, bf16[112,400]{1,0:T(8,128)(2,1)S(1)} %subtract_convert_fusion.1.refs_3_.refs_4_, ...), custom_call_target="tpu_custom_call" | custom-call | tf_op jit(solution)/shard_map/sweep_first/pallas_call | solution.py:269
  51.7 22.5 %all_to_all.35 = f32[32,16,128]{2,1,0:T(8,128)S(1)} all-to-all(f32[32,16,128]{2,1,0:T(8,128)S(1)} %get-tuple-element.10), channel_id=1, replica_groups=mesh['mem_0'=4,'mem_1'=8,'lat_0'=2,'lat_1'=2,'lon'=4] {'mem_0','mem_1'}, dimensions={0} | all-to-all | bytes 524288 | tf_op jit(solution)/shard_map/all_to_all | solution.py:368
  74.3 13.4 %all_to_all.36.refs_2_ = f32[16,16,128]{2,1,0:T(8,128)S(1)} all-to-all(f32[16,16,128]{2,1,0:T(8,128)S(1)} %broadcast_in_dim.15), channel_id=1, replica_groups=mesh['mem_0'=4,'mem_1'=8,'lat_0'=2,'lat_1'=2,'lon'=4] {'lat_0','lat_1','..., dimensions={0} | all-to-all | bytes 262144 | tf_op jit(solution)/shard_map/all_to_all | solution.py:29
  87.7 0.0 copy-start
  87.7 0.0 copy-start.1
  87.7 12.0 %sweep_second.1 = (f32[32,16,128]{2,1,0:T(8,128)S(1)}, f32[2,112,144]{2,1,0:T(8,128)}, f32[2,400,640]{2,1,0:T(8,128)}, f32[1,128]{1,0:T(1,128)S(1)}, f32[2,16,128]{2,1,0:T(8,128)S(1)}) custom-call(s32[1]{0:T(128)} %bitcast.refs_0_, f32[16,80,128]{2,1,0:T(8,128)S(1)} %all-to-all-done.refs_1_, f32[16,16,128]{2,1,0:T(8,128)S(1)} %all_to_all.36.refs_2_, ...), custom_call_target="tpu_custom_call" | custom-call | tf_op jit(solution)/shard_map/sweep_second/pallas_call | solution.py:269
  99.6 14.5 %all_to_all.37 = f32[32,16,128]{2,1,0:T(8,128)S(1)} all-to-all(f32[32,16,128]{2,1,0:T(8,128)S(1)} %get-tuple-element.12), channel_id=1, replica_groups=mesh['mem_0'=4,'mem_1'=8,'lat_0'=2,'lat_1'=2,'lon'=4] {'mem_0','mem_1'}, dimensions={0} | all-to-all | bytes 524288 | tf_op jit(solution)/shard_map/all_to_all | solution.py:373
  114.2 12.2 %all_to_all.38.ends_ref = f32[16,2,128]{2,1,0:T(2,128)S(1)} all-to-all(f32[16,2,128]{2,1,0:T(2,128)S(1)} %broadcast_in_dim.16), channel_id=1, replica_groups=mesh['mem_0'=4,'mem_1'=8,'lat_0'=2,'lat_1'=2,'lon'=4] {'lat_0','lat_1','..., dimensions={0} | all-to-all | bytes 32768 | tf_op jit(solution)/shard_map/all_to_all | solution.py:29
  126.4 0.0 copy-done
  126.4 0.0 copy-done.1
  126.4 0.0 copy-start.2
  126.4 0.9 copy-done.2
  127.3 1.8 field.1
  129.1 23.2 %all_to_all.39 = f32[32,48,128]{2,1,0:T(8,128)S(1)} all-to-all(f32[32,48,128]{2,1,0:T(8,128)S(1)} %field.1), channel_id=1, replica_groups=mesh['mem_0'=4,'mem_1'=8,'lat_0'=2,'lat_1'=2,'lon'=4] {'mem_0','mem_1'}, dimensions={0} | all-to-all | bytes 1572864 | tf_op jit(solution)/shard_map/all_to_all | solution.py:402
  152.3 0.1 reduce_sum.42
  152.4 0.9 broadcast_in_dim.17
  153.3 8.9 %all-to-all-start.6 = ((f32[32,48,128]{2,1,0:T(8,128)}), f32[32,48,128]{2,1,0:T(8,128)S(1)}, u32[]{:S(2)}, u32[]{:S(2)}) async-start(f32[32,48,128]{2,1,0:T(8,128)} %broadcast_in_dim.17), calls=%async_computation.6 | async-start | bytes 1572864 | tf_op jit(solution)/shard_map/all_to_all | solution.py:29
  162.2 0.1 fusion.51
  162.3 0.1 fusion.52
  162.4 0.1 fusion.31.left_ref
  162.5 0.3 fusion.16.right_ref
  162.8 0.0 copy-start.3
  162.8 1.6 copy-done.3
  164.4 0.0 copy-start.4
  164.4 1.6 copy-done.4
  166.0 2.8 %analysis.1 = f32[2,96,128]{2,1,0:T(8,128)} custom-call(f32[1,128]{1,0:T(1,128)S(1)} %get-tuple-element.11.length_ref, f32[16,2,128]{2,1,0:T(2,128)S(1)} %all_to_all.38.ends_ref, f32[2,400,640]{2,1,0:T(8,128)S(1)} %copy-done.3, f32[2,400,640]{2,1,0:T(8,128)S(1)} %copy-done.4, f32[96,400]{1,0:T(8,128)S(1)} %fusion.31.left_ref, f32[640,128]{1,0:T(8,128)S(1)} %fusion.16.right_ref), custom_call_target="tpu_custom_call" | custom-call | flops 2000000000 | bytes 5000000 | tf_op jit(solution)/shard_map/analysis/pallas_call | solution.py:393
  168.8 13.2 %all-to-all-done.6 = f32[32,48,128]{2,1,0:T(8,128)S(1)} async-done(((f32[32,48,128]{2,1,0:T(8,128)}), f32[32,48,128]{2,1,0:T(8,128)S(1)}, u32[]{:S(2)}, u32[]{:S(2)}) %all-to-all-start.6) | async-done | bytes 786464 | tf_op jit(solution)/shard_map/all_to_all | solution.py:29
  182.0 0.9 copy.23
  (15 shorter events, 0.2 us)
Async XLA Ops:
  7.2 11.9 %copy-start.6 = (f32[512]{0:T(512)S(1)}, f32[512]{0:T(512)}, u32[]{:S(2)}) copy-start(f32[512]{0:T(512)} %param.9) | copy-start | bytes 6148
  8.9 29.9 %all-to-all-start = ((f32[16,80,128]{2,1,0:T(8,128)}), f32[16,80,128]{2,1,0:T(8,128)S(1)}, u32[]{:S(2)}, u32[]{:S(2)}) async-start(f32[16,80,128]{2,1,0:T(8,128)} %broadcast_in_dim.12), calls=%async_computation | async-start | bytes 1310720 | tf_op jit(solution)/shard_map/all_to_all | solution.py:29
  21.4 0.7 copy-start.5
  87.7 38.7 %copy-start = (f32[2,384,512]{2,1,0:T(8,128)S(1)}, f32[2,384,512]{2,1,0:T(8,128)}, u32[]{:S(2)}) copy-start(f32[2,384,512]{2,1,0:T(8,128)} %perturb_ref.3) | copy-start | bytes 4718596
  87.7 38.7 %copy-start.1 = (f32[2,112,144]{2,1,0:T(8,128)S(1)}, f32[2,112,144]{2,1,0:T(8,128)}, u32[]{:S(2)}) copy-start(f32[2,112,144]{2,1,0:T(8,128)} %get-tuple-element.16.c1_far) | copy-start | bytes 387076
  126.4 0.9 copy-start.2
  153.3 28.7 %all-to-all-start.6 = ((f32[32,48,128]{2,1,0:T(8,128)}), f32[32,48,128]{2,1,0:T(8,128)S(1)}, u32[]{:S(2)}, u32[]{:S(2)}) async-start(f32[32,48,128]{2,1,0:T(8,128)} %broadcast_in_dim.17), calls=%async_computation.6 | async-start | bytes 1572864 | tf_op jit(solution)/shard_map/all_to_all | solution.py:29
  162.8 1.6 copy-start.3
  164.4 1.6 copy-start.4

commit v4 on v3

--- a/solution.py
+++ b/solution.py
@@ -12,6 +12,7 @@
 MEM = ("mem_0", "mem_1")
 LAT = ("lat_0", "lat_1")
 TILES = ("lat_0", "lat_1", "lon")
+X, Z = "mem_0", "mem_1"
 
 tiny_floor = 1e-06
 highest = lax.Precision.HIGHEST
@@ -65,7 +66,7 @@
     return jnp.concatenate([read(r) for r in range(count)], axis=1)
 
 
-def picked_kernel(count_ref, perturb_ref, cell_ref, innov_ref, error_ref, out_ref):
+def picked_kernel(count_ref, perturb_ref, cell_ref, innov_ref, error_ref, copies_ref, out_ref, sems):
     members, fine_lat, fine_lon = perturb_ref.shape
     lines = cell_ref.shape[0]
     step = 512
@@ -94,16 +95,24 @@
             for r in range(per_step):
                 at = (3 + k) * lines + start + r
                 out_ref[at : at + 1, :] = found[:, r * LANES : (r + 1) * LANES]
-
-
-def picked(count, perturb, cell, innovation, error):
+    sends = [
+        pltpu.make_async_copy(out_ref, copies_ref.at[n], sems.at[n]) for n in range(copies_ref.shape[0])
+    ]
+    for send in sends:
+        send.start()
+    for send in sends:
+        send.wait()
+
+
+def picked(count, perturb, cell, innovation, error, copies):
     whole = pl.BlockSpec(memory_space=pltpu.VMEM)
-    fields = 3 + perturb.shape[0]
+    message = ((3 + perturb.shape[0]) * cell.shape[0], LANES)
     return pl.pallas_call(
         picked_kernel,
-        out_shape=jax.ShapeDtypeStruct((fields * cell.shape[0], LANES), f32),
+        out_shape=pltpu.HBM((copies, *message), f32),
         in_specs=[pl.BlockSpec(memory_space=pltpu.SMEM)] + [whole] * 4,
-        out_specs=whole,
+        out_specs=pl.BlockSpec(memory_space=pltpu.HBM),
+        scratch_shapes=[pltpu.VMEM(message, f32), pltpu.SemaphoreType.DMA((copies,))],
         compiler_params=pltpu.CompilerParams(vmem_limit_bytes=60 * 1024 * 1024),
         name="picked",
     )(count, perturb, cell, innovation, error)
@@ -137,14 +146,21 @@
     tile_ref, known_ref = refs[:2]
     refs = refs[2:]
     if not first:
-        seen_ref = refs[0]
+        seen_ref, perturb_far = refs[:2]
+        refs = refs[2:]
+    left_ref, left_low_ref, right_ref, right_low_ref, part_ref, total_out_ref = refs[:6]
+    refs = refs[6:]
+    if first:
+        coarse_ref = refs[0]
         refs = refs[1:]
-    left_ref, left_low_ref, right_ref, right_low_ref, part_ref, coarse_ref, total_out_ref = refs[:7]
-    refs = refs[7:]
-    if not first:
+    else:
         length_ref, own_ref = refs[:2]
         refs = refs[2:]
-    hold, total_ref, coarse_own_ref, image_ref, sems = refs
+    hold, total_ref, coarse_own_ref, image_ref, sems = refs[:5]
+    if not first:
+        perturb_ref = refs[5]
+        perturb_copy = pltpu.make_async_copy(perturb_far, perturb_ref, sems.at[1])
+        perturb_copy.start()
     tiles = known_ref.shape[0]
     lines = known_ref.shape[1] // (3 + members)
     width = total_ref.shape[2]
@@ -225,8 +241,9 @@
     coarse = coarse[:count] + (coarse[count:] + dot(high, right_low_ref[...]))
     for k in range(members):
         coarse_own_ref[k] = coarse[k * ROWS : (k + 1) * ROWS]
-    coarse_copy = pltpu.make_async_copy(coarse_own_ref, coarse_ref, sems.at[1])
-    coarse_copy.start()
+    if first:
+        coarse_copy = pltpu.make_async_copy(coarse_own_ref, coarse_ref, sems.at[1])
+        coarse_copy.start()
     made = dot(jnp.concatenate(split_two(coarse), axis=0), cols)
     for k in range(members):
         mine = made[k * ROWS : (k + 1) * ROWS] + made[count + k * ROWS : count + (k + 1) * ROWS]
@@ -241,88 +258,123 @@
         own_ref[0] = known_ref[own, 2 * lines : 3 * lines, :]
         own_ref[1] = hold[6, own]
     for n in range(part_ref.shape[0]):
-        part_ref[n] = image
-    coarse_copy.wait()
+        part_ref[n, :lines, :] = image
+    if not first:
+        perturb_copy.wait()
+        put_field(perturb_ref, coarse_own_ref, scale, part_ref, lines)
+    else:
+        coarse_copy.wait()
     total_copy.wait()
 
 
-def sweep(tile, known, seen, kernels, scale, lon_tiles, members, groups):
+def sweep(tile, known, seen, perturb, kernels, scale, lon_tiles, part):
+    members, fine_lat, fine_lon = perturb.shape
     tiles = known.shape[0]
     lines = known.shape[1] // (3 + members)
     first = seen is None
     left, _, right, _ = kernels
     total = (members, left.shape[1], right.shape[0])
     whole = pl.BlockSpec(memory_space=pltpu.VMEM)
-    out_shape = [
-        jax.ShapeDtypeStruct((groups, lines, LANES), f32),
-        pltpu.HBM((members, ROWS, COLS), f32),
-        pltpu.HBM(total, f32),
-    ]
     far = pl.BlockSpec(memory_space=pltpu.HBM)
-    out_specs = [whole, far, far]
-    if not first:
+    out_shape = [jax.ShapeDtypeStruct(part, f32), pltpu.HBM(total, f32)]
+    out_specs = [whole, far]
+    if first:
+        out_shape.append(pltpu.HBM((members, ROWS, COLS), f32))
+        out_specs.append(far)
+    else:
         out_shape.append(jax.ShapeDtypeStruct((1, LANES), f32))
         out_shape.append(jax.ShapeDtypeStruct((2, lines, LANES), f32))
         out_specs += [whole, whole]
-    arrays = [known] if first else [known, seen]
+    arrays = [known] if first else [known, seen, perturb]
+    in_specs = [whole] if first else [whole, whole, far]
     arrays += kernels
+    in_specs += [whole] * len(kernels)
+    scratch = [
+        pltpu.VMEM((7 + 4 * members, tiles, lines, LANES), f32),
+        pltpu.VMEM(total, f32),
+        pltpu.VMEM((members, ROWS, COLS), f32),
+        pltpu.VMEM((members, lines, LANES), f32),
+        pltpu.SemaphoreType.DMA((2,)),
+    ]
+    if not first:
+        scratch.append(pltpu.VMEM(perturb.shape, f32))
     return pl.pallas_call(
         functools.partial(sweep_kernel, first, scale, lon_tiles, members),
         out_shape=out_shape,
-        in_specs=[pl.BlockSpec(memory_space=pltpu.SMEM)] + [whole] * len(arrays),
+        in_specs=[pl.BlockSpec(memory_space=pltpu.SMEM)] + in_specs,
         out_specs=out_specs,
-        scratch_shapes=[
-            pltpu.VMEM((7 + 4 * members, tiles, lines, LANES), f32),
-            pltpu.VMEM(total, f32),
-            pltpu.VMEM((members, ROWS, COLS), f32),
-            pltpu.VMEM((members, lines, LANES), f32),
-            pltpu.SemaphoreType.DMA((2,)),
-        ],
-        compiler_params=pltpu.CompilerParams(vmem_limit_bytes=24 * 1024 * 1024),
+        scratch_shapes=scratch,
+        compiler_params=pltpu.CompilerParams(vmem_limit_bytes=60 * 1024 * 1024),
+        cost_estimate=pl.CostEstimate(flops=8 * 10**9, bytes_accessed=10**7, transcendentals=0),
         name="sweep_first" if first else "sweep_second",
     )(tile, *arrays)
 
 
-def ends_length(ends_ref):
-    return length_of(jnp.sum(ends_ref[:, 1, :]), jnp.sum(ends_ref[:, 0, :]))
-
-
-def field_kernel(scale, perturb_ref, length_ref, ends_ref, c1_far, c2_far, out_ref, c1_ref, c2_ref, sems):
-    copies = [
-        pltpu.make_async_copy(c1_far, c1_ref, sems.at[0]),
-        pltpu.make_async_copy(c2_far, c2_ref, sems.at[1]),
-    ]
-    for copy in copies:
-        copy.start()
+def refined(count, cells, axis):
+    shape = (count, cells) if axis == 0 else (cells, count)
+    fine = lax.broadcasted_iota(jnp.int32, shape, axis).astype(f32)
+    cell = lax.broadcasted_iota(jnp.int32, shape, 1 - axis).astype(f32)
+    return jnp.maximum(1.0 - jnp.abs((fine + 2.5) * 0.25 - cell), 0.0).astype(bf16)
+
+
+def put_field(perturb_ref, coarse, scale, out_ref, skip):
     members, fine_lat, fine_lon = perturb_ref.shape
-    pieces, piece_rows, piece_cols = out_ref.shape
-    across = fine_lon // piece_cols
-    one = length_ref[0, 0]
-    two = ends_length(ends_ref)
-
-    def refined(count, cells, axis):
-        shape = (count, cells) if axis == 0 else (cells, count)
-        fine = lax.broadcasted_iota(jnp.int32, shape, axis).astype(f32)
-        cell = lax.broadcasted_iota(jnp.int32, shape, 1 - axis).astype(f32)
-        return jnp.maximum(1.0 - jnp.abs((fine + 2.5) * 0.25 - cell), 0.0).astype(bf16)
-
     to_rows = refined(fine_lat, ROWS, 0)
     to_cols = refined(fine_lon, COLS, 1)
     field = jnp.zeros((fine_lat, fine_lon), f32)
-    for copy in copies:
-        copy.wait()
     for k in range(members):
-        coarse = one * c1_ref[k] + two * c2_ref[k]
-        high, low = split_two(coarse)
+        high, low = split_two(coarse[k])
         tall = dot(to_rows, high) + dot(to_rows, low)
         high, low = split_two(tall)
         field = field + (dot(high, to_cols) + dot(low, to_cols)) * perturb_ref[k]
-    field = -scale * field
-    for n in range(pieces * piece_rows // 8):
+    field = scale * field
+    across = fine_lon // LANES
+    per_part = fine_lat // 8 * across // out_ref.shape[0]
+    for n in range(per_part * out_ref.shape[0]):
         i = n // across * 8
-        j = n % across * piece_cols
-        at = n * 8 % piece_rows
-        out_ref[n * 8 // piece_rows, at : at + 8, :] = field[i : i + 8, j : j + piece_cols]
+        j = n % across * LANES
+        at = skip + n % per_part * 8
+        out_ref[n // per_part, at : at + 8, :] = field[i : i + 8, j : j + LANES]
+
+
+def field_kernel(scale, perturb_ref, coarse_ref, out_ref):
+    put_field(perturb_ref, coarse_ref, scale, out_ref, 0)
+
+
+def gather_x_kernel(image_and_second_ref, first_ref, out_ref):
+    parts = out_ref.shape[0]
+    lines = image_and_second_ref.shape[1] - first_ref.shape[1]
+    rows = first_ref.shape[1] // parts
+    image = jnp.sum(image_and_second_ref[:, :lines, :], axis=0)
+    for n in range(parts):
+        out_ref[n, :lines, :] = image
+        out_ref[n, lines : lines + rows, :] = jnp.sum(first_ref[:, n * rows : (n + 1) * rows, :], axis=0)
+        at = lines + n * rows
+        out_ref[n, lines + rows :, :] = jnp.sum(image_and_second_ref[:, at : at + rows, :], axis=0)
+
+
+def gather_z_kernel(arrived_ref, own_ref, bent_ref, fields_ref):
+    lines = own_ref.shape[1]
+    image = jnp.sum(arrived_ref[:, :lines, :], axis=0)
+    fields_ref[...] = jnp.sum(arrived_ref[:, lines:, :], axis=0)
+    bent = jnp.sum((image * own_ref[0]) ** 2, axis=0, keepdims=True)
+    gain = jnp.sum(image * own_ref[1], axis=0, keepdims=True)
+    both = jnp.concatenate([bent, gain], axis=0)
+    for n in range(bent_ref.shape[0]):
+        bent_ref[n] = both
+
+
+def ends_length(ends_ref):
+    return length_of(jnp.sum(ends_ref[:, 1, :]), jnp.sum(ends_ref[:, 0, :]))
+
+
+def finish_kernel(length_ref, ends_ref, fields_ref, out_ref):
+    rows = fields_ref.shape[0] // 2
+    one = length_ref[0, 0]
+    two = ends_length(ends_ref)
+    done = -(one * fields_ref[:rows] + two * fields_ref[rows:])
+    for n in range(out_ref.shape[0]):
+        out_ref[n] = done
 
 
 def analysis_kernel(length_ref, ends_ref, total_1_ref, total_2_ref, left_ref, right_ref, out_ref):
@@ -332,6 +384,20 @@
         total = one * total_1_ref[k] + two * total_2_ref[k]
         half = jnp.dot(left_ref[...], total, precision=highest, preferred_element_type=f32)
         out_ref[k] = -jnp.dot(half, right_ref[...], precision=highest, preferred_element_type=f32)
+
+
+def small_call(kernel, shapes, flops, name, *arrays):
+    whole = pl.BlockSpec(memory_space=pltpu.VMEM)
+    made = pl.pallas_call(
+        kernel,
+        out_shape=[jax.ShapeDtypeStruct(shape, f32) for shape in shapes],
+        in_specs=[whole] * len(arrays),
+        out_specs=[whole] * len(shapes),
+        compiler_params=pltpu.CompilerParams(vmem_limit_bytes=60 * 1024 * 1024),
+        cost_estimate=pl.CostEstimate(flops=flops, bytes_accessed=2 * 10**6, transcendentals=0),
+        name=name,
+    )(*arrays)
+    return made if len(shapes) > 1 else made[0]
 
 
 def per_device(perturb, loc_lat, loc_lon, obs_cell, obs_count, obs_innov, obs_error):
@@ -350,8 +416,8 @@
     cell = obs_cell.reshape(lines, LANES)
     innovation = obs_innov.reshape(lines, LANES)
     error = obs_error.reshape(lines, LANES)
-    message = picked(obs_count.reshape(1), perturb, cell, innovation, error)
-    known = sent_to_all(message, TILES)
+    message = picked(obs_count.reshape(1), perturb, cell, innovation, error, lat_tiles * lon_tiles)
+    known = lax.all_to_all(message, TILES, 0, 0, tiled=True)
 
     first_lat, first_lon = lat * coarse_lat, lon * coarse_lon
     lat_all = kernel_block(loc_lat, -1, padded_lat, 0, total_lat)
@@ -364,46 +430,52 @@
     right_own = kernel_block(loc_lon, -1, padded_lon, first_lon, coarse_lon)
     kernels = [*split_two(left), *split_two(right)]
 
-    part, coarse_1, total_1 = sweep(tile, known, None, kernels, scale, lon_tiles, members, groups)
+    field_rows = fine_lat * fine_lon // LANES
+    along_x, along_z = lax.axis_size(X), lax.axis_size(Z)
+    part_rows, piece_rows = field_rows // along_x, field_rows // groups
+    part, total_1, coarse_1 = sweep(
+        tile, known, None, perturb, kernels, scale, lon_tiles, (groups, lines, LANES)
+    )
+    first_field = small_call(
+        functools.partial(field_kernel, scale), ((along_x, part_rows, LANES),), 3 * 10**8, "field", perturb, coarse_1
+    )
     mine = jnp.sum(lax.all_to_all(part, MEM, 0, 0, tiled=True), axis=0)
     seen = sent_to_all(mine, TILES)
-    part, coarse_2, total_2, length_1, own = sweep(
-        tile, known, seen, kernels, scale, lon_tiles, members, groups
-    )
-    mine = jnp.sum(lax.all_to_all(part, MEM, 0, 0, tiled=True), axis=0)
-    bent = jnp.sum(jnp.stack([(mine * own[0]) ** 2, mine * own[1]]), axis=1)
-    ends = sent_to_all(bent, TILES)
-
+    first_field, seen = lax.optimization_barrier((first_field, seen))
+    first_field = lax.all_to_all(first_field, X, 0, 0, tiled=True)
+    part, total_2, length_1, own = sweep(
+        tile, known, seen, perturb, kernels, scale, lon_tiles, (along_x, lines + part_rows, LANES)
+    )
+    part = lax.all_to_all(part, X, 0, 0, tiled=True)
+    part = small_call(
+        gather_x_kernel, ((along_z, lines + 2 * piece_rows, LANES),), 10**6, "gather_x", part, first_field
+    )
+    part = lax.all_to_all(part, Z, 0, 0, tiled=True)
+    bent, fields = small_call(
+        gather_z_kernel,
+        ((lat_tiles * lon_tiles, 2, LANES), (2 * piece_rows, LANES)),
+        10**6,
+        "gather_z",
+        part,
+        own,
+    )
+    ends = lax.all_to_all(bent, TILES, 0, 0, tiled=True)
+    done = small_call(finish_kernel, ((along_z, piece_rows, LANES),), 10**6, "finish", length_1, ends, fields)
+    done = lax.all_to_all(done, Z, 0, 0, tiled=True).reshape(part_rows, LANES)
+    everything = sent_to_all(done, X)
     whole = pl.BlockSpec(memory_space=pltpu.VMEM)
-    piece_cols = 128
-    piece_rows = fine_lat * fine_lon // groups // piece_cols
-    pieces = pl.pallas_call(
-        functools.partial(field_kernel, scale),
-        out_shape=jax.ShapeDtypeStruct((groups, piece_rows, piece_cols), f32),
-        in_specs=[whole] * 3 + [pl.BlockSpec(memory_space=pltpu.HBM)] * 2,
-        out_specs=whole,
-        scratch_shapes=[
-            pltpu.VMEM((members, ROWS, COLS), f32),
-            pltpu.VMEM((members, ROWS, COLS), f32),
-            pltpu.SemaphoreType.DMA((2,)),
-        ],
-        compiler_params=pltpu.CompilerParams(vmem_limit_bytes=24 * 1024 * 1024),
-        name="field",
-    )(perturb, length_1, ends, coarse_1, coarse_2)
     analysis = pl.pallas_call(
         analysis_kernel,
         out_shape=jax.ShapeDtypeStruct((members, coarse_lat, coarse_lon), f32),
         in_specs=[whole] * 6,
         out_specs=whole,
-        compiler_params=pltpu.CompilerParams(vmem_limit_bytes=24 * 1024 * 1024),
+        compiler_params=pltpu.CompilerParams(vmem_limit_bytes=60 * 1024 * 1024),
         cost_estimate=pl.CostEstimate(flops=2 * 10**9, bytes_accessed=5 * 10**6, transcendentals=0),
         name="analysis",
     )(length_1, ends, total_1, total_2, left_own, right_own)
-    summed = jnp.sum(lax.all_to_all(pieces, MEM, 0, 0, tiled=True), axis=0)
-    everything = sent_to_all(summed, MEM)
-    across = fine_lon // piece_cols
+    across = fine_lon // LANES
     increment = jnp.transpose(
-        everything.reshape(fine_lat // 8, across, 8, piece_cols), (0, 2, 1, 3)
+        everything.reshape(fine_lat // 8, across, 8, LANES), (0, 2, 1, 3)
     ).reshape(fine_lat, fine_lon)
     return analysis, increment
 

time: 186 us -> 193 us (1.038); the launches traced: 183 us -> 192 us
  Pallas kernels: 35.4 us -> 49.4 us
  blocking collectives: 85.7 us -> 71.7 us
  starting transfers between devices: 19.1 us -> 25.5 us
  waiting for transfers between devices: 28.4 us -> 33.1 us
  local copies, waits for them, and re-layouts: 8.48 us -> 4.25 us
  other arithmetic: 1.24 us -> 3.93 us
    all_to_all x0 -> x3, waiting for transfers between devices: none -> 22.8 us  [the longest x1 13.9 us: per_device(): known = lax.all_to_all(message, TILES, 0, 0, tiled=True)]
    all_to_all x2, waiting for transfers between devices: 28.4 us -> 10.3 us  [sent_to_all(): return lax.all_to_all(copies, axis, split_axis=0, concat_axis=0, tiled=True)]
    all_to_all x0 -> x3, starting transfers between devices: none -> 17.3 us  [the longest x1 10.3 us: per_device(): known = lax.all_to_all(message, TILES, 0, 0, tiled=True)]
    all_to_all x2 -> x1, blocking collectives: 37 us -> 22.7 us  [per_device(): mine = jnp.sum(lax.all_to_all(part, MEM, 0, 0, tiled=True), axis=0)]
    all_to_all x2, starting transfers between devices: 19.1 us -> 8.22 us  [sent_to_all(): return lax.all_to_all(copies, axis, split_axis=0, concat_axis=0, tiled=True)]
    pallas_call x2 -> x5, Pallas kernels: 7.73 us -> 15.2 us  [the longest x4 8.86 us: small_call(): pl.pallas_call(kernel, out_shape=[jax.ShapeDtypeStruct(shape, f32) for sh...]
    pallas_call x2, Pallas kernels: 24.9 us -> 29.2 us  [sweep(): pl.pallas_call(functools.partial(sweep_kernel, first, scale, lon_tiles, m...]
    unnamed x15, local copies, waits for them, and re-layouts: 5.21 us -> 2.01 us
  transfers between devices with their start and end apart: 2 -> 5, of which waited for: 2 -> 4; matrix products, arithmetic and copies ran while one was open for 3% -> 4% of each run, Pallas kernels for 2% -> 12%
where the time goes in v4:
time: 193 us; the launch traced here: 192 us
  blocking collectives  71.7 us (37%)
  Pallas kernels  49.4 us (26%)
  waiting for transfers between devices  33.1 us (17%)
  starting transfers between devices  25.5 us (13%)
  local copies, waits for them, and re-layouts  4.25 us (2%)
  other arithmetic  3.93 us (2%)
  matrix products  2.97 us (2%)
    pallas_call x2, Pallas kernels, sweep(): pl.pallas_call(functools.partial(sweep_kernel, first, scale, lon_tiles, m...  29.2 us
    all_to_all x1, blocking collectives, per_device(): mine = jnp.sum(lax.all_to_all(part, MEM, 0, 0, tiled=True), axis=0)  22.7 us
    all_to_all x1, blocking collectives, per_device(): part = lax.all_to_all(part, Z, 0, 0, tiled=True)  18.4 us
    all_to_all x1, blocking collectives, per_device(): part = lax.all_to_all(part, X, 0, 0, tiled=True)  16.6 us
    all_to_all x1, blocking collectives, per_device(): ends = lax.all_to_all(bent, TILES, 0, 0, tiled=True)  13.9 us
    all_to_all x1, waiting for transfers between devices, per_device(): known = lax.all_to_all(message, TILES, 0, 0, tiled=True)  13.9 us
    all_to_all x2, waiting for transfers between devices, sent_to_all(): return lax.all_to_all(copies, axis, split_axis=0, concat_axis=0, tiled=True)  10.3 us
    all_to_all x1, starting transfers between devices, per_device(): known = lax.all_to_all(message, TILES, 0, 0, tiled=True)  10.3 us
  transfers between devices with their start and end apart: 5, of which 4 were waited for; matrix products, arithmetic and copies ran while one was open for 4% of the time, Pallas kernels for 12%

profile of v4, /device:TPU:1, one launch (start us, length us, event | category | flops | bytes accessed | tf_op | source)
XLA Modules:
  0.0 192.3 jit_solution(7849919747649658399)
XLA Ops:
  1.3 0.0 copy-start.6
  1.3 6.3 %picked.1 = f32[16,80,128]{2,1,0:T(8,128)} custom-call(s32[1]{0:T(128)} %bitcast.11.count_ref, f32[2,384,512]{2,1,0:T(8,128)} %refs_3_.1, s32[16,128]{1,0:T(8,128)} %bitcast.14, f32[16,128]{1,0:T(8,128)} %bitcast.15, f32[16,128]{1,0:T(8,128)} %bitcast.16), custom_call_target="tpu_custom_call" | custom-call | tf_op jit(solution)/shard_map/picked/pallas_call | solution.py:110
  7.6 10.3 %all-to-all-start = ((f32[16,80,128]{2,1,0:T(8,128)}), f32[16,80,128]{2,1,0:T(8,128)S(1)}, u32[]{:S(2)}, u32[]{:S(2)}) async-start(f32[16,80,128]{2,1,0:T(8,128)} %picked.1), calls=%async_computation | async-start | bytes 1310720 | tf_op jit(solution)/shard_map/all_to_all | solution.py:420
  17.8 0.0 copy-done.6
  17.9 0.1 power_select_fusion
  18.0 0.1 and_select_fusion
  18.0 2.0 %fusion.55 = (bf16[640,144]{0,1:T(8,128)(2,1)S(1)}, f32[640,144]{0,1:T(8,128)S(1)}) fusion(f32[512]{0:T(512)S(1)} %integer_pow.40, f32[144]{0:T(256)S(1)} %get-tuple-element.25, s32[144]{0:T(256)S(1)} %iota_add_fusion.2, f32[144]{0:T(256)S(1)} %get-tuple-element.24, f32[640]{0:T(1024)S(1)} %get-tuple-element.27, s32[640]{0:T(1024)S(1)} %iota_add_fusion, ...), kind=kOutput, calls=%fused_computation.75 | convolution fusion | flops 569133056 | bytes 564416 | tf_op jit(solution)/shard_map/ab,cb->ac/dot_general | solution.py:428
  20.1 0.0 copy-start.5
  20.1 0.2 copy.18.refs_4_.refs_6_
  20.3 0.2 copy.16
  20.5 0.2 copy-done.5
  20.8 0.1 and_select_fusion.1
  20.8 0.1 power_select_fusion.1
  20.9 1.0 fusion.54
  21.9 0.1 copy.17.refs_2_.refs_4_
  22.0 0.0 copy-start.3
  22.0 0.1 copy.14
  22.2 0.7 subtract_convert_fusion.1.refs_3_.refs_5_
  22.8 0.8 subtract_convert_fusion.refs_5_.refs_7_
  23.6 13.9 %all-to-all-done.refs_1_ = f32[16,80,128]{2,1,0:T(8,128)S(1)} async-done(((f32[16,80,128]{2,1,0:T(8,128)}), f32[16,80,128]{2,1,0:T(8,128)S(1)}, u32[]{:S(2)}, u32[]{:S(2)}) %all-to-all-start) | async-done | bytes 655392 | tf_op jit(solution)/shard_map/all_to_all | solution.py:420
  37.5 0.9 copy-done.2
  38.4 13.7 %sweep_first.1 = (f32[32,16,128]{2,1,0:T(8,128)}, f32[2,400,640]{2,1,0:T(8,128)}, f32[2,112,144]{2,1,0:T(8,128)}) custom-call(s32[1]{0:T(128)} %bitcast.refs_0_, f32[16,80,128]{2,1,0:T(8,128)} %copy-done.2, bf16[112,400]{1,0:T(8,128)(2,1)} %copy-done.3, bf16[112,400]{1,0:T(8,128)(2,1)} %subtract_convert_fusion.1.refs_3_.refs_5_, bf16[640,144]{1,0:T(8,128)(2,1)} %copy-done.1, ...), custom_call_target="tpu_custom_call" | custom-call | flops 8000000000 | bytes 10000000 | tf_op jit(solution)/shard_map/sweep_first/pallas_call | solution.py:301
  52.1 22.7 %all_to_all.45 = f32[32,16,128]{2,1,0:T(8,128)S(1)} all-to-all(f32[32,16,128]{2,1,0:T(8,128)} %get-tuple-element.14), channel_id=1, replica_groups=mesh['mem_0'=4,'mem_1'=8,'lat_0'=2,'lat_1'=2,'lon'=4] {'mem_0','mem_1'}, dimensions={0} | all-to-all | bytes 524288 | tf_op jit(solution)/shard_map/all_to_all | solution.py:442
  74.8 0.7 broadcast_in_dim.10
  75.5 4.7 %all-to-all-start.2 = ((f32[16,16,128]{2,1,0:T(8,128)}), f32[16,16,128]{2,1,0:T(8,128)S(1)}, u32[]{:S(2)}, u32[]{:S(2)}) async-start(f32[16,16,128]{2,1,0:T(8,128)} %broadcast_in_dim.10), calls=%async_computation.2 | async-start | bytes 262144 | tf_op jit(solution)/shard_map/all_to_all | solution.py:30
  80.2 3.3 %field.1 = f32[4,384,128]{2,1,0:T(8,128)} custom-call(f32[2,384,512]{2,1,0:T(8,128)} %refs_3_.1, f32[2,112,144]{2,1,0:T(8,128)} %get-tuple-element.13.coarse_ref), custom_call_target="tpu_custom_call" | custom-call | flops 300000000 | bytes 2000000 | tf_op jit(solution)/shard_map/field/pallas_call | solution.py:391
  83.5 5.6 %all-to-all-done.2.refs_2_ = f32[16,16,128]{2,1,0:T(8,128)S(1)} async-done(((f32[16,16,128]{2,1,0:T(8,128)}), f32[16,16,128]{2,1,0:T(8,128)S(1)}, u32[]{:S(2)}, u32[]{:S(2)}) %all-to-all-start.2) | async-done | bytes 131104 | tf_op jit(solution)/shard_map/all_to_all | solution.py:30
  89.1 3.7 %all-to-all-start.4 = ((f32[4,384,128]{2,1,0:T(8,128)}), f32[4,384,128]{2,1,0:T(8,128)S(1)}, u32[]{:S(2)}, u32[]{:S(2)}) async-start(f32[4,384,128]{2,1,0:T(8,128)} %field.1), calls=%async_computation.4 | async-start | bytes 1572864 | tf_op jit(solution)/shard_map/all_to_all | solution.py:445
  92.8 15.5 %sweep_second.1 = (f32[4,400,128]{2,1,0:T(8,128)}, f32[2,400,640]{2,1,0:T(8,128)}, f32[1,128]{1,0:T(1,128)}, f32[2,16,128]{2,1,0:T(8,128)}) custom-call(s32[1]{0:T(128)} %bitcast.refs_0_, f32[16,80,128]{2,1,0:T(8,128)} %copy-done.2, f32[16,16,128]{2,1,0:T(8,128)} %copy-done.4, f32[2,384,512]{2,1,0:T(8,128)} %refs_3_.1, bf16[112,400]{1,0:T(8,128)(2,1)} %copy-done.3, ...), custom_call_target="tpu_custom_call" | custom-call | flops 8000000000 | bytes 10000000 | tf_op jit(solution)/shard_map/sweep_second/pallas_call | solution.py:301
  108.4 0.0 all-to-all-done.4.first_ref
  108.4 0.0 copy-start
  108.4 16.6 %all_to_all.46.image_and_second_ref = f32[4,400,128]{2,1,0:T(8,128)} all-to-all(f32[4,400,128]{2,1,0:T(8,128)} %get-tuple-element.17), channel_id=1, replica_groups=mesh['mem_0'=4,'mem_1'=8,'lat_0'=2,'lat_1'=2,'lon'=4] {'mem_0'}, dimensions={0} | all-to-all | bytes 1638400 | tf_op jit(solution)/shard_map/all_to_all | solution.py:449
  125.0 2.2 %gather_x.1 = f32[8,112,128]{2,1,0:T(8,128)} custom-call(f32[4,400,128]{2,1,0:T(8,128)} %all_to_all.46.image_and_second_ref, f32[4,384,128]{2,1,0:T(8,128)} %copy-done), custom_call_target="tpu_custom_call" | custom-call | flops 1000000 | bytes 2000000 | tf_op jit(solution)/shard_map/gather_x/pallas_call | solution.py:391
  127.2 18.4 %all_to_all.47.arrived_ref = f32[8,112,128]{2,1,0:T(8,128)} all-to-all(f32[8,112,128]{2,1,0:T(8,128)} %gather_x.1), channel_id=1, replica_groups=mesh['mem_0'=4,'mem_1'=8,'lat_0'=2,'lat_1'=2,'lon'=4] {'mem_1'}, dimensions={0} | all-to-all | bytes 917504 | tf_op jit(solution)/shard_map/all_to_all | solution.py:453
  145.6 1.7 gather_z.1
  147.3 13.9 %all_to_all.48.ends_ref = f32[16,2,128]{2,1,0:T(2,128)} all-to-all(f32[16,2,128]{2,1,0:T(2,128)} %get-tuple-element.20), channel_id=1, replica_groups=mesh['mem_0'=4,'mem_1'=8,'lat_0'=2,'lat_1'=2,'lon'=4] {'lat_0','lat_1','..., dimensions={0} | all-to-all | bytes 32768 | tf_op jit(solution)/shard_map/all_to_all | solution.py:462
  161.2 1.7 finish.1
  162.9 3.4 %all-to-all-start.7 = ((f32[8,48,128]{2,1,0:T(8,128)}), f32[8,48,128]{2,1,0:T(8,128)S(1)}, u32[]{:S(2)}, u32[]{:S(2)}) async-start(f32[8,48,128]{2,1,0:T(8,128)} %finish.1), calls=%async_computation.7 | async-start | bytes 393216 | tf_op jit(solution)/shard_map/all_to_all | solution.py:464
  166.3 0.1 fusion.50
  166.4 0.8 fusion.31.left_ref
  167.2 8.9 %all-to-all-done.7 = f32[8,48,128]{2,1,0:T(8,128)S(1)} async-done(((f32[8,48,128]{2,1,0:T(8,128)}), f32[8,48,128]{2,1,0:T(8,128)S(1)}, u32[]{:S(2)}, u32[]{:S(2)}) %all-to-all-start.7) | async-done | bytes 196640 | tf_op jit(solution)/shard_map/all_to_all | solution.py:464
  176.2 0.9 broadcast_in_dim.11
  177.1 3.5 %all-to-all-start.8 = ((f32[4,384,128]{2,1,0:T(8,128)}), f32[4,384,128]{2,1,0:T(8,128)S(1)}, u32[]{:S(2)}, u32[]{:S(2)}) async-start(f32[4,384,128]{2,1,0:T(8,128)} %broadcast_in_dim.11), calls=%async_computation.8 | async-start | bytes 1572864 | tf_op jit(solution)/shard_map/all_to_all | solution.py:30
  180.6 0.1 fusion.51
  180.7 1.1 fusion.16.right_ref
  181.7 5.0 %analysis.1 = f32[2,96,128]{2,1,0:T(8,128)} custom-call(f32[1,128]{1,0:T(1,128)} %get-tuple-element.16.length_ref, f32[16,2,128]{2,1,0:T(2,128)} %all_to_all.48.ends_ref, f32[2,400,640]{2,1,0:T(8,128)} %get-tuple-element.21.total_1_ref, f32[2,400,640]{2,1,0:T(8,128)} %get-tuple-element.22.total_2_ref, f32[96,400]{1,0:T(8,128)} %fusion.31.left_ref, ...), custom_call_target="tpu_custom_call" | custom-call | flops 2000000000 | bytes 5000000 | tf_op jit(solution)/shard_map/analysis/pallas_call | solution.py:467
  186.8 4.7 %all-to-all-done.8 = f32[4,384,128]{2,1,0:T(8,128)S(1)} async-done(((f32[4,384,128]{2,1,0:T(8,128)}), f32[4,384,128]{2,1,0:T(8,128)S(1)}, u32[]{:S(2)}, u32[]{:S(2)}) %all-to-all-start.8) | async-done | bytes 786464 | tf_op jit(solution)/shard_map/all_to_all | solution.py:30
  191.4 0.9 copy.23
  (16 shorter events, 0.1 us)
Async XLA Ops:
  1.3 16.6 %copy-start.6 = (f32[512]{0:T(512)S(1)}, f32[512]{0:T(512)}, u32[]{:S(2)}) copy-start(f32[512]{0:T(512)} %param.9) | copy-start | bytes 6148
  7.6 29.9 %all-to-all-start = ((f32[16,80,128]{2,1,0:T(8,128)}), f32[16,80,128]{2,1,0:T(8,128)S(1)}, u32[]{:S(2)}, u32[]{:S(2)}) async-start(f32[16,80,128]{2,1,0:T(8,128)} %picked.1), calls=%async_computation | async-start | bytes 1310720 | tf_op jit(solution)/shard_map/all_to_all | solution.py:420
  20.1 0.7 copy-start.5
  20.3 2.6 %copy-start.1 = (bf16[640,144]{1,0:T(8,128)(2,1)}, bf16[640,144]{1,0:T(8,128)(2,1)S(1)}, u32[]{:S(2)}) copy-start(bf16[640,144]{1,0:T(8,128)(2,1)S(1)} %copy.18.refs_4_.refs_6_) | copy-start | bytes 552964
  22.0 15.5 %copy-start.3 = (bf16[112,400]{1,0:T(8,128)(2,1)}, bf16[112,400]{1,0:T(8,128)(2,1)S(1)}, u32[]{:S(2)}) copy-start(bf16[112,400]{1,0:T(8,128)(2,1)S(1)} %copy.17.refs_2_.refs_4_) | copy-start | bytes 268804
  37.5 0.9 copy-start.2
  75.5 13.7 %all-to-all-start.2 = ((f32[16,16,128]{2,1,0:T(8,128)}), f32[16,16,128]{2,1,0:T(8,128)S(1)}, u32[]{:S(2)}, u32[]{:S(2)}) async-start(f32[16,16,128]{2,1,0:T(8,128)} %broadcast_in_dim.10), calls=%async_computation.2 | async-start | bytes 262144 | tf_op jit(solution)/shard_map/all_to_all | solution.py:30
  89.1 3.7 %copy-start.4 = (f32[16,16,128]{2,1,0:T(8,128)}, f32[16,16,128]{2,1,0:T(8,128)S(1)}, u32[]{:S(2)}) copy-start(f32[16,16,128]{2,1,0:T(8,128)S(1)} %all-to-all-done.2.refs_2_) | copy-start | bytes 393220
  89.1 19.2 %all-to-all-start.4 = ((f32[4,384,128]{2,1,0:T(8,128)}), f32[4,384,128]{2,1,0:T(8,128)S(1)}, u32[]{:S(2)}, u32[]{:S(2)}) async-start(f32[4,384,128]{2,1,0:T(8,128)} %field.1), calls=%async_computation.4 | async-start | bytes 1572864 | tf_op jit(solution)/shard_map/all_to_all | solution.py:445
  108.4 16.6 %copy-start = (f32[4,384,128]{2,1,0:T(8,128)}, f32[4,384,128]{2,1,0:T(8,128)S(1)}, u32[]{:S(2)}) copy-start(f32[4,384,128]{2,1,0:T(8,128)S(1)} %all-to-all-done.4.first_ref) | copy-start | bytes 2359300
  162.9 13.3 %all-to-all-start.7 = ((f32[8,48,128]{2,1,0:T(8,128)}), f32[8,48,128]{2,1,0:T(8,128)S(1)}, u32[]{:S(2)}, u32[]{:S(2)}) async-start(f32[8,48,128]{2,1,0:T(8,128)} %finish.1), calls=%async_computation.7 | async-start | bytes 393216 | tf_op jit(solution)/shard_map/all_to_all | solution.py:464
  177.1 14.4 %all-to-all-start.8 = ((f32[4,384,128]{2,1,0:T(8,128)}), f32[4,384,128]{2,1,0:T(8,128)S(1)}, u32[]{:S(2)}, u32[]{:S(2)}) async-start(f32[4,384,128]{2,1,0:T(8,128)} %broadcast_in_dim.11), calls=%async_computation.8 | async-start | bytes 1572864 | tf_op jit(solution)/shard_map/all_to_all | solution.py:30

commit v5 on v3

--- a/solution.py
+++ b/solution.py
@@ -12,6 +12,7 @@
 MEM = ("mem_0", "mem_1")
 LAT = ("lat_0", "lat_1")
 TILES = ("lat_0", "lat_1", "lon")
+X, Z = "mem_0", "mem_1"
 
 tiny_floor = 1e-06
 highest = lax.Precision.HIGHEST
@@ -21,7 +22,6 @@
 ROWS = 112
 COLS = 144
 LANES = 128
-TOGETHER = 2
 
 
 def sent_to_all(x, axis):
@@ -65,7 +65,7 @@
     return jnp.concatenate([read(r) for r in range(count)], axis=1)
 
 
-def picked_kernel(count_ref, perturb_ref, cell_ref, innov_ref, error_ref, out_ref):
+def picked_kernel(count_ref, perturb_ref, cell_ref, innov_ref, error_ref, copies_ref, out_ref, sems):
     members, fine_lat, fine_lon = perturb_ref.shape
     lines = cell_ref.shape[0]
     step = 512
@@ -94,16 +94,24 @@
             for r in range(per_step):
                 at = (3 + k) * lines + start + r
                 out_ref[at : at + 1, :] = found[:, r * LANES : (r + 1) * LANES]
-
-
-def picked(count, perturb, cell, innovation, error):
+    sends = [
+        pltpu.make_async_copy(out_ref, copies_ref.at[n], sems.at[n]) for n in range(copies_ref.shape[0])
+    ]
+    for send in sends:
+        send.start()
+    for send in sends:
+        send.wait()
+
+
+def picked(count, perturb, cell, innovation, error, copies):
     whole = pl.BlockSpec(memory_space=pltpu.VMEM)
-    fields = 3 + perturb.shape[0]
+    message = ((3 + perturb.shape[0]) * cell.shape[0], LANES)
     return pl.pallas_call(
         picked_kernel,
-        out_shape=jax.ShapeDtypeStruct((fields * cell.shape[0], LANES), f32),
+        out_shape=pltpu.HBM((copies, *message), f32),
         in_specs=[pl.BlockSpec(memory_space=pltpu.SMEM)] + [whole] * 4,
-        out_specs=whole,
+        out_specs=pl.BlockSpec(memory_space=pltpu.HBM),
+        scratch_shapes=[pltpu.VMEM(message, f32), pltpu.SemaphoreType.DMA((copies,))],
         compiler_params=pltpu.CompilerParams(vmem_limit_bytes=60 * 1024 * 1024),
         name="picked",
     )(count, perturb, cell, innovation, error)
@@ -144,7 +152,7 @@
     if not first:
         length_ref, own_ref = refs[:2]
         refs = refs[2:]
-    hold, total_ref, coarse_own_ref, image_ref, sems = refs
+    hold, total_ref, coarse_own_ref, image_ref, quarters_ref, sems = refs
     tiles = known_ref.shape[0]
     lines = known_ref.shape[1] // (3 + members)
     width = total_ref.shape[2]
@@ -180,21 +188,26 @@
             n += 2
     total_ref[...] = jnp.zeros_like(total_ref)
 
-    def line(i, t):
+    quarter = lines // 4
+    for t in range(tiles):
+        used = jnp.sum(jnp.where(inverse[t] > 0.0, 1.0, 0.0)).astype(jnp.int32)
+        quarters_ref[t] = jnp.maximum((used + (quarter * LANES - 1)) // (quarter * LANES), 1)
+
+    def line(i, t, count):
         return lane_rows(
-            lambda r: jnp.broadcast_to(hold[i, t, r : r + 1, :], (16, LANES)).astype(bf16), lines
+            lambda r: jnp.broadcast_to(hold[i, t, r : r + 1, :], (16, LANES)).astype(bf16), count
         )
 
-    def add_tile(t):
+    def add_tile(t, count):
         lat = t // lon_tiles
         lon = t - lat * lon_tiles
-        cols = hat(masks(line(1, t), COLS), line(2, t), line(3, t))
-        where = masks(line(0, t), ROWS)
+        cols = hat(masks(line(1, t, count), COLS), line(2, t, count), line(3, t, count))
+        where = masks(line(0, t, count), ROWS)
         blocks = []
         for k in range(members):
             for term in range(2):
                 at = 7 + 4 * k + term
-                blocks.append(hat(where, line(at, t), line(at + 2, t)))
+                blocks.append(hat(where, line(at, t, count), line(at + 2, t, count)))
         made = nt_dot(jnp.concatenate(blocks, axis=0), cols)
         at = pl.ds(pl.multiple_of(lat * 96, 8), ROWS)
         for k in range(members):
@@ -202,18 +215,18 @@
             total_ref[k, at, pl.ds(pl.multiple_of(lon * 128, 128), 128)] += both[:, :128]
             total_ref[k, at, pl.ds(pl.multiple_of(lon * 128 + 128, 128), COLS - 128)] += both[:, 128:]
 
-    def some_tiles(t, carry):
-        for n in range(TOGETHER):
-            add_tile(t * TOGETHER + n)
+    def one_tile(t, carry):
+        for n in range(1, 5):
+            pl.when(quarters_ref[t] == n)(functools.partial(add_tile, t, n * quarter))
         return carry
 
-    lax.fori_loop(0, tiles // TOGETHER, some_tiles, 0)
+    lax.fori_loop(0, tiles, one_tile, 0)
     total_copy = pltpu.make_async_copy(total_ref, total_out_ref, sems.at[0])
     total_copy.start()
 
     own = tile_ref[0]
-    rows = hat(masks(line(0, own), ROWS), line(4, own), line(5, own)).astype(f32)
-    cols = hat(masks(line(1, own), COLS), line(2, own), line(3, own))
+    rows = hat(masks(line(0, own, lines), ROWS), line(4, own, lines), line(5, own, lines)).astype(f32)
+    cols = hat(masks(line(1, own, lines), COLS), line(2, own, lines), line(3, own, lines))
     high, low = zip(*(split_two(total_ref[k]) for k in range(members)))
     high, low = jnp.concatenate(high, axis=1), jnp.concatenate(low, axis=1)
     half = dot(jnp.concatenate([left_ref[...], left_low_ref[...]], axis=0), high)
@@ -276,6 +289,7 @@
             pltpu.VMEM(total, f32),
             pltpu.VMEM((members, ROWS, COLS), f32),
             pltpu.VMEM((members, lines, LANES), f32),
+            pltpu.SMEM((tiles,), jnp.int32),
             pltpu.SemaphoreType.DMA((2,)),
         ],
         compiler_params=pltpu.CompilerParams(vmem_limit_bytes=24 * 1024 * 1024),
@@ -283,46 +297,44 @@
     )(tile, *arrays)
 
 
-def ends_length(ends_ref):
-    return length_of(jnp.sum(ends_ref[:, 1, :]), jnp.sum(ends_ref[:, 0, :]))
-
-
-def field_kernel(scale, perturb_ref, length_ref, ends_ref, c1_far, c2_far, out_ref, c1_ref, c2_ref, sems):
-    copies = [
-        pltpu.make_async_copy(c1_far, c1_ref, sems.at[0]),
-        pltpu.make_async_copy(c2_far, c2_ref, sems.at[1]),
-    ]
-    for copy in copies:
-        copy.start()
+def refined(count, cells, axis):
+    shape = (count, cells) if axis == 0 else (cells, count)
+    fine = lax.broadcasted_iota(jnp.int32, shape, axis).astype(f32)
+    cell = lax.broadcasted_iota(jnp.int32, shape, 1 - axis).astype(f32)
+    return jnp.maximum(1.0 - jnp.abs((fine + 2.5) * 0.25 - cell), 0.0).astype(bf16)
+
+
+def put_field(perturb_ref, coarse, scale, out_ref, skip):
     members, fine_lat, fine_lon = perturb_ref.shape
-    pieces, piece_rows, piece_cols = out_ref.shape
-    across = fine_lon // piece_cols
-    one = length_ref[0, 0]
-    two = ends_length(ends_ref)
-
-    def refined(count, cells, axis):
-        shape = (count, cells) if axis == 0 else (cells, count)
-        fine = lax.broadcasted_iota(jnp.int32, shape, axis).astype(f32)
-        cell = lax.broadcasted_iota(jnp.int32, shape, 1 - axis).astype(f32)
-        return jnp.maximum(1.0 - jnp.abs((fine + 2.5) * 0.25 - cell), 0.0).astype(bf16)
-
     to_rows = refined(fine_lat, ROWS, 0)
     to_cols = refined(fine_lon, COLS, 1)
     field = jnp.zeros((fine_lat, fine_lon), f32)
-    for copy in copies:
-        copy.wait()
-    for k in range(members):
-        coarse = one * c1_ref[k] + two * c2_ref[k]
-        high, low = split_two(coarse)
+    for k in range(members):
+        high, low = split_two(coarse[k])
         tall = dot(to_rows, high) + dot(to_rows, low)
         high, low = split_two(tall)
         field = field + (dot(high, to_cols) + dot(low, to_cols)) * perturb_ref[k]
-    field = -scale * field
-    for n in range(pieces * piece_rows // 8):
+    field = scale * field
+    across = fine_lon // LANES
+    per_part = fine_lat // 8 * across // out_ref.shape[0]
+    for n in range(per_part * out_ref.shape[0]):
         i = n // across * 8
-        j = n % across * piece_cols
-        at = n * 8 % piece_rows
-        out_ref[n * 8 // piece_rows, at : at + 8, :] = field[i : i + 8, j : j + piece_cols]
+        j = n % across * LANES
+        at = skip + n % per_part * 8
+        out_ref[n // per_part, at : at + 8, :] = field[i : i + 8, j : j + LANES]
+
+
+def fields_kernel(scale, perturb_ref, length_ref, coarse_1_ref, coarse_2_ref, out_ref):
+    put_field(perturb_ref, coarse_1_ref, -scale * length_ref[0, 0], out_ref.at[0], 0)
+    put_field(perturb_ref, coarse_2_ref, -scale, out_ref.at[1], 0)
+
+
+def ends_length(ends_ref):
+    return length_of(jnp.sum(ends_ref[:, 1, :]), jnp.sum(ends_ref[:, 0, :]))
+
+
+def join_kernel(ends_ref, fields_ref, out_ref):
+    out_ref[...] = fields_ref[0] + ends_length(ends_ref) * fields_ref[1]
 
 
 def analysis_kernel(length_ref, ends_ref, total_1_ref, total_2_ref, left_ref, right_ref, out_ref):
@@ -332,6 +344,20 @@
         total = one * total_1_ref[k] + two * total_2_ref[k]
         half = jnp.dot(left_ref[...], total, precision=highest, preferred_element_type=f32)
         out_ref[k] = -jnp.dot(half, right_ref[...], precision=highest, preferred_element_type=f32)
+
+
+def small_call(kernel, shapes, flops, name, *arrays):
+    whole = pl.BlockSpec(memory_space=pltpu.VMEM)
+    made = pl.pallas_call(
+        kernel,
+        out_shape=[jax.ShapeDtypeStruct(shape, f32) for shape in shapes],
+        in_specs=[whole] * len(arrays),
+        out_specs=[whole] * len(shapes),
+        compiler_params=pltpu.CompilerParams(vmem_limit_bytes=20 * 1024 * 1024),
+        cost_estimate=pl.CostEstimate(flops=flops, bytes_accessed=2 * 10**6, transcendentals=0),
+        name=name,
+    )(*arrays)
+    return made if len(shapes) > 1 else made[0]
 
 
 def per_device(perturb, loc_lat, loc_lon, obs_cell, obs_count, obs_innov, obs_error):
@@ -350,8 +376,8 @@
     cell = obs_cell.reshape(lines, LANES)
     innovation = obs_innov.reshape(lines, LANES)
     error = obs_error.reshape(lines, LANES)
-    message = picked(obs_count.reshape(1), perturb, cell, innovation, error)
-    known = sent_to_all(message, TILES)
+    message = picked(obs_count.reshape(1), perturb, cell, innovation, error, lat_tiles * lon_tiles)
+    known = lax.all_to_all(message, TILES, 0, 0, tiled=True)
 
     first_lat, first_lon = lat * coarse_lat, lon * coarse_lon
     lat_all = kernel_block(loc_lat, -1, padded_lat, 0, total_lat)
@@ -374,22 +400,25 @@
     bent = jnp.sum(jnp.stack([(mine * own[0]) ** 2, mine * own[1]]), axis=1)
     ends = sent_to_all(bent, TILES)
 
+    field_rows = fine_lat * fine_lon // LANES
+    along_x, along_z = lax.axis_size(X), lax.axis_size(Z)
+    part_rows, piece_rows = field_rows // along_x, field_rows // groups
+    part = (along_x, part_rows, LANES)
+    fields = small_call(
+        functools.partial(fields_kernel, scale),
+        ((2, *part),),
+        10**9,
+        "fields",
+        perturb,
+        length_1,
+        coarse_1,
+        coarse_2,
+    )
+    field = small_call(join_kernel, (part,), 10**6, "join", ends, fields)
+    field = jnp.sum(lax.all_to_all(field, X, 0, 0, tiled=True), axis=0).reshape(along_z, piece_rows, LANES)
+    field = jnp.sum(lax.all_to_all(field, Z, 0, 0, tiled=True), axis=0)
+    everything = sent_to_all(sent_to_all(field, Z).reshape(part_rows, LANES), X)
     whole = pl.BlockSpec(memory_space=pltpu.VMEM)
-    piece_cols = 128
-    piece_rows = fine_lat * fine_lon // groups // piece_cols
-    pieces = pl.pallas_call(
-        functools.partial(field_kernel, scale),
-        out_shape=jax.ShapeDtypeStruct((groups, piece_rows, piece_cols), f32),
-        in_specs=[whole] * 3 + [pl.BlockSpec(memory_space=pltpu.HBM)] * 2,
-        out_specs=whole,
-        scratch_shapes=[
-            pltpu.VMEM((members, ROWS, COLS), f32),
-            pltpu.VMEM((members, ROWS, COLS), f32),
-            pltpu.SemaphoreType.DMA((2,)),
-        ],
-        compiler_params=pltpu.CompilerParams(vmem_limit_bytes=24 * 1024 * 1024),
-        name="field",
-    )(perturb, length_1, ends, coarse_1, coarse_2)
     analysis = pl.pallas_call(
         analysis_kernel,
         out_shape=jax.ShapeDtypeStruct((members, coarse_lat, coarse_lon), f32),
@@ -399,11 +428,9 @@
         cost_estimate=pl.CostEstimate(flops=2 * 10**9, bytes_accessed=5 * 10**6, transcendentals=0),
         name="analysis",
     )(length_1, ends, total_1, total_2, left_own, right_own)
-    summed = jnp.sum(lax.all_to_all(pieces, MEM, 0, 0, tiled=True), axis=0)
-    everything = sent_to_all(summed, MEM)
-    across = fine_lon // piece_cols
+    across = fine_lon // LANES
     increment = jnp.transpose(
-        everything.reshape(fine_lat // 8, across, 8, piece_cols), (0, 2, 1, 3)
+        everything.reshape(fine_lat // 8, across, 8, LANES), (0, 2, 1, 3)
     ).reshape(fine_lat, fine_lon)
     return analysis, increment
 

time: 186 us -> 185 us (level)
  the two profiles are of different devices: /device:TPU:1 before, /device:TPU:2 now
where the time goes in v5:
time: 185 us; the launch traced here: 184 us
  blocking collectives  84.2 us (46%)
  Pallas kernels  36.7 us (20%)
  waiting for transfers between devices  29.5 us (16%)
  starting transfers between devices  19 us (10%)
  local copies, waits for them, and re-layouts  9.11 us (5%)
  matrix products  2.98 us (2%)
    all_to_all x2, blocking collectives, per_device(): mine = jnp.sum(lax.all_to_all(part, MEM, 0, 0, tiled=True), axis=0)  40 us
    pallas_call x2, Pallas kernels, sweep(): pl.pallas_call(functools.partial(sweep_kernel, first, scale, lon_tiles, m...  25.6 us
    all_to_all x3, waiting for transfers between devices, sent_to_all(): return lax.all_to_all(copies, axis, split_axis=0, concat_axis=0, tiled=True)  16.3 us
    all_to_all x1, blocking collectives, per_device(): lax.all_to_all(field, X, 0, 0, tiled=True)  15.7 us
    all_to_all x1, blocking collectives, sent_to_all(): return lax.all_to_all(copies, axis, split_axis=0, concat_axis=0, tiled=True)  15.3 us
    all_to_all x1, waiting for transfers between devices, per_device(): known = lax.all_to_all(message, TILES, 0, 0, tiled=True)  13.2 us
    all_to_all x1, blocking collectives, per_device(): field = jnp.sum(lax.all_to_all(field, Z, 0, 0, tiled=True), axis=0)  13.1 us
    all_to_all x3, starting transfers between devices, sent_to_all(): return lax.all_to_all(copies, axis, split_axis=0, concat_axis=0, tiled=True)  11.8 us
  transfers between devices with their start and end apart: 4, of which 4 were waited for; matrix products, arithmetic and copies ran while one was open for 3% of the time, Pallas kernels for 2%

profile of v5, /device:TPU:2, one launch (start us, length us, event | category | flops | bytes accessed | tf_op | source)
XLA Modules:
  0.0 184.3 jit_solution(15809757121539857164)
XLA Ops:
  1.3 0.0 copy-start.8
  1.3 6.3 %picked.1 = f32[16,80,128]{2,1,0:T(8,128)} custom-call(s32[1]{0:T(128)} %bitcast.17.count_ref, f32[2,384,512]{2,1,0:T(8,128)} %perturb_ref.3, s32[16,128]{1,0:T(8,128)} %bitcast.21, f32[16,128]{1,0:T(8,128)} %bitcast.22, f32[16,128]{1,0:T(8,128)} %bitcast.23), custom_call_target="tpu_custom_call" | custom-call | tf_op jit(solution)/shard_map/picked/pallas_call | solution.py:109
  7.6 7.2 %all-to-all-start = ((f32[16,80,128]{2,1,0:T(8,128)}), f32[16,80,128]{2,1,0:T(8,128)S(1)}, u32[]{:S(2)}, u32[]{:S(2)}) async-start(f32[16,80,128]{2,1,0:T(8,128)} %picked.1), calls=%async_computation | async-start | bytes 1310720 | tf_op jit(solution)/shard_map/all_to_all | solution.py:380
  14.8 0.0 copy-done.8
  14.8 0.1 power_select_fusion
  14.9 0.1 and_select_fusion
  15.0 2.0 %fusion.56 = (bf16[640,144]{0,1:T(8,128)(2,1)S(1)}, f32[640,144]{0,1:T(8,128)S(1)}) fusion(f32[512]{0:T(512)S(1)} %integer_pow.44, f32[144]{0:T(256)S(1)} %get-tuple-element.21, s32[144]{0:T(256)S(1)} %iota_add_fusion.2, f32[144]{0:T(256)S(1)} %get-tuple-element.20, f32[640]{0:T(1024)S(1)} %get-tuple-element.23, s32[640]{0:T(1024)S(1)} %iota_add_fusion, ...), kind=kOutput, calls=%fused_computation.79 | convolution fusion | flops 569133056 | bytes 564416 | tf_op jit(solution)/shard_map/ab,cb->ac/dot_general | solution.py:388
  17.0 0.0 copy-start.7
  17.1 0.2 copy.22.refs_4_.refs_5_
  17.3 0.2 copy.20
  17.5 0.2 copy-done.7
  17.7 0.1 and_select_fusion.1
  17.8 0.1 power_select_fusion.1
  17.9 1.0 fusion.55
  18.9 0.1 copy.21.refs_2_.refs_3_
  19.0 0.1 copy.18
  19.2 0.1 subtract_convert_fusion.refs_5_.refs_6_
  19.3 13.2 %all-to-all-done.refs_1_ = f32[16,80,128]{2,1,0:T(8,128)S(1)} async-done(((f32[16,80,128]{2,1,0:T(8,128)}), f32[16,80,128]{2,1,0:T(8,128)S(1)}, u32[]{:S(2)}, u32[]{:S(2)}) %all-to-all-start) | async-done | bytes 655392 | tf_op jit(solution)/shard_map/all_to_all | solution.py:380
  32.5 13.3 %sweep_first.1 = (f32[32,16,128]{2,1,0:T(8,128)S(1)}, f32[2,112,144]{2,1,0:T(8,128)}, f32[2,400,640]{2,1,0:T(8,128)}) custom-call(s32[1]{0:T(128)} %bitcast.refs_0_, f32[16,80,128]{2,1,0:T(8,128)S(1)} %all-to-all-done.refs_1_, bf16[112,400]{1,0:T(8,128)(2,1)S(1)} %copy.21.refs_2_.refs_3_, bf16[112,400]{1,0:T(8,128)(2,1)S(1)} %subtract_convert_fusion.1.refs_3_.refs_4_, ...), custom_call_target="tpu_custom_call" | custom-call | tf_op jit(solution)/shard_map/sweep_first/pallas_call | solution.py:282
  45.8 23.0 %all_to_all.45 = f32[32,16,128]{2,1,0:T(8,128)S(1)} all-to-all(f32[32,16,128]{2,1,0:T(8,128)S(1)} %get-tuple-element.10), channel_id=1, replica_groups=mesh['mem_0'=4,'mem_1'=8,'lat_0'=2,'lat_1'=2,'lon'=4] {'mem_0','mem_1'}, dimensions={0} | all-to-all | bytes 524288 | tf_op jit(solution)/shard_map/all_to_all | solution.py:394
  68.9 15.3 %all_to_all.46.refs_2_ = f32[16,16,128]{2,1,0:T(8,128)S(1)} all-to-all(f32[16,16,128]{2,1,0:T(8,128)S(1)} %broadcast_in_dim.14), channel_id=1, replica_groups=mesh['mem_0'=4,'mem_1'=8,'lat_0'=2,'lat_1'=2,'lon'=4] {'lat_0','lat_1','..., dimensions={0} | all-to-all | bytes 262144 | tf_op jit(solution)/shard_map/all_to_all | solution.py:29
  84.2 12.3 %sweep_second.1 = (f32[32,16,128]{2,1,0:T(8,128)S(1)}, f32[2,112,144]{2,1,0:T(8,128)}, f32[2,400,640]{2,1,0:T(8,128)}, f32[1,128]{1,0:T(1,128)S(1)}, f32[2,16,128]{2,1,0:T(8,128)S(1)}) custom-call(s32[1]{0:T(128)} %bitcast.refs_0_, f32[16,80,128]{2,1,0:T(8,128)S(1)} %all-to-all-done.refs_1_, f32[16,16,128]{2,1,0:T(8,128)S(1)} %all_to_all.46.refs_2_, ...), custom_call_target="tpu_custom_call" | custom-call | tf_op jit(solution)/shard_map/sweep_second/pallas_call | solution.py:282
  96.5 17.0 %all_to_all.47 = f32[32,16,128]{2,1,0:T(8,128)S(1)} all-to-all(f32[32,16,128]{2,1,0:T(8,128)S(1)} %get-tuple-element.12), channel_id=1, replica_groups=mesh['mem_0'=4,'mem_1'=8,'lat_0'=2,'lat_1'=2,'lon'=4] {'mem_0','mem_1'}, dimensions={0} | all-to-all | bytes 524288 | tf_op jit(solution)/shard_map/all_to_all | solution.py:399
  113.5 0.6 broadcast_in_dim.15
  114.2 3.5 %all-to-all-start.4 = ((f32[16,2,128]{2,1,0:T(2,128)}), f32[16,2,128]{2,1,0:T(2,128)S(1)}, u32[]{:S(2)}, u32[]{:S(2)}) async-start(f32[16,2,128]{2,1,0:T(2,128)} %broadcast_in_dim.15), calls=%async_computation.4 | async-start | bytes 32768 | tf_op jit(solution)/shard_map/all_to_all | solution.py:29
  117.7 0.0 copy-done
  117.7 0.0 copy-done.5
  117.7 0.9 copy-done.6
  118.6 1.7 fields.1.fields_ref
  120.3 1.2 copy-done.1
  121.5 3.7 %all-to-all-done.4.ends_ref = f32[16,2,128]{2,1,0:T(2,128)S(1)} async-done(((f32[16,2,128]{2,1,0:T(2,128)}), f32[16,2,128]{2,1,0:T(2,128)S(1)}, u32[]{:S(2)}, u32[]{:S(2)}) %all-to-all-start.4) | async-done | bytes 16416 | tf_op jit(solution)/shard_map/all_to_all | solution.py:29
  125.2 1.4 copy-done.2
  126.6 0.3 join.1
  126.9 15.7 %all_to_all.48 = f32[4,384,128]{2,1,0:T(8,128)S(1)} all-to-all(f32[4,384,128]{2,1,0:T(8,128)S(1)} %join.1), channel_id=1, replica_groups=mesh['mem_0'=4,'mem_1'=8,'lat_0'=2,'lat_1'=2,'lon'=4] {'mem_0'}, dimensions={0} | all-to-all | bytes 1572864 | tf_op jit(solution)/shard_map/all_to_all | solution.py:418
  142.6 13.1 %all_to_all.49 = f32[8,48,128]{2,1,0:T(8,128)S(1)} all-to-all(f32[8,48,128]{2,1,0:T(8,128)S(1)} %bitcast.19), channel_id=1, replica_groups=mesh['mem_0'=4,'mem_1'=8,'lat_0'=2,'lat_1'=2,'lon'=4] {'mem_1'}, dimensions={0} | all-to-all | bytes 393216 | tf_op jit(solution)/shard_map/all_to_all | solution.py:419
  155.8 0.7 broadcast_in_dim.16
  156.5 3.4 %all-to-all-start.7 = ((f32[8,48,128]{2,1,0:T(8,128)}), f32[8,48,128]{2,1,0:T(8,128)S(1)}, u32[]{:S(2)}, u32[]{:S(2)}) async-start(f32[8,48,128]{2,1,0:T(8,128)} %broadcast_in_dim.16), calls=%async_computation.7 | async-start | bytes 393216 | tf_op jit(solution)/shard_map/all_to_all | solution.py:29
  159.9 0.1 fusion.51
  160.0 0.1 fusion.31.left_ref
  160.1 9.4 %all-to-all-done.7 = f32[8,48,128]{2,1,0:T(8,128)S(1)} async-done(((f32[8,48,128]{2,1,0:T(8,128)}), f32[8,48,128]{2,1,0:T(8,128)S(1)}, u32[]{:S(2)}, u32[]{:S(2)}) %all-to-all-start.7) | async-done | bytes 196640 | tf_op jit(solution)/shard_map/all_to_all | solution.py:29
  169.6 0.9 broadcast_in_dim.17
  170.5 4.9 %all-to-all-start.8 = ((f32[4,384,128]{2,1,0:T(8,128)}), f32[4,384,128]{2,1,0:T(8,128)S(1)}, u32[]{:S(2)}, u32[]{:S(2)}) async-start(f32[4,384,128]{2,1,0:T(8,128)} %broadcast_in_dim.17), calls=%async_computation.8 | async-start | bytes 1572864 | tf_op jit(solution)/shard_map/all_to_all | solution.py:29
  175.4 0.1 fusion.52
  175.5 0.3 fusion.16.right_ref
  175.8 1.6 copy-done.4
  177.4 2.8 %analysis.1 = f32[2,96,128]{2,1,0:T(8,128)} custom-call(f32[1,128]{1,0:T(1,128)S(1)} %get-tuple-element.11.length_ref, f32[16,2,128]{2,1,0:T(2,128)S(1)} %all-to-all-done.4.ends_ref, f32[2,400,640]{2,1,0:T(8,128)S(1)} %copy-done.3, f32[2,400,640]{2,1,0:T(8,128)S(1)} %copy-done.4, f32[96,400]{1,0:T(8,128)S(1)} %fusion.31.left_ref, ...), custom_call_target="tpu_custom_call" | custom-call | flops 2000000000 | bytes 5000000 | tf_op jit(solution)/shard_map/analysis/pallas_call | solution.py:422
  180.2 3.2 %all-to-all-done.8 = f32[4,384,128]{2,1,0:T(8,128)S(1)} async-done(((f32[4,384,128]{2,1,0:T(8,128)}), f32[4,384,128]{2,1,0:T(8,128)S(1)}, u32[]{:S(2)}, u32[]{:S(2)}) %all-to-all-start.8) | async-done | bytes 786464 | tf_op jit(solution)/shard_map/all_to_all | solution.py:29
  183.4 0.9 copy.27
  (24 shorter events, 0.2 us)
Async XLA Ops:
  1.3 13.5 %copy-start.8 = (f32[512]{0:T(512)S(1)}, f32[512]{0:T(512)}, u32[]{:S(2)}) copy-start(f32[512]{0:T(512)} %param.9) | copy-start | bytes 6148
  7.6 24.9 %all-to-all-start = ((f32[16,80,128]{2,1,0:T(8,128)}), f32[16,80,128]{2,1,0:T(8,128)S(1)}, u32[]{:S(2)}, u32[]{:S(2)}) async-start(f32[16,80,128]{2,1,0:T(8,128)} %picked.1), calls=%async_computation | async-start | bytes 1310720 | tf_op jit(solution)/shard_map/all_to_all | solution.py:380
  17.0 0.7 copy-start.7
  84.2 33.5 %copy-start = (f32[2,384,512]{2,1,0:T(8,128)S(1)}, f32[2,384,512]{2,1,0:T(8,128)}, u32[]{:S(2)}) copy-start(f32[2,384,512]{2,1,0:T(8,128)} %perturb_ref.3) | copy-start | bytes 4718596
  84.2 33.5 %copy-start.5 = (f32[2,112,144]{2,1,0:T(8,128)S(1)}, f32[2,112,144]{2,1,0:T(8,128)}, u32[]{:S(2)}) copy-start(f32[2,112,144]{2,1,0:T(8,128)} %get-tuple-element.16.coarse_1_ref) | copy-start | bytes 387076
  114.2 11.0 %all-to-all-start.4 = ((f32[16,2,128]{2,1,0:T(2,128)}), f32[16,2,128]{2,1,0:T(2,128)S(1)}, u32[]{:S(2)}, u32[]{:S(2)}) async-start(f32[16,2,128]{2,1,0:T(2,128)} %broadcast_in_dim.15), calls=%async_computation.4 | async-start | bytes 32768 | tf_op jit(solution)/shard_map/all_to_all | solution.py:29
  117.7 0.9 copy-start.6
  120.3 1.2 copy-start.1
  125.2 1.4 copy-start.2
  156.5 13.1 %all-to-all-start.7 = ((f32[8,48,128]{2,1,0:T(8,128)}), f32[8,48,128]{2,1,0:T(8,128)S(1)}, u32[]{:S(2)}, u32[]{:S(2)}) async-start(f32[8,48,128]{2,1,0:T(8,128)} %broadcast_in_dim.16), calls=%async_computation.7 | async-start | bytes 393216 | tf_op jit(solution)/shard_map/all_to_all | solution.py:29
  169.6 6.3 %copy-start.3 = (f32[2,400,640]{2,1,0:T(8,128)S(1)}, f32[2,400,640]{2,1,0:T(8,128)}, u32[]{:S(2)}) copy-start(f32[2,400,640]{2,1,0:T(8,128)} %get-tuple-element.14.total_1_ref) | copy-start | bytes 6144004
  170.5 13.0 %all-to-all-start.8 = ((f32[4,384,128]{2,1,0:T(8,128)}), f32[4,384,128]{2,1,0:T(8,128)S(1)}, u32[]{:S(2)}, u32[]{:S(2)}) async-start(f32[4,384,128]{2,1,0:T(8,128)} %broadcast_in_dim.17), calls=%async_computation.8 | async-start | bytes 1572864 | tf_op jit(solution)/shard_map/all_to_all | solution.py:29
  175.8 1.6 copy-start.4

commit v6 on v4

--- a/solution.py
+++ b/solution.py
@@ -146,8 +146,8 @@
     tile_ref, known_ref = refs[:2]
     refs = refs[2:]
     if not first:
-        seen_ref, perturb_far = refs[:2]
-        refs = refs[2:]
+        seen_ref, perturb_ref, coarse_1_ref = refs[:3]
+        refs = refs[3:]
     left_ref, left_low_ref, right_ref, right_low_ref, part_ref, total_out_ref = refs[:6]
     refs = refs[6:]
     if first:
@@ -156,11 +156,7 @@
     else:
         length_ref, own_ref = refs[:2]
         refs = refs[2:]
-    hold, total_ref, coarse_own_ref, image_ref, sems = refs[:5]
-    if not first:
-        perturb_ref = refs[5]
-        perturb_copy = pltpu.make_async_copy(perturb_far, perturb_ref, sems.at[1])
-        perturb_copy.start()
+    hold, total_ref, coarse_own_ref, image_ref, sems = refs
     tiles = known_ref.shape[0]
     lines = known_ref.shape[1] // (3 + members)
     width = total_ref.shape[2]
@@ -259,19 +255,18 @@
         own_ref[1] = hold[6, own]
     for n in range(part_ref.shape[0]):
         part_ref[n, :lines, :] = image
-    if not first:
-        perturb_copy.wait()
-        put_field(perturb_ref, coarse_own_ref, scale, part_ref, lines)
+    if first:
+        coarse_copy.wait()
     else:
-        coarse_copy.wait()
+        put_field(perturb_ref, coarse_1_ref, -scale * length, part_ref, lines)
+        put_field(perturb_ref, coarse_own_ref, -scale, part_ref, (part_ref.shape[1] + lines) // 2)
     total_copy.wait()
 
 
-def sweep(tile, known, seen, perturb, kernels, scale, lon_tiles, part):
-    members, fine_lat, fine_lon = perturb.shape
+def sweep(tile, known, later, kernels, scale, lon_tiles, members, part):
     tiles = known.shape[0]
     lines = known.shape[1] // (3 + members)
-    first = seen is None
+    first = not later
     left, _, right, _ = kernels
     total = (members, left.shape[1], right.shape[0])
     whole = pl.BlockSpec(memory_space=pltpu.VMEM)
@@ -285,27 +280,20 @@
         out_shape.append(jax.ShapeDtypeStruct((1, LANES), f32))
         out_shape.append(jax.ShapeDtypeStruct((2, lines, LANES), f32))
         out_specs += [whole, whole]
-    arrays = [known] if first else [known, seen, perturb]
-    in_specs = [whole] if first else [whole, whole, far]
-    arrays += kernels
-    in_specs += [whole] * len(kernels)
-    scratch = [
-        pltpu.VMEM((7 + 4 * members, tiles, lines, LANES), f32),
-        pltpu.VMEM(total, f32),
-        pltpu.VMEM((members, ROWS, COLS), f32),
-        pltpu.VMEM((members, lines, LANES), f32),
-        pltpu.SemaphoreType.DMA((2,)),
-    ]
-    if not first:
-        scratch.append(pltpu.VMEM(perturb.shape, f32))
+    arrays = [known, *later, *kernels]
     return pl.pallas_call(
         functools.partial(sweep_kernel, first, scale, lon_tiles, members),
         out_shape=out_shape,
-        in_specs=[pl.BlockSpec(memory_space=pltpu.SMEM)] + in_specs,
+        in_specs=[pl.BlockSpec(memory_space=pltpu.SMEM)] + [whole] * len(arrays),
         out_specs=out_specs,
-        scratch_shapes=scratch,
-        compiler_params=pltpu.CompilerParams(vmem_limit_bytes=60 * 1024 * 1024),
-        cost_estimate=pl.CostEstimate(flops=8 * 10**9, bytes_accessed=10**7, transcendentals=0),
+        scratch_shapes=[
+            pltpu.VMEM((7 + 4 * members, tiles, lines, LANES), f32),
+            pltpu.VMEM(total, f32),
+            pltpu.VMEM((members, ROWS, COLS), f32),
+            pltpu.VMEM((members, lines, LANES), f32),
+            pltpu.SemaphoreType.DMA((2,)),
+        ],
+        compiler_params=pltpu.CompilerParams(vmem_limit_bytes=28 * 1024 * 1024),
         name="sweep_first" if first else "sweep_second",
     )(tile, *arrays)
 
@@ -337,20 +325,18 @@
         out_ref[n // per_part, at : at + 8, :] = field[i : i + 8, j : j + LANES]
 
 
-def field_kernel(scale, perturb_ref, coarse_ref, out_ref):
-    put_field(perturb_ref, coarse_ref, scale, out_ref, 0)
-
-
-def gather_x_kernel(image_and_second_ref, first_ref, out_ref):
-    parts = out_ref.shape[0]
-    lines = image_and_second_ref.shape[1] - first_ref.shape[1]
-    rows = first_ref.shape[1] // parts
-    image = jnp.sum(image_and_second_ref[:, :lines, :], axis=0)
+def gather_x_kernel(arrived_ref, out_ref):
+    parts, rows, _ = out_ref.shape
+    lines = rows - (arrived_ref.shape[1] - rows) // (parts - 1)
+    fields = (arrived_ref.shape[1] - lines) // 2
+    piece = fields // parts
+    image = jnp.sum(arrived_ref[:, :lines, :], axis=0)
     for n in range(parts):
         out_ref[n, :lines, :] = image
-        out_ref[n, lines : lines + rows, :] = jnp.sum(first_ref[:, n * rows : (n + 1) * rows, :], axis=0)
-        at = lines + n * rows
-        out_ref[n, lines + rows :, :] = jnp.sum(image_and_second_ref[:, at : at + rows, :], axis=0)
+        for k in range(2):
+            at = lines + k * fields + n * piece
+            to = lines + k * piece
+            out_ref[n, to : to + piece, :] = jnp.sum(arrived_ref[:, at : at + piece, :], axis=0)
 
 
 def gather_z_kernel(arrived_ref, own_ref, bent_ref, fields_ref):
@@ -368,11 +354,9 @@
     return length_of(jnp.sum(ends_ref[:, 1, :]), jnp.sum(ends_ref[:, 0, :]))
 
 
-def finish_kernel(length_ref, ends_ref, fields_ref, out_ref):
+def finish_kernel(ends_ref, fields_ref, out_ref):
     rows = fields_ref.shape[0] // 2
-    one = length_ref[0, 0]
-    two = ends_length(ends_ref)
-    done = -(one * fields_ref[:rows] + two * fields_ref[rows:])
+    done = fields_ref[:rows] + ends_length(ends_ref) * fields_ref[rows:]
     for n in range(out_ref.shape[0]):
         out_ref[n] = done
 
@@ -393,7 +377,7 @@
         out_shape=[jax.ShapeDtypeStruct(shape, f32) for shape in shapes],
         in_specs=[whole] * len(arrays),
         out_specs=[whole] * len(shapes),
-        compiler_params=pltpu.CompilerParams(vmem_limit_bytes=60 * 1024 * 1024),
+        compiler_params=pltpu.CompilerParams(vmem_limit_bytes=20 * 1024 * 1024),
         cost_estimate=pl.CostEstimate(flops=flops, bytes_accessed=2 * 10**6, transcendentals=0),
         name=name,
     )(*arrays)
@@ -433,34 +417,20 @@
     field_rows = fine_lat * fine_lon // LANES
     along_x, along_z = lax.axis_size(X), lax.axis_size(Z)
     part_rows, piece_rows = field_rows // along_x, field_rows // groups
-    part, total_1, coarse_1 = sweep(
-        tile, known, None, perturb, kernels, scale, lon_tiles, (groups, lines, LANES)
-    )
-    first_field = small_call(
-        functools.partial(field_kernel, scale), ((along_x, part_rows, LANES),), 3 * 10**8, "field", perturb, coarse_1
-    )
+    part, total_1, coarse_1 = sweep(tile, known, (), kernels, scale, lon_tiles, members, (groups, lines, LANES))
     mine = jnp.sum(lax.all_to_all(part, MEM, 0, 0, tiled=True), axis=0)
     seen = sent_to_all(mine, TILES)
-    first_field, seen = lax.optimization_barrier((first_field, seen))
-    first_field = lax.all_to_all(first_field, X, 0, 0, tiled=True)
+    shape = (along_x, lines + 2 * part_rows, LANES)
     part, total_2, length_1, own = sweep(
-        tile, known, seen, perturb, kernels, scale, lon_tiles, (along_x, lines + part_rows, LANES)
+        tile, known, (seen, perturb, coarse_1), kernels, scale, lon_tiles, members, shape
     )
     part = lax.all_to_all(part, X, 0, 0, tiled=True)
-    part = small_call(
-        gather_x_kernel, ((along_z, lines + 2 * piece_rows, LANES),), 10**6, "gather_x", part, first_field
-    )
+    part = small_call(gather_x_kernel, ((along_z, lines + 2 * piece_rows, LANES),), 10**6, "gather_x", part)
     part = lax.all_to_all(part, Z, 0, 0, tiled=True)
-    bent, fields = small_call(
-        gather_z_kernel,
-        ((lat_tiles * lon_tiles, 2, LANES), (2 * piece_rows, LANES)),
-        10**6,
-        "gather_z",
-        part,
-        own,
-    )
+    shapes = ((lat_tiles * lon_tiles, 2, LANES), (2 * piece_rows, LANES))
+    bent, fields = small_call(gather_z_kernel, shapes, 10**6, "gather_z", part, own)
     ends = lax.all_to_all(bent, TILES, 0, 0, tiled=True)
-    done = small_call(finish_kernel, ((along_z, piece_rows, LANES),), 10**6, "finish", length_1, ends, fields)
+    done = small_call(finish_kernel, ((along_z, piece_rows, LANES),), 10**6, "finish", ends, fields)
     done = lax.all_to_all(done, Z, 0, 0, tiled=True).reshape(part_rows, LANES)
     everything = sent_to_all(done, X)
     whole = pl.BlockSpec(memory_space=pltpu.VMEM)
@@ -469,7 +439,7 @@
         out_shape=jax.ShapeDtypeStruct((members, coarse_lat, coarse_lon), f32),
         in_specs=[whole] * 6,
         out_specs=whole,
-        compiler_params=pltpu.CompilerParams(vmem_limit_bytes=60 * 1024 * 1024),
+        compiler_params=pltpu.CompilerParams(vmem_limit_bytes=24 * 1024 * 1024),
         cost_estimate=pl.CostEstimate(flops=2 * 10**9, bytes_accessed=5 * 10**6, transcendentals=0),
         name="analysis",
     )(length_1, ends, total_1, total_2, left_own, right_own)

time: 193 us -> 186 us (0.964)
  blocking collectives: 71.7 us -> 89.5 us
  Pallas kernels: 49.4 us -> 36.5 us
  starting transfers between devices: 25.5 us -> 17.1 us
  waiting for transfers between devices: 33.1 us -> 30.9 us
    all_to_all x0 -> x1, blocking collectives: none -> 13.4 us  [sent_to_all(): return lax.all_to_all(copies, axis, split_axis=0, concat_axis=0, tiled=True)]
    pallas_call x4 -> x3, Pallas kernels: 8.86 us -> 0.98 us  [small_call(): pl.pallas_call(kernel, out_shape=[jax.ShapeDtypeStruct(shape, f32) for sh...]
    all_to_all x1, blocking collectives: 16.6 us -> 23.6 us  [per_device(): part = lax.all_to_all(part, X, 0, 0, tiled=True)]
    all_to_all x2 -> x1, starting transfers between devices: 8.22 us -> 3.49 us  [sent_to_all(): return lax.all_to_all(copies, axis, split_axis=0, concat_axis=0, tiled=True)]
    all_to_all x2 -> x1, waiting for transfers between devices: 10.3 us -> 6.04 us  [sent_to_all(): return lax.all_to_all(copies, axis, split_axis=0, concat_axis=0, tiled=True)]
    all_to_all x1 -> x0, starting transfers between devices: 3.68 us -> none  [per_device(): first_field = lax.all_to_all(first_field, X, 0, 0, tiled=True)]
    pallas_call x2, Pallas kernels: 29.2 us -> 26.4 us  [sweep(): pl.pallas_call(functools.partial(sweep_kernel, first, scale, lon_tiles, m...]
    pallas_call x1, Pallas kernels: 5.03 us -> 2.81 us  [per_device(): pl.pallas_call(analysis_kernel, out_shape=jax.ShapeDtypeStruct((members,...]
  transfers between devices with their start and end apart: 5 -> 3, of which waited for: 4 -> 3; matrix products, arithmetic and copies ran while one was open for 4% -> 3% of each run, Pallas kernels for 12% -> 2%
where the time goes in v6:
time: 186 us; the launch traced here: 185 us
  blocking collectives  89.5 us (48%)
  Pallas kernels  36.5 us (20%)
  waiting for transfers between devices  30.9 us (17%)
  starting transfers between devices  17.1 us (9%)
  local copies, waits for them, and re-layouts  4.3 us (2%)
  matrix products  2.98 us (2%)
  other arithmetic  2.08 us (1%)
    pallas_call x2, Pallas kernels, sweep(): pl.pallas_call(functools.partial(sweep_kernel, first, scale, lon_tiles, m...  26.4 us
    all_to_all x1, blocking collectives, per_device(): part = lax.all_to_all(part, X, 0, 0, tiled=True)  23.6 us
    all_to_all x1, blocking collectives, per_device(): mine = jnp.sum(lax.all_to_all(part, MEM, 0, 0, tiled=True), axis=0)  22.7 us
    all_to_all x1, blocking collectives, per_device(): part = lax.all_to_all(part, Z, 0, 0, tiled=True)  17.9 us
    all_to_all x1, waiting for transfers between devices, per_device(): known = lax.all_to_all(message, TILES, 0, 0, tiled=True)  15.2 us
    all_to_all x1, blocking collectives, sent_to_all(): return lax.all_to_all(copies, axis, split_axis=0, concat_axis=0, tiled=True)  13.4 us
    all_to_all x1, blocking collectives, per_device(): ends = lax.all_to_all(bent, TILES, 0, 0, tiled=True)  11.8 us
    all_to_all x1, starting transfers between devices, per_device(): known = lax.all_to_all(message, TILES, 0, 0, tiled=True)  10.3 us
  transfers between devices with their start and end apart: 3, of which 3 were waited for; matrix products, arithmetic and copies ran while one was open for 3% of the time, Pallas kernels for 2%

profile of v6, /device:TPU:1, one launch (start us, length us, event | category | flops | bytes accessed | tf_op | source)
XLA Modules:
  0.0 184.9 jit_solution(16355760107837826635)
XLA Ops:
  1.3 0.0 copy-start.5
  1.3 6.3 %picked.1 = f32[16,80,128]{2,1,0:T(8,128)} custom-call(s32[1]{0:T(128)} %bitcast.11.count_ref, f32[2,384,512]{2,1,0:T(8,128)} %refs_3_.1, s32[16,128]{1,0:T(8,128)} %bitcast.14, f32[16,128]{1,0:T(8,128)} %bitcast.15, f32[16,128]{1,0:T(8,128)} %bitcast.16), custom_call_target="tpu_custom_call" | custom-call | tf_op jit(solution)/shard_map/picked/pallas_call | solution.py:110
  7.6 10.3 %all-to-all-start = ((f32[16,80,128]{2,1,0:T(8,128)}), f32[16,80,128]{2,1,0:T(8,128)S(1)}, u32[]{:S(2)}, u32[]{:S(2)}) async-start(f32[16,80,128]{2,1,0:T(8,128)} %picked.1), calls=%async_computation | async-start | bytes 1310720 | tf_op jit(solution)/shard_map/all_to_all | solution.py:404
  17.8 0.0 copy-done.5
  17.9 0.1 power_select_fusion
  18.0 0.1 and_select_fusion
  18.0 2.0 %fusion.55 = (bf16[640,144]{0,1:T(8,128)(2,1)S(1)}, f32[640,144]{0,1:T(8,128)S(1)}) fusion(f32[512]{0:T(512)S(1)} %integer_pow.40, f32[144]{0:T(256)S(1)} %get-tuple-element.21, s32[144]{0:T(256)S(1)} %iota_add_fusion.2, f32[144]{0:T(256)S(1)} %get-tuple-element.20, f32[640]{0:T(1024)S(1)} %get-tuple-element.23, s32[640]{0:T(1024)S(1)} %iota_add_fusion, ...), kind=kOutput, calls=%fused_computation.75 | convolution fusion | flops 569133056 | bytes 564416 | tf_op jit(solution)/shard_map/ab,cb->ac/dot_general | solution.py:412
  20.1 0.0 copy-start.4
  20.1 0.2 copy.18.refs_4_.refs_7_
  20.3 0.2 copy.16
  20.5 0.2 copy-done.4
  20.8 0.1 and_select_fusion.1
  20.8 0.1 power_select_fusion.1
  20.9 1.0 fusion.54
  21.9 0.1 copy.17.refs_2_.refs_5_
  22.0 0.1 copy.14
  22.2 0.1 subtract_convert_fusion.refs_5_.refs_8_
  22.3 15.2 %all-to-all-done.refs_1_ = f32[16,80,128]{2,1,0:T(8,128)S(1)} async-done(((f32[16,80,128]{2,1,0:T(8,128)}), f32[16,80,128]{2,1,0:T(8,128)S(1)}, u32[]{:S(2)}, u32[]{:S(2)}) %all-to-all-start) | async-done | bytes 655392 | tf_op jit(solution)/shard_map/all_to_all | solution.py:404
  37.5 0.0 copy-start
  37.5 12.9 %sweep_first.1 = (f32[32,16,128]{2,1,0:T(8,128)S(1)}, f32[2,400,640]{2,1,0:T(8,128)}, f32[2,112,144]{2,1,0:T(8,128)}) custom-call(s32[1]{0:T(128)} %bitcast.refs_0_, f32[16,80,128]{2,1,0:T(8,128)S(1)} %all-to-all-done.refs_1_, bf16[112,400]{1,0:T(8,128)(2,1)S(1)} %copy.17.refs_2_.refs_5_, bf16[112,400]{1,0:T(8,128)(2,1)S(1)} %subtract_convert_fusion.1.refs_3_.refs_6_, ...), custom_call_target="tpu_custom_call" | custom-call | tf_op jit(solution)/shard_map/sweep_first/pallas_call | solution.py:284
  50.4 0.0 copy-start.1
  50.4 22.7 %all_to_all.40 = f32[32,16,128]{2,1,0:T(8,128)} all-to-all(f32[32,16,128]{2,1,0:T(8,128)S(1)} %get-tuple-element.11), channel_id=1, replica_groups=mesh['mem_0'=4,'mem_1'=8,'lat_0'=2,'lat_1'=2,'lon'=4] {'mem_0','mem_1'}, dimensions={0} | all-to-all | bytes 524288 | tf_op jit(solution)/shard_map/all_to_all | solution.py:421
  73.2 1.0 reduce_sum.9
  74.2 13.4 %all_to_all.41.refs_2_ = f32[16,16,128]{2,1,0:T(8,128)S(1)} all-to-all(f32[16,16,128]{2,1,0:T(8,128)S(1)} %broadcast_in_dim.10), channel_id=1, replica_groups=mesh['mem_0'=4,'mem_1'=8,'lat_0'=2,'lat_1'=2,'lon'=4] {'lat_0','lat_1','..., dimensions={0} | all-to-all | bytes 262144 | tf_op jit(solution)/shard_map/all_to_all | solution.py:30
  87.6 0.0 copy-done
  87.6 0.0 copy-done.1
  87.6 13.5 %sweep_second.1 = (f32[4,784,128]{2,1,0:T(8,128)S(1)}, f32[2,400,640]{2,1,0:T(8,128)}, f32[1,128]{1,0:T(1,128)S(1)}, f32[2,16,128]{2,1,0:T(8,128)S(1)}) custom-call(s32[1]{0:T(128)} %bitcast.refs_0_, f32[16,80,128]{2,1,0:T(8,128)S(1)} %all-to-all-done.refs_1_, f32[16,16,128]{2,1,0:T(8,128)S(1)} %all_to_all.41.refs_2_, f32[2,384,512]{2,1,0:T(8,128)S(1)} %copy-done, ...), custom_call_target="tpu_custom_call" | custom-call | tf_op jit(solution)/shard_map/sweep_second/pallas_call | solution.py:284
  101.1 23.6 %all_to_all.42.arrived_ref = f32[4,784,128]{2,1,0:T(8,128)S(1)} all-to-all(f32[4,784,128]{2,1,0:T(8,128)S(1)} %get-tuple-element.14), channel_id=1, replica_groups=mesh['mem_0'=4,'mem_1'=8,'lat_0'=2,'lat_1'=2,'lon'=4] {'mem_0'}, dimensions={0} | all-to-all | bytes 3211264 | tf_op jit(solution)/shard_map/all_to_all | solution.py:427
  124.8 0.1 gather_x.1
  124.8 17.9 %all_to_all.43.arrived_ref = f32[8,112,128]{2,1,0:T(8,128)S(1)} all-to-all(f32[8,112,128]{2,1,0:T(8,128)S(1)} %gather_x.1), channel_id=1, replica_groups=mesh['mem_0'=4,'mem_1'=8,'lat_0'=2,'lat_1'=2,'lon'=4] {'mem_1'}, dimensions={0} | all-to-all | bytes 917504 | tf_op jit(solution)/shard_map/all_to_all | solution.py:429
  142.8 11.8 %all_to_all.44.ends_ref = f32[16,2,128]{2,1,0:T(2,128)S(1)} all-to-all(f32[16,2,128]{2,1,0:T(2,128)S(1)} %get-tuple-element.16), channel_id=1, replica_groups=mesh['mem_0'=4,'mem_1'=8,'lat_0'=2,'lat_1'=2,'lon'=4] {'lat_0','lat_1','..., dimensions={0} | all-to-all | bytes 32768 | tf_op jit(solution)/shard_map/all_to_all | solution.py:432
  154.6 0.9 finish.1
  155.5 3.4 %all-to-all-start.6 = ((f32[8,48,128]{2,1,0:T(8,128)}), f32[8,48,128]{2,1,0:T(8,128)S(1)}, u32[]{:S(2)}, u32[]{:S(2)}) async-start(f32[8,48,128]{2,1,0:T(8,128)} %finish.1), calls=%async_computation.6 | async-start | bytes 393216 | tf_op jit(solution)/shard_map/all_to_all | solution.py:434
  158.9 0.1 fusion.50
  159.0 0.1 fusion.31.left_ref
  159.1 9.6 %all-to-all-done.6 = f32[8,48,128]{2,1,0:T(8,128)S(1)} async-done(((f32[8,48,128]{2,1,0:T(8,128)}), f32[8,48,128]{2,1,0:T(8,128)S(1)}, u32[]{:S(2)}, u32[]{:S(2)}) %all-to-all-start.6) | async-done | bytes 196640 | tf_op jit(solution)/shard_map/all_to_all | solution.py:434
  168.7 0.0 copy-start.2
  168.7 0.9 broadcast_in_dim.11
  169.7 3.5 %all-to-all-start.7 = ((f32[4,384,128]{2,1,0:T(8,128)}), f32[4,384,128]{2,1,0:T(8,128)S(1)}, u32[]{:S(2)}, u32[]{:S(2)}) async-start(f32[4,384,128]{2,1,0:T(8,128)} %broadcast_in_dim.11), calls=%async_computation.7 | async-start | bytes 1572864 | tf_op jit(solution)/shard_map/all_to_all | solution.py:30
  173.2 0.1 fusion.51
  173.3 0.3 fusion.16.right_ref
  173.6 0.0 copy-done.2
  173.6 0.0 copy-start.3
  173.6 1.6 copy-done.3
  175.2 2.8 %analysis.1 = f32[2,96,128]{2,1,0:T(8,128)} custom-call(f32[1,128]{1,0:T(1,128)S(1)} %get-tuple-element.13.length_ref, f32[16,2,128]{2,1,0:T(2,128)S(1)} %all_to_all.44.ends_ref, f32[2,400,640]{2,1,0:T(8,128)S(1)} %copy-done.2, f32[2,400,640]{2,1,0:T(8,128)S(1)} %copy-done.3, f32[96,400]{1,0:T(8,128)S(1)} %fusion.31.left_ref, f32[640,128]{1,0:T(8,128)S(1)} %fusion.16.right_ref), custom_call_target="tpu_custom_call" | custom-call | flops 2000000000 | bytes 5000000 | tf_op jit(solution)/shard_map/analysis/pallas_call | solution.py:437
  178.0 6.0 %all-to-all-done.7 = f32[4,384,128]{2,1,0:T(8,128)S(1)} async-done(((f32[4,384,128]{2,1,0:T(8,128)}), f32[4,384,128]{2,1,0:T(8,128)S(1)}, u32[]{:S(2)}, u32[]{:S(2)}) %all-to-all-start.7) | async-done | bytes 786464 | tf_op jit(solution)/shard_map/all_to_all | solution.py:30
  184.0 0.9 copy.23
  (11 shorter events, 0.1 us)
Async XLA Ops:
  1.3 16.6 %copy-start.5 = (f32[512]{0:T(512)S(1)}, f32[512]{0:T(512)}, u32[]{:S(2)}) copy-start(f32[512]{0:T(512)} %param.9) | copy-start | bytes 6148
  7.6 29.9 %all-to-all-start = ((f32[16,80,128]{2,1,0:T(8,128)}), f32[16,80,128]{2,1,0:T(8,128)S(1)}, u32[]{:S(2)}, u32[]{:S(2)}) async-start(f32[16,80,128]{2,1,0:T(8,128)} %picked.1), calls=%async_computation | async-start | bytes 1310720 | tf_op jit(solution)/shard_map/all_to_all | solution.py:404
  20.1 0.7 copy-start.4
  37.5 50.1 %copy-start = (f32[2,384,512]{2,1,0:T(8,128)S(1)}, f32[2,384,512]{2,1,0:T(8,128)}, u32[]{:S(2)}) copy-start(f32[2,384,512]{2,1,0:T(8,128)} %refs_3_.1) | copy-start | bytes 4718596
  50.4 37.2 %copy-start.1 = (f32[2,112,144]{2,1,0:T(8,128)S(1)}, f32[2,112,144]{2,1,0:T(8,128)}, u32[]{:S(2)}) copy-start(f32[2,112,144]{2,1,0:T(8,128)} %get-tuple-element.12.refs_4_) | copy-start | bytes 387076
  155.5 13.3 %all-to-all-start.6 = ((f32[8,48,128]{2,1,0:T(8,128)}), f32[8,48,128]{2,1,0:T(8,128)S(1)}, u32[]{:S(2)}, u32[]{:S(2)}) async-start(f32[8,48,128]{2,1,0:T(8,128)} %finish.1), calls=%async_computation.6 | async-start | bytes 393216 | tf_op jit(solution)/shard_map/all_to_all | solution.py:434
  168.7 4.9 %copy-start.2 = (f32[2,400,640]{2,1,0:T(8,128)S(1)}, f32[2,400,640]{2,1,0:T(8,128)}, u32[]{:S(2)}) copy-start(f32[2,400,640]{2,1,0:T(8,128)} %get-tuple-element.17.total_1_ref) | copy-start | bytes 6144004
  169.7 14.4 %all-to-all-start.7 = ((f32[4,384,128]{2,1,0:T(8,128)}), f32[4,384,128]{2,1,0:T(8,128)S(1)}, u32[]{:S(2)}, u32[]{:S(2)}) async-start(f32[4,384,128]{2,1,0:T(8,128)} %broadcast_in_dim.11), calls=%async_computation.7 | async-start | bytes 1572864 | tf_op jit(solution)/shard_map/all_to_all | solution.py:30
  173.6 1.6 copy-start.3

commit v7 on v6

--- a/solution.py
+++ b/solution.py
@@ -432,7 +432,6 @@
     ends = lax.all_to_all(bent, TILES, 0, 0, tiled=True)
     done = small_call(finish_kernel, ((along_z, piece_rows, LANES),), 10**6, "finish", ends, fields)
     done = lax.all_to_all(done, Z, 0, 0, tiled=True).reshape(part_rows, LANES)
-    everything = sent_to_all(done, X)
     whole = pl.BlockSpec(memory_space=pltpu.VMEM)
     analysis = pl.pallas_call(
         analysis_kernel,
@@ -443,6 +442,8 @@
         cost_estimate=pl.CostEstimate(flops=2 * 10**9, bytes_accessed=5 * 10**6, transcendentals=0),
         name="analysis",
     )(length_1, ends, total_1, total_2, left_own, right_own)
+    done, analysis = lax.optimization_barrier((done, analysis))
+    everything = sent_to_all(done, X)
     across = fine_lon // LANES
     increment = jnp.transpose(
         everything.reshape(fine_lat // 8, across, 8, LANES), (0, 2, 1, 3)

time: 186 us -> 186 us (level)
  blocking collectives: 89.5 us -> 72.8 us
  waiting for transfers between devices: 30.9 us -> 43.8 us
  starting transfers between devices: 17.1 us -> 21 us
    all_to_all x2 -> x0, blocking collectives: 29.7 us -> none  [the longest x1 17.9 us: per_device(): part = lax.all_to_all(part, Z, 0, 0, tiled=True)]
    all_to_all x1 -> x2, waiting for transfers between devices: 6.04 us -> 23.2 us  [the longest x1 16 us: per_device(): part = lax.all_to_all(part, Z, 0, 0, tiled=True)]
    all_to_all x1 -> x2, blocking collectives: 13.4 us -> 26.5 us  [sent_to_all(): return lax.all_to_all(copies, axis, split_axis=0, concat_axis=0, tiled=True)]
    all_to_all x1, waiting for transfers between devices: 9.6 us -> 5.35 us  [per_device(): done = lax.all_to_all(done, Z, 0, 0, tiled=True).reshape(part_rows, LANES)]
    all_to_all x1 -> x2, starting transfers between devices: 3.49 us -> 7.4 us  [the longest x1 3.8 us: per_device(): ends = lax.all_to_all(bent, TILES, 0, 0, tiled=True)]
  transfers between devices with their start and end apart: 3 -> 4, of which waited for: 3 -> 4; matrix products, arithmetic and copies ran while one was open for 3% -> 3% of each run, Pallas kernels for 2% -> 1%
where the time goes in v7:
time: 186 us; the launch traced here: 185 us
  blocking collectives  72.8 us (39%)
  waiting for transfers between devices  43.8 us (24%)
  Pallas kernels  37.7 us (20%)
  starting transfers between devices  21 us (11%)
  local copies, waits for them, and re-layouts  3.42 us (2%)
  matrix products  2.97 us (2%)
  other arithmetic  2.07 us (1%)
    all_to_all x2, blocking collectives, sent_to_all(): return lax.all_to_all(copies, axis, split_axis=0, concat_axis=0, tiled=True)  26.5 us
    pallas_call x2, Pallas kernels, sweep(): pl.pallas_call(functools.partial(sweep_kernel, first, scale, lon_tiles, m...  26.3 us
    all_to_all x1, blocking collectives, per_device(): part = lax.all_to_all(part, X, 0, 0, tiled=True)  23.6 us
    all_to_all x1, blocking collectives, per_device(): mine = jnp.sum(lax.all_to_all(part, MEM, 0, 0, tiled=True), axis=0)  22.7 us
    all_to_all x1, waiting for transfers between devices, per_device(): part = lax.all_to_all(part, Z, 0, 0, tiled=True)  16 us
    all_to_all x1, waiting for transfers between devices, per_device(): known = lax.all_to_all(message, TILES, 0, 0, tiled=True)  15.2 us
    all_to_all x1, starting transfers between devices, per_device(): known = lax.all_to_all(message, TILES, 0, 0, tiled=True)  10.3 us
    all_to_all x1, waiting for transfers between devices, per_device(): ends = lax.all_to_all(bent, TILES, 0, 0, tiled=True)  7.22 us
  transfers between devices with their start and end apart: 4, of which 4 were waited for; matrix products, arithmetic and copies ran while one was open for 3% of the time, Pallas kernels for 1%

profile of v7, /device:TPU:1, one launch (start us, length us, event | category | flops | bytes accessed | tf_op | source)
XLA Modules:
  0.0 185.3 jit_solution(11234198736701645366)
XLA Ops:
  1.3 0.0 copy-start.4
  1.3 6.3 %picked.1 = f32[16,80,128]{2,1,0:T(8,128)} custom-call(s32[1]{0:T(128)} %bitcast.11.count_ref, f32[2,384,512]{2,1,0:T(8,128)} %refs_3_.1, s32[16,128]{1,0:T(8,128)} %bitcast.14, f32[16,128]{1,0:T(8,128)} %bitcast.15, f32[16,128]{1,0:T(8,128)} %bitcast.16), custom_call_target="tpu_custom_call" | custom-call | tf_op jit(solution)/shard_map/picked/pallas_call | solution.py:110
  7.6 10.3 %all-to-all-start = ((f32[16,80,128]{2,1,0:T(8,128)}), f32[16,80,128]{2,1,0:T(8,128)S(1)}, u32[]{:S(2)}, u32[]{:S(2)}) async-start(f32[16,80,128]{2,1,0:T(8,128)} %picked.1), calls=%async_computation | async-start | bytes 1310720 | tf_op jit(solution)/shard_map/all_to_all | solution.py:404
  17.8 0.0 copy-done.4
  17.9 0.1 power_select_fusion
  18.0 0.1 and_select_fusion
  18.0 2.0 %fusion.55 = (bf16[640,144]{0,1:T(8,128)(2,1)S(1)}, f32[640,144]{0,1:T(8,128)S(1)}) fusion(f32[512]{0:T(512)S(1)} %integer_pow.40, f32[144]{0:T(256)S(1)} %get-tuple-element.25, s32[144]{0:T(256)S(1)} %iota_add_fusion.2, f32[144]{0:T(256)S(1)} %get-tuple-element.24, f32[640]{0:T(1024)S(1)} %get-tuple-element.27, s32[640]{0:T(1024)S(1)} %iota_add_fusion, ...), kind=kOutput, calls=%fused_computation.75 | convolution fusion | flops 569133056 | bytes 564416 | tf_op jit(solution)/shard_map/ab,cb->ac/dot_general | solution.py:412
  20.1 0.0 copy-start.5
  20.1 0.2 copy.18.refs_4_.refs_7_
  20.3 0.2 copy.16
  20.5 0.2 copy-done.5
  20.8 0.1 and_select_fusion.1
  20.8 0.1 power_select_fusion.1
  20.9 1.0 fusion.54
  21.9 0.1 copy.17.refs_2_.refs_5_
  22.0 0.1 copy.14
  22.2 0.1 subtract_convert_fusion.refs_5_.refs_8_
  22.3 15.2 %all-to-all-done.refs_1_ = f32[16,80,128]{2,1,0:T(8,128)S(1)} async-done(((f32[16,80,128]{2,1,0:T(8,128)}), f32[16,80,128]{2,1,0:T(8,128)S(1)}, u32[]{:S(2)}, u32[]{:S(2)}) %all-to-all-start) | async-done | bytes 655392 | tf_op jit(solution)/shard_map/all_to_all | solution.py:404
  37.5 0.0 copy-start
  37.5 12.9 %sweep_first.1 = (f32[32,16,128]{2,1,0:T(8,128)S(1)}, f32[2,400,640]{2,1,0:T(8,128)}, f32[2,112,144]{2,1,0:T(8,128)}) custom-call(s32[1]{0:T(128)} %bitcast.refs_0_, f32[16,80,128]{2,1,0:T(8,128)S(1)} %all-to-all-done.refs_1_, bf16[112,400]{1,0:T(8,128)(2,1)S(1)} %copy.17.refs_2_.refs_5_, bf16[112,400]{1,0:T(8,128)(2,1)S(1)} %subtract_convert_fusion.1.refs_3_.refs_6_, ...), custom_call_target="tpu_custom_call" | custom-call | tf_op jit(solution)/shard_map/sweep_first/pallas_call | solution.py:284
  50.4 0.0 copy-start.1
  50.4 22.7 %all_to_all.40 = f32[32,16,128]{2,1,0:T(8,128)} all-to-all(f32[32,16,128]{2,1,0:T(8,128)S(1)} %get-tuple-element.13), channel_id=1, replica_groups=mesh['mem_0'=4,'mem_1'=8,'lat_0'=2,'lat_1'=2,'lon'=4] {'mem_0','mem_1'}, dimensions={0} | all-to-all | bytes 524288 | tf_op jit(solution)/shard_map/all_to_all | solution.py:421
  73.1 1.0 reduce_sum.9
  74.1 13.4 %all_to_all.41.refs_2_ = f32[16,16,128]{2,1,0:T(8,128)S(1)} all-to-all(f32[16,16,128]{2,1,0:T(8,128)S(1)} %broadcast_in_dim.10), channel_id=1, replica_groups=mesh['mem_0'=4,'mem_1'=8,'lat_0'=2,'lat_1'=2,'lon'=4] {'lat_0','lat_1','..., dimensions={0} | all-to-all | bytes 262144 | tf_op jit(solution)/shard_map/all_to_all | solution.py:30
  87.6 0.0 copy-done
  87.6 0.0 copy-done.1
  87.6 13.4 %sweep_second.1 = (f32[4,784,128]{2,1,0:T(8,128)S(1)}, f32[2,400,640]{2,1,0:T(8,128)}, f32[1,128]{1,0:T(1,128)S(1)}, f32[2,16,128]{2,1,0:T(8,128)S(1)}) custom-call(s32[1]{0:T(128)} %bitcast.refs_0_, f32[16,80,128]{2,1,0:T(8,128)S(1)} %all-to-all-done.refs_1_, f32[16,16,128]{2,1,0:T(8,128)S(1)} %all_to_all.41.refs_2_, f32[2,384,512]{2,1,0:T(8,128)S(1)} %copy-done, ...), custom_call_target="tpu_custom_call" | custom-call | tf_op jit(solution)/shard_map/sweep_second/pallas_call | solution.py:284
  101.0 23.6 %all_to_all.42.arrived_ref = f32[4,784,128]{2,1,0:T(8,128)S(1)} all-to-all(f32[4,784,128]{2,1,0:T(8,128)S(1)} %get-tuple-element.15), channel_id=1, replica_groups=mesh['mem_0'=4,'mem_1'=8,'lat_0'=2,'lat_1'=2,'lon'=4] {'mem_0'}, dimensions={0} | all-to-all | bytes 3211264 | tf_op jit(solution)/shard_map/all_to_all | solution.py:427
  124.6 0.8 gather_x.1
  125.5 3.6 %all-to-all-start.4 = ((f32[8,112,128]{2,1,0:T(8,128)}), f32[8,112,128]{2,1,0:T(8,128)S(1)}, u32[]{:S(2)}, u32[]{:S(2)}) async-start(f32[8,112,128]{2,1,0:T(8,128)} %gather_x.1), calls=%async_computation.4 | async-start | bytes 917504 | tf_op jit(solution)/shard_map/all_to_all | solution.py:429
  129.1 0.1 fusion.51
  129.2 0.3 fusion.16.right_ref
  129.5 16.0 %all-to-all-done.4.arrived_ref = f32[8,112,128]{2,1,0:T(8,128)S(1)} async-done(((f32[8,112,128]{2,1,0:T(8,128)}), f32[8,112,128]{2,1,0:T(8,128)S(1)}, u32[]{:S(2)}, u32[]{:S(2)}) %all-to-all-start.4) | async-done | bytes 458784 | tf_op jit(solution)/shard_map/all_to_all | solution.py:429
  145.5 0.6 gather_z.1
  146.2 3.8 %all-to-all-start.5 = ((f32[16,2,128]{2,1,0:T(2,128)}), f32[16,2,128]{2,1,0:T(2,128)S(1)}, u32[]{:S(2)}, u32[]{:S(2)}) async-start(f32[16,2,128]{2,1,0:T(2,128)} %get-tuple-element.17), calls=%async_computation.5 | async-start | bytes 32768 | tf_op jit(solution)/shard_map/all_to_all | solution.py:432
  150.0 0.1 fusion.50
  150.1 7.2 %all-to-all-done.5.ends_ref = f32[16,2,128]{2,1,0:T(2,128)S(1)} async-done(((f32[16,2,128]{2,1,0:T(2,128)}), f32[16,2,128]{2,1,0:T(2,128)S(1)}, u32[]{:S(2)}, u32[]{:S(2)}) %all-to-all-start.5) | async-done | bytes 16416 | tf_op jit(solution)/shard_map/all_to_all | solution.py:432
  157.3 0.9 finish.1
  158.1 3.4 %all-to-all-start.6 = ((f32[8,48,128]{2,1,0:T(8,128)}), f32[8,48,128]{2,1,0:T(8,128)S(1)}, u32[]{:S(2)}, u32[]{:S(2)}) async-start(f32[8,48,128]{2,1,0:T(8,128)} %finish.1), calls=%async_computation.6 | async-start | bytes 393216 | tf_op jit(solution)/shard_map/all_to_all | solution.py:434
  161.5 0.1 fusion.31.left_ref
  161.7 0.0 copy-done.2
  161.7 0.0 copy-start.3
  161.7 1.6 copy-done.3
  163.3 2.8 %analysis.1 = f32[2,96,128]{2,1,0:T(8,128)} custom-call(f32[1,128]{1,0:T(1,128)S(1)} %get-tuple-element.19.length_ref, f32[16,2,128]{2,1,0:T(2,128)S(1)} %all-to-all-done.5.ends_ref, f32[2,400,640]{2,1,0:T(8,128)S(1)} %copy-done.2, f32[2,400,640]{2,1,0:T(8,128)S(1)} %copy-done.3, f32[96,400]{1,0:T(8,128)S(1)} %fusion.31.left_ref, ...), custom_call_target="tpu_custom_call" | custom-call | flops 2000000000 | bytes 5000000 | tf_op jit(solution)/shard_map/analysis/pallas_call | solution.py:436
  166.0 5.4 %all-to-all-done.6 = f32[8,48,128]{2,1,0:T(8,128)S(1)} async-done(((f32[8,48,128]{2,1,0:T(8,128)}), f32[8,48,128]{2,1,0:T(8,128)S(1)}, u32[]{:S(2)}, u32[]{:S(2)}) %all-to-all-start.6) | async-done | bytes 196640 | tf_op jit(solution)/shard_map/all_to_all | solution.py:434
  171.4 0.1 broadcast_in_dim.11
  171.4 13.0 %all_to_all.43 = f32[4,384,128]{2,1,0:T(8,128)S(1)} all-to-all(f32[4,384,128]{2,1,0:T(8,128)S(1)} %broadcast_in_dim.11), channel_id=1, replica_groups=mesh['mem_0'=4,'mem_1'=8,'lat_0'=2,'lat_1'=2,'lon'=4] {'mem_0'}, dimensions={0} | all-to-all | bytes 1572864 | tf_op jit(solution)/shard_map/all_to_all | solution.py:30
  184.5 0.9 copy.23
  (11 shorter events, 0.1 us)
Async XLA Ops:
  1.3 16.6 %copy-start.4 = (f32[512]{0:T(512)S(1)}, f32[512]{0:T(512)}, u32[]{:S(2)}) copy-start(f32[512]{0:T(512)} %param.9) | copy-start | bytes 6148
  7.6 29.9 %all-to-all-start = ((f32[16,80,128]{2,1,0:T(8,128)}), f32[16,80,128]{2,1,0:T(8,128)S(1)}, u32[]{:S(2)}, u32[]{:S(2)}) async-start(f32[16,80,128]{2,1,0:T(8,128)} %picked.1), calls=%async_computation | async-start | bytes 1310720 | tf_op jit(solution)/shard_map/all_to_all | solution.py:404
  20.1 0.7 copy-start.5
  37.5 50.1 %copy-start = (f32[2,384,512]{2,1,0:T(8,128)S(1)}, f32[2,384,512]{2,1,0:T(8,128)}, u32[]{:S(2)}) copy-start(f32[2,384,512]{2,1,0:T(8,128)} %refs_3_.1) | copy-start | bytes 4718596
  50.4 37.2 %copy-start.1 = (f32[2,112,144]{2,1,0:T(8,128)S(1)}, f32[2,112,144]{2,1,0:T(8,128)}, u32[]{:S(2)}) copy-start(f32[2,112,144]{2,1,0:T(8,128)} %get-tuple-element.14.refs_4_) | copy-start | bytes 387076
  125.5 36.2 %copy-start.2 = (f32[2,400,640]{2,1,0:T(8,128)S(1)}, f32[2,400,640]{2,1,0:T(8,128)}, u32[]{:S(2)}) copy-start(f32[2,400,640]{2,1,0:T(8,128)} %get-tuple-element.20.total_1_ref) | copy-start | bytes 6144004
  125.5 20.1 %all-to-all-start.4 = ((f32[8,112,128]{2,1,0:T(8,128)}), f32[8,112,128]{2,1,0:T(8,128)S(1)}, u32[]{:S(2)}, u32[]{:S(2)}) async-start(f32[8,112,128]{2,1,0:T(8,128)} %gather_x.1), calls=%async_computation.4 | async-start | bytes 917504 | tf_op jit(solution)/shard_map/all_to_all | solution.py:429
  146.2 11.1 %all-to-all-start.5 = ((f32[16,2,128]{2,1,0:T(2,128)}), f32[16,2,128]{2,1,0:T(2,128)S(1)}, u32[]{:S(2)}, u32[]{:S(2)}) async-start(f32[16,2,128]{2,1,0:T(2,128)} %get-tuple-element.17), calls=%async_computation.5 | async-start | bytes 32768 | tf_op jit(solution)/shard_map/all_to_all | solution.py:432
  158.1 13.3 %all-to-all-start.6 = ((f32[8,48,128]{2,1,0:T(8,128)}), f32[8,48,128]{2,1,0:T(8,128)S(1)}, u32[]{:S(2)}, u32[]{:S(2)}) async-start(f32[8,48,128]{2,1,0:T(8,128)} %finish.1), calls=%async_computation.6 | async-start | bytes 393216 | tf_op jit(solution)/shard_map/all_to_all | solution.py:434
  161.7 1.6 copy-start.3

commit v8 on v5

--- a/solution.py
+++ b/solution.py
@@ -22,6 +22,7 @@
 ROWS = 112
 COLS = 144
 LANES = 128
+TOGETHER = 2
 
 
 def sent_to_all(x, axis):
@@ -78,7 +79,7 @@
     out_ref[2 * lines : 3 * lines] = jnp.where(slot < count_ref[0], 1.0 / error_ref[...], 0.0)
     blocks = []
     for k in range(members):
-        blocks.append(jnp.concatenate(split_two(perturb_ref[k]), axis=1))
+        blocks.extend(split_two(perturb_ref[k]))
     field = jnp.concatenate(blocks, axis=0)
     for start in range(0, lines, per_step):
         cell = lane_rows(lambda r: cell_ref[start + r : start + r + 1, :], per_step)
@@ -86,10 +87,11 @@
         col = cell - row * fine_lon
         at_col = lax.broadcasted_iota(jnp.int32, (fine_lon, step), 0) == col
         one = jnp.where(at_col, 1.0, 0.0).astype(bf16)
-        values = dot(field, jnp.concatenate([one, one], axis=0))
+        values = dot(field, one)
         at_row = lax.broadcasted_iota(jnp.int32, (fine_lat, step), 0) == row
         for k in range(members):
-            mine = values[k * fine_lat : (k + 1) * fine_lat]
+            at = 2 * k * fine_lat
+            mine = values[at : at + fine_lat] + values[at + fine_lat : at + 2 * fine_lat]
             found = jnp.sum(jnp.where(at_row, mine, 0.0), axis=0, keepdims=True)
             for r in range(per_step):
                 at = (3 + k) * lines + start + r
@@ -152,7 +154,7 @@
     if not first:
         length_ref, own_ref = refs[:2]
         refs = refs[2:]
-    hold, total_ref, coarse_own_ref, image_ref, quarters_ref, sems = refs
+    hold, total_ref, coarse_own_ref, image_ref, sems = refs
     tiles = known_ref.shape[0]
     lines = known_ref.shape[1] // (3 + members)
     width = total_ref.shape[2]
@@ -188,26 +190,21 @@
             n += 2
     total_ref[...] = jnp.zeros_like(total_ref)
 
-    quarter = lines // 4
-    for t in range(tiles):
-        used = jnp.sum(jnp.where(inverse[t] > 0.0, 1.0, 0.0)).astype(jnp.int32)
-        quarters_ref[t] = jnp.maximum((used + (quarter * LANES - 1)) // (quarter * LANES), 1)
-
-    def line(i, t, count):
+    def line(i, t):
         return lane_rows(
-            lambda r: jnp.broadcast_to(hold[i, t, r : r + 1, :], (16, LANES)).astype(bf16), count
+            lambda r: jnp.broadcast_to(hold[i, t, r : r + 1, :], (16, LANES)).astype(bf16), lines
         )
 
-    def add_tile(t, count):
+    def add_tile(t):
         lat = t // lon_tiles
         lon = t - lat * lon_tiles
-        cols = hat(masks(line(1, t, count), COLS), line(2, t, count), line(3, t, count))
-        where = masks(line(0, t, count), ROWS)
+        cols = hat(masks(line(1, t), COLS), line(2, t), line(3, t))
+        where = masks(line(0, t), ROWS)
         blocks = []
         for k in range(members):
             for term in range(2):
                 at = 7 + 4 * k + term
-                blocks.append(hat(where, line(at, t, count), line(at + 2, t, count)))
+                blocks.append(hat(where, line(at, t), line(at + 2, t)))
         made = nt_dot(jnp.concatenate(blocks, axis=0), cols)
         at = pl.ds(pl.multiple_of(lat * 96, 8), ROWS)
         for k in range(members):
@@ -215,18 +212,18 @@
             total_ref[k, at, pl.ds(pl.multiple_of(lon * 128, 128), 128)] += both[:, :128]
             total_ref[k, at, pl.ds(pl.multiple_of(lon * 128 + 128, 128), COLS - 128)] += both[:, 128:]
 
-    def one_tile(t, carry):
-        for n in range(1, 5):
-            pl.when(quarters_ref[t] == n)(functools.partial(add_tile, t, n * quarter))
+    def some_tiles(t, carry):
+        for n in range(TOGETHER):
+            add_tile(t * TOGETHER + n)
         return carry
 
-    lax.fori_loop(0, tiles, one_tile, 0)
+    lax.fori_loop(0, tiles // TOGETHER, some_tiles, 0)
     total_copy = pltpu.make_async_copy(total_ref, total_out_ref, sems.at[0])
     total_copy.start()
 
     own = tile_ref[0]
-    rows = hat(masks(line(0, own, lines), ROWS), line(4, own, lines), line(5, own, lines)).astype(f32)
-    cols = hat(masks(line(1, own, lines), COLS), line(2, own, lines), line(3, own, lines))
+    rows = hat(masks(line(0, own), ROWS), line(4, own), line(5, own)).astype(f32)
+    cols = hat(masks(line(1, own), COLS), line(2, own), line(3, own))
     high, low = zip(*(split_two(total_ref[k]) for k in range(members)))
     high, low = jnp.concatenate(high, axis=1), jnp.concatenate(low, axis=1)
     half = dot(jnp.concatenate([left_ref[...], left_low_ref[...]], axis=0), high)
@@ -289,7 +286,6 @@
             pltpu.VMEM(total, f32),
             pltpu.VMEM((members, ROWS, COLS), f32),
             pltpu.VMEM((members, lines, LANES), f32),
-            pltpu.SMEM((tiles,), jnp.int32),
             pltpu.SemaphoreType.DMA((2,)),
         ],
         compiler_params=pltpu.CompilerParams(vmem_limit_bytes=24 * 1024 * 1024),
@@ -401,7 +397,7 @@
     ends = sent_to_all(bent, TILES)
 
     field_rows = fine_lat * fine_lon // LANES
-    along_x, along_z = lax.axis_size(X), lax.axis_size(Z)
+    along_x = lax.axis_size(X)
     part_rows, piece_rows = field_rows // along_x, field_rows // groups
     part = (along_x, part_rows, LANES)
     fields = small_call(
@@ -415,8 +411,8 @@
         coarse_2,
     )
     field = small_call(join_kernel, (part,), 10**6, "join", ends, fields)
-    field = jnp.sum(lax.all_to_all(field, X, 0, 0, tiled=True), axis=0).reshape(along_z, piece_rows, LANES)
-    field = jnp.sum(lax.all_to_all(field, Z, 0, 0, tiled=True), axis=0)
+    field = lax.all_to_all(field.reshape(groups, piece_rows, LANES), MEM, 0, 0, tiled=True)
+    field = jnp.sum(field, axis=0)
     everything = sent_to_all(sent_to_all(field, Z).reshape(part_rows, LANES), X)
     whole = pl.BlockSpec(memory_space=pltpu.VMEM)
     analysis = pl.pallas_call(
@@ -424,7 +420,7 @@
         out_shape=jax.ShapeDtypeStruct((members, coarse_lat, coarse_lon), f32),
         in_specs=[whole] * 6,
         out_specs=whole,
-        compiler_params=pltpu.CompilerParams(vmem_limit_bytes=24 * 1024 * 1024),
+        compiler_params=pltpu.CompilerParams(vmem_limit_bytes=66584576),
         cost_estimate=pl.CostEstimate(flops=2 * 10**9, bytes_accessed=5 * 10**6, transcendentals=0),
         name="analysis",
     )(length_1, ends, total_1, total_2, left_own, right_own)

time: 185 us -> 187 us (1.011)
  the two profiles are of different devices: /device:TPU:2 before, /device:TPU:1 now
where the time goes in v8:
time: 187 us; the launch traced here: 184 us
  blocking collectives  74.2 us (40%)
  Pallas kernels  37.9 us (20%)
  waiting for transfers between devices  29.5 us (16%)
  starting transfers between devices  26.6 us (14%)
  local copies, waits for them, and re-layouts  8.72 us (5%)
  matrix products  2.96 us (2%)
  other arithmetic  2.68 us (1%)
    all_to_all x2, blocking collectives, per_device(): mine = jnp.sum(lax.all_to_all(part, MEM, 0, 0, tiled=True), axis=0)  37.1 us
    pallas_call x2, Pallas kernels, sweep(): pl.pallas_call(functools.partial(sweep_kernel, first, scale, lon_tiles, m...  24.8 us
    all_to_all x1, blocking collectives, per_device(): lax.all_to_all(field.reshape(groups, piece_rows, LANES), MEM, 0, 0, tiled...  23.7 us
    all_to_all x3, starting transfers between devices, sent_to_all(): return lax.all_to_all(copies, axis, split_axis=0, concat_axis=0, tiled=True)  16.4 us
    all_to_all x1, waiting for transfers between devices, per_device(): known = lax.all_to_all(message, TILES, 0, 0, tiled=True)  15.2 us
    all_to_all x3, waiting for transfers between devices, sent_to_all(): return lax.all_to_all(copies, axis, split_axis=0, concat_axis=0, tiled=True)  14.2 us
    all_to_all x1, blocking collectives, sent_to_all(): return lax.all_to_all(copies, axis, split_axis=0, concat_axis=0, tiled=True)  13.4 us
    all_to_all x1, starting transfers between devices, per_device(): known = lax.all_to_all(message, TILES, 0, 0, tiled=True)  10.3 us
  transfers between devices with their start and end apart: 4, of which 4 were waited for; matrix products, arithmetic and copies ran while one was open for 3% of the time, Pallas kernels for 4%

profile of v8, /device:TPU:1, one launch (start us, length us, event | category | flops | bytes accessed | tf_op | source)
XLA Modules:
  0.0 184.1 jit_solution(1021429434669318114)
XLA Ops:
  1.3 0.0 copy-start.8
  1.3 6.1 %picked.1 = f32[16,80,128]{2,1,0:T(8,128)} custom-call(s32[1]{0:T(128)} %bitcast.17.count_ref, f32[2,384,512]{2,1,0:T(8,128)} %perturb_ref.3, s32[16,128]{1,0:T(8,128)} %bitcast.20, f32[16,128]{1,0:T(8,128)} %bitcast.21, f32[16,128]{1,0:T(8,128)} %bitcast.22), custom_call_target="tpu_custom_call" | custom-call | tf_op jit(solution)/shard_map/picked/pallas_call | solution.py:111
  7.3 10.3 %all-to-all-start = ((f32[16,80,128]{2,1,0:T(8,128)}), f32[16,80,128]{2,1,0:T(8,128)S(1)}, u32[]{:S(2)}, u32[]{:S(2)}) async-start(f32[16,80,128]{2,1,0:T(8,128)} %picked.1), calls=%async_computation | async-start | bytes 1310720 | tf_op jit(solution)/shard_map/all_to_all | solution.py:376
  17.6 0.0 copy-done.8
  17.6 0.1 power_select_fusion
  17.7 0.1 and_select_fusion
  17.8 2.0 %fusion.56 = (bf16[640,144]{0,1:T(8,128)(2,1)S(1)}, f32[640,144]{0,1:T(8,128)S(1)}) fusion(f32[512]{0:T(512)S(1)} %integer_pow.44, f32[144]{0:T(256)S(1)} %get-tuple-element.21, s32[144]{0:T(256)S(1)} %iota_add_fusion.2, f32[144]{0:T(256)S(1)} %get-tuple-element.20, f32[640]{0:T(1024)S(1)} %get-tuple-element.23, s32[640]{0:T(1024)S(1)} %iota_add_fusion, ...), kind=kOutput, calls=%fused_computation.79 | convolution fusion | flops 569133056 | bytes 564416 | tf_op jit(solution)/shard_map/ab,cb->ac/dot_general | solution.py:384
  19.8 0.0 copy-start.7
  19.9 0.2 copy.18.refs_4_.refs_5_
  20.0 0.2 copy.16
  20.3 0.2 copy-done.7
  20.5 0.1 and_select_fusion.1
  20.6 0.1 power_select_fusion.1
  20.7 1.0 fusion.55
  21.7 0.1 copy.17.refs_2_.refs_3_
  21.8 0.1 copy.14
  21.9 0.1 subtract_convert_fusion.refs_5_.refs_6_
  22.0 15.2 %all-to-all-done.refs_1_ = f32[16,80,128]{2,1,0:T(8,128)S(1)} async-done(((f32[16,80,128]{2,1,0:T(8,128)}), f32[16,80,128]{2,1,0:T(8,128)S(1)}, u32[]{:S(2)}, u32[]{:S(2)}) %all-to-all-start) | async-done | bytes 655392 | tf_op jit(solution)/shard_map/all_to_all | solution.py:376
  37.3 12.9 %sweep_first.1 = (f32[32,16,128]{2,1,0:T(8,128)S(1)}, f32[2,112,144]{2,1,0:T(8,128)}, f32[2,400,640]{2,1,0:T(8,128)}) custom-call(s32[1]{0:T(128)} %bitcast.refs_0_, f32[16,80,128]{2,1,0:T(8,128)S(1)} %all-to-all-done.refs_1_, bf16[112,400]{1,0:T(8,128)(2,1)S(1)} %copy.17.refs_2_.refs_3_, bf16[112,400]{1,0:T(8,128)(2,1)S(1)} %subtract_convert_fusion.1.refs_3_.refs_4_, ...), custom_call_target="tpu_custom_call" | custom-call | tf_op jit(solution)/shard_map/sweep_first/pallas_call | solution.py:279
  50.1 22.6 %all_to_all.40 = f32[32,16,128]{2,1,0:T(8,128)S(1)} all-to-all(f32[32,16,128]{2,1,0:T(8,128)S(1)} %get-tuple-element.10), channel_id=1, replica_groups=mesh['mem_0'=4,'mem_1'=8,'lat_0'=2,'lat_1'=2,'lon'=4] {'mem_0','mem_1'}, dimensions={0} | all-to-all | bytes 524288 | tf_op jit(solution)/shard_map/all_to_all | solution.py:390
  72.8 13.4 %all_to_all.41.refs_2_ = f32[16,16,128]{2,1,0:T(8,128)S(1)} all-to-all(f32[16,16,128]{2,1,0:T(8,128)S(1)} %broadcast_in_dim.14), channel_id=1, replica_groups=mesh['mem_0'=4,'mem_1'=8,'lat_0'=2,'lat_1'=2,'lon'=4] {'lat_0','lat_1','..., dimensions={0} | all-to-all | bytes 262144 | tf_op jit(solution)/shard_map/all_to_all | solution.py:30
  86.2 11.9 %sweep_second.1 = (f32[32,16,128]{2,1,0:T(8,128)S(1)}, f32[2,112,144]{2,1,0:T(8,128)}, f32[2,400,640]{2,1,0:T(8,128)}, f32[1,128]{1,0:T(1,128)S(1)}, f32[2,16,128]{2,1,0:T(8,128)S(1)}) custom-call(s32[1]{0:T(128)} %bitcast.refs_0_, f32[16,80,128]{2,1,0:T(8,128)S(1)} %all-to-all-done.refs_1_, f32[16,16,128]{2,1,0:T(8,128)S(1)} %all_to_all.41.refs_2_, ...), custom_call_target="tpu_custom_call" | custom-call | tf_op jit(solution)/shard_map/sweep_second/pallas_call | solution.py:279
  98.2 0.0 copy-start.6
  98.2 14.5 %all_to_all.42 = f32[32,16,128]{2,1,0:T(8,128)S(1)} all-to-all(f32[32,16,128]{2,1,0:T(8,128)S(1)} %get-tuple-element.12), channel_id=1, replica_groups=mesh['mem_0'=4,'mem_1'=8,'lat_0'=2,'lat_1'=2,'lon'=4] {'mem_0','mem_1'}, dimensions={0} | all-to-all | bytes 524288 | tf_op jit(solution)/shard_map/all_to_all | solution.py:395
  112.8 0.6 broadcast_in_dim.15
  113.4 5.2 %all-to-all-start.4 = ((f32[16,2,128]{2,1,0:T(2,128)}), f32[16,2,128]{2,1,0:T(2,128)S(1)}, u32[]{:S(2)}, u32[]{:S(2)}) async-start(f32[16,2,128]{2,1,0:T(2,128)} %broadcast_in_dim.15), calls=%async_computation.4 | async-start | bytes 32768 | tf_op jit(solution)/shard_map/all_to_all | solution.py:30
  118.7 0.9 copy-done.5
  119.6 1.7 fields.1.fields_ref
  121.3 0.0 copy-done.6
  121.3 0.0 copy-start.1
  121.3 1.2 copy-done.1
  122.5 3.5 %all-to-all-done.4.ends_ref = f32[16,2,128]{2,1,0:T(2,128)S(1)} async-done(((f32[16,2,128]{2,1,0:T(2,128)}), f32[16,2,128]{2,1,0:T(2,128)S(1)}, u32[]{:S(2)}, u32[]{:S(2)}) %all-to-all-start.4) | async-done | bytes 16416 | tf_op jit(solution)/shard_map/all_to_all | solution.py:30
  125.9 1.4 copy-done.2
  127.3 0.3 join.1
  127.6 23.7 %all_to_all.43 = f32[32,48,128]{2,1,0:T(8,128)S(1)} all-to-all(f32[32,48,128]{2,1,0:T(8,128)S(1)} %bitcast.18), channel_id=1, replica_groups=mesh['mem_0'=4,'mem_1'=8,'lat_0'=2,'lat_1'=2,'lon'=4] {'mem_0','mem_1'}, dimensions={0} | all-to-all | bytes 1572864 | tf_op jit(solution)/shard_map/all_to_all | solution.py:414
  151.3 0.1 reduce_sum.42
  151.4 0.7 broadcast_in_dim.16
  152.1 6.9 %all-to-all-start.6 = ((f32[8,48,128]{2,1,0:T(8,128)}), f32[8,48,128]{2,1,0:T(8,128)S(1)}, u32[]{:S(2)}, u32[]{:S(2)}) async-start(f32[8,48,128]{2,1,0:T(8,128)} %broadcast_in_dim.16), calls=%async_computation.6 | async-start | bytes 393216 | tf_op jit(solution)/shard_map/all_to_all | solution.py:30
  159.0 0.1 fusion.51
  159.1 0.8 fusion.31.left_ref
  160.0 7.8 %all-to-all-done.6 = f32[8,48,128]{2,1,0:T(8,128)S(1)} async-done(((f32[8,48,128]{2,1,0:T(8,128)}), f32[8,48,128]{2,1,0:T(8,128)S(1)}, u32[]{:S(2)}, u32[]{:S(2)}) %all-to-all-start.6) | async-done | bytes 196640 | tf_op jit(solution)/shard_map/all_to_all | solution.py:30
  167.8 0.9 broadcast_in_dim.17
  168.7 4.2 %all-to-all-start.7 = ((f32[4,384,128]{2,1,0:T(8,128)}), f32[4,384,128]{2,1,0:T(8,128)}, u32[]{:S(2)}, u32[]{:S(2)}) async-start(f32[4,384,128]{2,1,0:T(8,128)} %broadcast_in_dim.17), calls=%async_computation.7 | async-start | bytes 1572864 | tf_op jit(solution)/shard_map/all_to_all | solution.py:30
  172.9 0.1 fusion.52
  173.0 1.0 fusion.16.right_ref
  174.0 5.0 %analysis.1 = f32[2,96,128]{2,1,0:T(8,128)} custom-call(f32[1,128]{1,0:T(1,128)} %copy-done.6, f32[16,2,128]{2,1,0:T(2,128)} %copy-done.3, f32[2,400,640]{2,1,0:T(8,128)} %get-tuple-element.14.total_1_ref, f32[2,400,640]{2,1,0:T(8,128)} %get-tuple-element.15.total_2_ref, f32[96,400]{1,0:T(8,128)} %fusion.31.left_ref, f32[640,128]{1,0:T(8,128)} %fusion.16.right_ref), custom_call_target="tpu_custom_call" | custom-call | flops 2000000000 | bytes 5000000 | tf_op jit(solution)/shard_map/analysis/pallas_call | solution.py:418
  179.1 3.0 %all-to-all-done.7 = f32[4,384,128]{2,1,0:T(8,128)} async-done(((f32[4,384,128]{2,1,0:T(8,128)}), f32[4,384,128]{2,1,0:T(8,128)}, u32[]{:S(2)}, u32[]{:S(2)}) %all-to-all-start.7) | async-done | bytes 786464 | tf_op jit(solution)/shard_map/all_to_all | solution.py:30
  182.0 2.1 %copy.23 = f32[384,512]{1,0:T(8,128)} copy(f32[384,512]{1,0:T(8,128)} %bitcast.10) | data formatting | bytes 1572864
  (22 shorter events, 0.2 us)
Async XLA Ops:
  1.3 16.3 %copy-start.8 = (f32[512]{0:T(512)S(1)}, f32[512]{0:T(512)}, u32[]{:S(2)}) copy-start(f32[512]{0:T(512)} %param.9) | copy-start | bytes 6148
  7.3 29.9 %all-to-all-start = ((f32[16,80,128]{2,1,0:T(8,128)}), f32[16,80,128]{2,1,0:T(8,128)S(1)}, u32[]{:S(2)}, u32[]{:S(2)}) async-start(f32[16,80,128]{2,1,0:T(8,128)} %picked.1), calls=%async_computation | async-start | bytes 1310720 | tf_op jit(solution)/shard_map/all_to_all | solution.py:376
  19.8 0.7 copy-start.7
  86.2 32.4 %copy-start = (f32[2,384,512]{2,1,0:T(8,128)S(1)}, f32[2,384,512]{2,1,0:T(8,128)}, u32[]{:S(2)}) copy-start(f32[2,384,512]{2,1,0:T(8,128)} %perturb_ref.3) | copy-start | bytes 4718596
  86.2 32.4 %copy-start.4 = (f32[2,112,144]{2,1,0:T(8,128)S(1)}, f32[2,112,144]{2,1,0:T(8,128)}, u32[]{:S(2)}) copy-start(f32[2,112,144]{2,1,0:T(8,128)} %get-tuple-element.16.coarse_1_ref) | copy-start | bytes 387076
  98.2 23.1 %copy-start.6 = (f32[1,128]{1,0:T(1,128)}, f32[1,128]{1,0:T(1,128)S(1)}, u32[]{:S(2)}) copy-start(f32[1,128]{1,0:T(1,128)S(1)} %get-tuple-element.11.length_ref) | copy-start | bytes 1540
  113.4 12.6 %all-to-all-start.4 = ((f32[16,2,128]{2,1,0:T(2,128)}), f32[16,2,128]{2,1,0:T(2,128)S(1)}, u32[]{:S(2)}, u32[]{:S(2)}) async-start(f32[16,2,128]{2,1,0:T(2,128)} %broadcast_in_dim.15), calls=%async_computation.4 | async-start | bytes 32768 | tf_op jit(solution)/shard_map/all_to_all | solution.py:30
  118.6 0.9 copy-start.5
  121.3 1.2 copy-start.1
  125.9 1.4 copy-start.2
  127.3 24.0 %copy-start.3 = (f32[16,2,128]{2,1,0:T(2,128)}, f32[16,2,128]{2,1,0:T(2,128)S(1)}, u32[]{:S(2)}) copy-start(f32[16,2,128]{2,1,0:T(2,128)S(1)} %all-to-all-done.4.ends_ref) | copy-start | bytes 49156
  152.1 15.7 %all-to-all-start.6 = ((f32[8,48,128]{2,1,0:T(8,128)}), f32[8,48,128]{2,1,0:T(8,128)S(1)}, u32[]{:S(2)}, u32[]{:S(2)}) async-start(f32[8,48,128]{2,1,0:T(8,128)} %broadcast_in_dim.16), calls=%async_computation.6 | async-start | bytes 393216 | tf_op jit(solution)/shard_map/all_to_all | solution.py:30
  168.7 13.3 %all-to-all-start.7 = ((f32[4,384,128]{2,1,0:T(8,128)}), f32[4,384,128]{2,1,0:T(8,128)}, u32[]{:S(2)}, u32[]{:S(2)}) async-start(f32[4,384,128]{2,1,0:T(8,128)} %broadcast_in_dim.17), calls=%async_computation.7 | async-start | bytes 1572864 | tf_op jit(solution)/shard_map/all_to_all | solution.py:30

commit v9 on v8

--- a/solution.py
+++ b/solution.py
@@ -420,7 +420,7 @@
         out_shape=jax.ShapeDtypeStruct((members, coarse_lat, coarse_lon), f32),
         in_specs=[whole] * 6,
         out_specs=whole,
-        compiler_params=pltpu.CompilerParams(vmem_limit_bytes=66584576),
+        compiler_params=pltpu.CompilerParams(vmem_limit_bytes=24 * 1024 * 1024),
         cost_estimate=pl.CostEstimate(flops=2 * 10**9, bytes_accessed=5 * 10**6, transcendentals=0),
         name="analysis",
     )(length_1, ends, total_1, total_2, left_own, right_own)

time: 187 us -> 185 us (0.989)
  Pallas kernels: 37.9 us -> 35.7 us
  waiting for transfers between devices: 29.5 us -> 31.4 us
    pallas_call x1, Pallas kernels: 5.03 us -> 2.81 us  [per_device(): pl.pallas_call(analysis_kernel, out_shape=jax.ShapeDtypeStruct((members,...]
    all_to_all x3, waiting for transfers between devices: 14.2 us -> 16.2 us  [sent_to_all(): return lax.all_to_all(copies, axis, split_axis=0, concat_axis=0, tiled=True)]
  transfers between devices with their start and end apart: 4 -> 4, of which waited for: 4 -> 4; matrix products, arithmetic and copies ran while one was open for 3% -> 3% of each run, Pallas kernels for 4% -> 2%
where the time goes in v9:
time: 185 us; the launch traced here: 182 us
  blocking collectives  74.3 us (40%)
  Pallas kernels  35.7 us (19%)
  waiting for transfers between devices  31.4 us (17%)
  starting transfers between devices  25.9 us (14%)
  local copies, waits for them, and re-layouts  9.1 us (5%)
  matrix products  2.98 us (2%)
    all_to_all x2, blocking collectives, per_device(): mine = jnp.sum(lax.all_to_all(part, MEM, 0, 0, tiled=True), axis=0)  37.2 us
    pallas_call x2, Pallas kernels, sweep(): pl.pallas_call(functools.partial(sweep_kernel, first, scale, lon_tiles, m...  24.9 us
    all_to_all x1, blocking collectives, per_device(): lax.all_to_all(field.reshape(groups, piece_rows, LANES), MEM, 0, 0, tiled...  23.7 us
    all_to_all x3, waiting for transfers between devices, sent_to_all(): return lax.all_to_all(copies, axis, split_axis=0, concat_axis=0, tiled=True)  16.2 us
    all_to_all x3, starting transfers between devices, sent_to_all(): return lax.all_to_all(copies, axis, split_axis=0, concat_axis=0, tiled=True)  15.6 us
    all_to_all x1, waiting for transfers between devices, per_device(): known = lax.all_to_all(message, TILES, 0, 0, tiled=True)  15.2 us
    all_to_all x1, blocking collectives, sent_to_all(): return lax.all_to_all(copies, axis, split_axis=0, concat_axis=0, tiled=True)  13.4 us
    all_to_all x1, starting transfers between devices, per_device(): known = lax.all_to_all(message, TILES, 0, 0, tiled=True)  10.3 us
  transfers between devices with their start and end apart: 4, of which 4 were waited for; matrix products, arithmetic and copies ran while one was open for 3% of the time, Pallas kernels for 2%

profile of v9, /device:TPU:1, one launch (start us, length us, event | category | flops | bytes accessed | tf_op | source)
XLA Modules:
  0.0 182.2 jit_solution(15435476503877657839)
XLA Ops:
  1.3 0.0 copy-start.8
  1.3 6.1 %picked.1 = f32[16,80,128]{2,1,0:T(8,128)} custom-call(s32[1]{0:T(128)} %bitcast.17.count_ref, f32[2,384,512]{2,1,0:T(8,128)} %perturb_ref.3, s32[16,128]{1,0:T(8,128)} %bitcast.21, f32[16,128]{1,0:T(8,128)} %bitcast.22, f32[16,128]{1,0:T(8,128)} %bitcast.23), custom_call_target="tpu_custom_call" | custom-call | tf_op jit(solution)/shard_map/picked/pallas_call | solution.py:111
  7.3 10.3 %all-to-all-start = ((f32[16,80,128]{2,1,0:T(8,128)}), f32[16,80,128]{2,1,0:T(8,128)S(1)}, u32[]{:S(2)}, u32[]{:S(2)}) async-start(f32[16,80,128]{2,1,0:T(8,128)} %picked.1), calls=%async_computation | async-start | bytes 1310720 | tf_op jit(solution)/shard_map/all_to_all | solution.py:376
  17.6 0.0 copy-done.8
  17.6 0.1 power_select_fusion
  17.7 0.1 and_select_fusion
  17.8 2.0 %fusion.56 = (bf16[640,144]{0,1:T(8,128)(2,1)S(1)}, f32[640,144]{0,1:T(8,128)S(1)}) fusion(f32[512]{0:T(512)S(1)} %integer_pow.44, f32[144]{0:T(256)S(1)} %get-tuple-element.21, s32[144]{0:T(256)S(1)} %iota_add_fusion.2, f32[144]{0:T(256)S(1)} %get-tuple-element.20, f32[640]{0:T(1024)S(1)} %get-tuple-element.23, s32[640]{0:T(1024)S(1)} %iota_add_fusion, ...), kind=kOutput, calls=%fused_computation.79 | convolution fusion | flops 569133056 | bytes 564416 | tf_op jit(solution)/shard_map/ab,cb->ac/dot_general | solution.py:384
  19.8 0.0 copy-start.7
  19.9 0.2 copy.18.refs_4_.refs_5_
  20.0 0.2 copy.16
  20.3 0.2 copy-done.7
  20.5 0.1 and_select_fusion.1
  20.6 0.1 power_select_fusion.1
  20.7 1.0 fusion.55
  21.7 0.1 copy.17.refs_2_.refs_3_
  21.8 0.1 copy.14
  22.0 0.1 subtract_convert_fusion.refs_5_.refs_6_
  22.0 15.2 %all-to-all-done.refs_1_ = f32[16,80,128]{2,1,0:T(8,128)S(1)} async-done(((f32[16,80,128]{2,1,0:T(8,128)}), f32[16,80,128]{2,1,0:T(8,128)S(1)}, u32[]{:S(2)}, u32[]{:S(2)}) %all-to-all-start) | async-done | bytes 655392 | tf_op jit(solution)/shard_map/all_to_all | solution.py:376
  37.3 12.9 %sweep_first.1 = (f32[32,16,128]{2,1,0:T(8,128)S(1)}, f32[2,112,144]{2,1,0:T(8,128)}, f32[2,400,640]{2,1,0:T(8,128)}) custom-call(s32[1]{0:T(128)} %bitcast.refs_0_, f32[16,80,128]{2,1,0:T(8,128)S(1)} %all-to-all-done.refs_1_, bf16[112,400]{1,0:T(8,128)(2,1)S(1)} %copy.17.refs_2_.refs_3_, bf16[112,400]{1,0:T(8,128)(2,1)S(1)} %subtract_convert_fusion.1.refs_3_.refs_4_, ...), custom_call_target="tpu_custom_call" | custom-call | tf_op jit(solution)/shard_map/sweep_first/pallas_call | solution.py:279
  50.1 22.6 %all_to_all.40 = f32[32,16,128]{2,1,0:T(8,128)S(1)} all-to-all(f32[32,16,128]{2,1,0:T(8,128)S(1)} %get-tuple-element.10), channel_id=1, replica_groups=mesh['mem_0'=4,'mem_1'=8,'lat_0'=2,'lat_1'=2,'lon'=4] {'mem_0','mem_1'}, dimensions={0} | all-to-all | bytes 524288 | tf_op jit(solution)/shard_map/all_to_all | solution.py:390
  72.8 13.4 %all_to_all.41.refs_2_ = f32[16,16,128]{2,1,0:T(8,128)S(1)} all-to-all(f32[16,16,128]{2,1,0:T(8,128)S(1)} %broadcast_in_dim.14), channel_id=1, replica_groups=mesh['mem_0'=4,'mem_1'=8,'lat_0'=2,'lat_1'=2,'lon'=4] {'lat_0','lat_1','..., dimensions={0} | all-to-all | bytes 262144 | tf_op jit(solution)/shard_map/all_to_all | solution.py:30
  86.2 12.0 %sweep_second.1 = (f32[32,16,128]{2,1,0:T(8,128)S(1)}, f32[2,112,144]{2,1,0:T(8,128)}, f32[2,400,640]{2,1,0:T(8,128)}, f32[1,128]{1,0:T(1,128)S(1)}, f32[2,16,128]{2,1,0:T(8,128)S(1)}) custom-call(s32[1]{0:T(128)} %bitcast.refs_0_, f32[16,80,128]{2,1,0:T(8,128)S(1)} %all-to-all-done.refs_1_, f32[16,16,128]{2,1,0:T(8,128)S(1)} %all_to_all.41.refs_2_, ...), custom_call_target="tpu_custom_call" | custom-call | tf_op jit(solution)/shard_map/sweep_second/pallas_call | solution.py:279
  98.2 14.6 %all_to_all.42 = f32[32,16,128]{2,1,0:T(8,128)S(1)} all-to-all(f32[32,16,128]{2,1,0:T(8,128)S(1)} %get-tuple-element.12), channel_id=1, replica_groups=mesh['mem_0'=4,'mem_1'=8,'lat_0'=2,'lat_1'=2,'lon'=4] {'mem_0','mem_1'}, dimensions={0} | all-to-all | bytes 524288 | tf_op jit(solution)/shard_map/all_to_all | solution.py:395
  112.9 0.6 broadcast_in_dim.15
  113.5 5.2 %all-to-all-start.4 = ((f32[16,2,128]{2,1,0:T(2,128)}), f32[16,2,128]{2,1,0:T(2,128)S(1)}, u32[]{:S(2)}, u32[]{:S(2)}) async-start(f32[16,2,128]{2,1,0:T(2,128)} %broadcast_in_dim.15), calls=%async_computation.4 | async-start | bytes 32768 | tf_op jit(solution)/shard_map/all_to_all | solution.py:30
  118.7 0.9 copy-done.6
  119.6 1.7 fields.1.fields_ref
  121.3 1.2 copy-done.1
  122.5 3.5 %all-to-all-done.4.ends_ref = f32[16,2,128]{2,1,0:T(2,128)S(1)} async-done(((f32[16,2,128]{2,1,0:T(2,128)}), f32[16,2,128]{2,1,0:T(2,128)S(1)}, u32[]{:S(2)}, u32[]{:S(2)}) %all-to-all-start.4) | async-done | bytes 16416 | tf_op jit(solution)/shard_map/all_to_all | solution.py:30
  126.0 1.4 copy-done.2
  127.4 0.3 join.1
  127.7 23.7 %all_to_all.43 = f32[32,48,128]{2,1,0:T(8,128)S(1)} all-to-all(f32[32,48,128]{2,1,0:T(8,128)S(1)} %bitcast.18), channel_id=1, replica_groups=mesh['mem_0'=4,'mem_1'=8,'lat_0'=2,'lat_1'=2,'lon'=4] {'mem_0','mem_1'}, dimensions={0} | all-to-all | bytes 1572864 | tf_op jit(solution)/shard_map/all_to_all | solution.py:414
  151.4 0.1 reduce_sum.42
  151.5 0.7 broadcast_in_dim.16
  152.1 6.9 %all-to-all-start.6 = ((f32[8,48,128]{2,1,0:T(8,128)}), f32[8,48,128]{2,1,0:T(8,128)S(1)}, u32[]{:S(2)}, u32[]{:S(2)}) async-start(f32[8,48,128]{2,1,0:T(8,128)} %broadcast_in_dim.16), calls=%async_computation.6 | async-start | bytes 393216 | tf_op jit(solution)/shard_map/all_to_all | solution.py:30
  159.1 0.1 fusion.51
  159.2 0.1 fusion.31.left_ref
  159.3 8.5 %all-to-all-done.6 = f32[8,48,128]{2,1,0:T(8,128)S(1)} async-done(((f32[8,48,128]{2,1,0:T(8,128)}), f32[8,48,128]{2,1,0:T(8,128)S(1)}, u32[]{:S(2)}, u32[]{:S(2)}) %all-to-all-start.6) | async-done | bytes 196640 | tf_op jit(solution)/shard_map/all_to_all | solution.py:30
  167.8 0.9 broadcast_in_dim.17
  168.8 3.5 %all-to-all-start.7 = ((f32[4,384,128]{2,1,0:T(8,128)}), f32[4,384,128]{2,1,0:T(8,128)S(1)}, u32[]{:S(2)}, u32[]{:S(2)}) async-start(f32[4,384,128]{2,1,0:T(8,128)} %broadcast_in_dim.17), calls=%async_computation.7 | async-start | bytes 1572864 | tf_op jit(solution)/shard_map/all_to_all | solution.py:30
  172.3 0.1 fusion.52
  172.4 0.3 fusion.16.right_ref
  172.7 0.0 copy-done.3
  172.7 0.0 copy-start.4
  172.7 1.6 copy-done.4
  174.3 2.8 %analysis.1 = f32[2,96,128]{2,1,0:T(8,128)} custom-call(f32[1,128]{1,0:T(1,128)S(1)} %get-tuple-element.11.length_ref, f32[16,2,128]{2,1,0:T(2,128)S(1)} %all-to-all-done.4.ends_ref, f32[2,400,640]{2,1,0:T(8,128)S(1)} %copy-done.3, f32[2,400,640]{2,1,0:T(8,128)S(1)} %copy-done.4, f32[96,400]{1,0:T(8,128)S(1)} %fusion.31.left_ref, ...), custom_call_target="tpu_custom_call" | custom-call | flops 2000000000 | bytes 5000000 | tf_op jit(solution)/shard_map/analysis/pallas_call | solution.py:418
  177.1 4.2 %all-to-all-done.7 = f32[4,384,128]{2,1,0:T(8,128)S(1)} async-done(((f32[4,384,128]{2,1,0:T(8,128)}), f32[4,384,128]{2,1,0:T(8,128)S(1)}, u32[]{:S(2)}, u32[]{:S(2)}) %all-to-all-start.7) | async-done | bytes 786464 | tf_op jit(solution)/shard_map/all_to_all | solution.py:30
  181.3 0.9 copy.23
  (22 shorter events, 0.2 us)
Async XLA Ops:
  1.3 16.3 %copy-start.8 = (f32[512]{0:T(512)S(1)}, f32[512]{0:T(512)}, u32[]{:S(2)}) copy-start(f32[512]{0:T(512)} %param.9) | copy-start | bytes 6148
  7.3 29.9 %all-to-all-start = ((f32[16,80,128]{2,1,0:T(8,128)}), f32[16,80,128]{2,1,0:T(8,128)S(1)}, u32[]{:S(2)}, u32[]{:S(2)}) async-start(f32[16,80,128]{2,1,0:T(8,128)} %picked.1), calls=%async_computation | async-start | bytes 1310720 | tf_op jit(solution)/shard_map/all_to_all | solution.py:376
  19.8 0.7 copy-start.7
  86.2 32.4 %copy-start = (f32[2,384,512]{2,1,0:T(8,128)S(1)}, f32[2,384,512]{2,1,0:T(8,128)}, u32[]{:S(2)}) copy-start(f32[2,384,512]{2,1,0:T(8,128)} %perturb_ref.3) | copy-start | bytes 4718596
  86.2 32.4 %copy-start.5 = (f32[2,112,144]{2,1,0:T(8,128)S(1)}, f32[2,112,144]{2,1,0:T(8,128)}, u32[]{:S(2)}) copy-start(f32[2,112,144]{2,1,0:T(8,128)} %get-tuple-element.16.coarse_1_ref) | copy-start | bytes 387076
  113.5 12.5 %all-to-all-start.4 = ((f32[16,2,128]{2,1,0:T(2,128)}), f32[16,2,128]{2,1,0:T(2,128)S(1)}, u32[]{:S(2)}, u32[]{:S(2)}) async-start(f32[16,2,128]{2,1,0:T(2,128)} %broadcast_in_dim.15), calls=%async_computation.4 | async-start | bytes 32768 | tf_op jit(solution)/shard_map/all_to_all | solution.py:30
  118.7 0.9 copy-start.6
  121.3 1.2 copy-start.1
  125.9 1.4 copy-start.2
  152.1 15.7 %all-to-all-start.6 = ((f32[8,48,128]{2,1,0:T(8,128)}), f32[8,48,128]{2,1,0:T(8,128)S(1)}, u32[]{:S(2)}, u32[]{:S(2)}) async-start(f32[8,48,128]{2,1,0:T(8,128)} %broadcast_in_dim.16), calls=%async_computation.6 | async-start | bytes 393216 | tf_op jit(solution)/shard_map/all_to_all | solution.py:30
  167.8 4.9 %copy-start.3 = (f32[2,400,640]{2,1,0:T(8,128)S(1)}, f32[2,400,640]{2,1,0:T(8,128)}, u32[]{:S(2)}) copy-start(f32[2,400,640]{2,1,0:T(8,128)} %get-tuple-element.14.total_1_ref) | copy-start | bytes 6144004
  168.8 12.5 %all-to-all-start.7 = ((f32[4,384,128]{2,1,0:T(8,128)}), f32[4,384,128]{2,1,0:T(8,128)S(1)}, u32[]{:S(2)}, u32[]{:S(2)}) async-start(f32[4,384,128]{2,1,0:T(8,128)} %broadcast_in_dim.17), calls=%async_computation.7 | async-start | bytes 1572864 | tf_op jit(solution)/shard_map/all_to_all | solution.py:30
  172.7 1.6 copy-start.4

commit v10 on v9

--- a/solution.py
+++ b/solution.py
@@ -333,6 +333,22 @@
     out_ref[...] = fields_ref[0] + ends_length(ends_ref) * fields_ref[1]
 
 
+def join(ends, fields):
+    _, parts, rows, lanes = fields.shape
+    return pl.pallas_call(
+        join_kernel,
+        grid=(parts,),
+        out_shape=jax.ShapeDtypeStruct((parts, rows, lanes), f32),
+        in_specs=[
+            pl.BlockSpec(memory_space=pltpu.VMEM),
+            pl.BlockSpec((2, 1, rows, lanes), lambda n: (0, n, 0, 0)),
+        ],
+        out_specs=pl.BlockSpec((1, rows, lanes), lambda n: (n, 0, 0)),
+        compiler_params=pltpu.CompilerParams(vmem_limit_bytes=60 * 1024 * 1024),
+        name="join",
+    )(ends, fields)
+
+
 def analysis_kernel(length_ref, ends_ref, total_1_ref, total_2_ref, left_ref, right_ref, out_ref):
     one = length_ref[0, 0]
     two = ends_length(ends_ref)
@@ -394,8 +410,6 @@
     )
     mine = jnp.sum(lax.all_to_all(part, MEM, 0, 0, tiled=True), axis=0)
     bent = jnp.sum(jnp.stack([(mine * own[0]) ** 2, mine * own[1]]), axis=1)
-    ends = sent_to_all(bent, TILES)
-
     field_rows = fine_lat * fine_lon // LANES
     along_x = lax.axis_size(X)
     part_rows, piece_rows = field_rows // along_x, field_rows // groups
@@ -410,7 +424,10 @@
         coarse_1,
         coarse_2,
     )
-    field = small_call(join_kernel, (part,), 10**6, "join", ends, fields)
+    bent, fields = lax.optimization_barrier((bent, fields))
+    ends = sent_to_all(bent, TILES)
+
+    field = join(ends, fields)
     field = lax.all_to_all(field.reshape(groups, piece_rows, LANES), MEM, 0, 0, tiled=True)
     field = jnp.sum(field, axis=0)
     everything = sent_to_all(sent_to_all(field, Z).reshape(part_rows, LANES), X)

time: 185 us -> 187 us (1.011)
  Pallas kernels: 35.7 us -> 39.9 us
  waiting for transfers between devices: 31.4 us -> 34.7 us
  blocking collectives: 74.3 us -> 72.2 us
  local copies, waits for them, and re-layouts: 9.1 us -> 7.09 us
    all_to_all x2 -> x1, blocking collectives: 37.2 us -> 22.6 us  [per_device(): mine = jnp.sum(lax.all_to_all(part, MEM, 0, 0, tiled=True), axis=0)]
    all_to_all x1 -> x2, blocking collectives: 13.4 us -> 25.7 us  [sent_to_all(): return lax.all_to_all(copies, axis, split_axis=0, concat_axis=0, tiled=True)]
    all_to_all x0 -> x1, waiting for transfers between devices: none -> 6.83 us  [per_device(): mine = jnp.sum(lax.all_to_all(part, MEM, 0, 0, tiled=True), axis=0)]
    all_to_all x3 -> x2, starting transfers between devices: 15.6 us -> 10.4 us  [sent_to_all(): return lax.all_to_all(copies, axis, split_axis=0, concat_axis=0, tiled=True)]
    all_to_all x0 -> x1, starting transfers between devices: none -> 4.22 us  [per_device(): mine = jnp.sum(lax.all_to_all(part, MEM, 0, 0, tiled=True), axis=0)]
    pallas_call x0 -> x1, Pallas kernels: none -> 3.76 us  [join(): pl.pallas_call(join_kernel, grid=(parts,), out_shape=jax.ShapeDtypeStruct...]
    all_to_all x3 -> x2, waiting for transfers between devices: 16.2 us -> 12.7 us  [sent_to_all(): return lax.all_to_all(copies, axis, split_axis=0, concat_axis=0, tiled=True)]
where the time goes in v10:
time: 187 us; the launch traced here: 185 us
  blocking collectives  72.2 us (39%)
  Pallas kernels  39.9 us (21%)
  waiting for transfers between devices  34.7 us (19%)
  starting transfers between devices  24.9 us (13%)
  local copies, waits for them, and re-layouts  7.09 us (4%)
  matrix products  2.98 us (2%)
    all_to_all x2, blocking collectives, sent_to_all(): return lax.all_to_all(copies, axis, split_axis=0, concat_axis=0, tiled=True)  25.7 us
    pallas_call x2, Pallas kernels, sweep(): pl.pallas_call(functools.partial(sweep_kernel, first, scale, lon_tiles, m...  25.6 us
    all_to_all x1, blocking collectives, per_device(): lax.all_to_all(field.reshape(groups, piece_rows, LANES), MEM, 0, 0, tiled...  23.9 us
    all_to_all x1, blocking collectives, per_device(): mine = jnp.sum(lax.all_to_all(part, MEM, 0, 0, tiled=True), axis=0)  22.6 us
    all_to_all x1, waiting for transfers between devices, per_device(): known = lax.all_to_all(message, TILES, 0, 0, tiled=True)  15.2 us
    all_to_all x2, waiting for transfers between devices, sent_to_all(): return lax.all_to_all(copies, axis, split_axis=0, concat_axis=0, tiled=True)  12.7 us
    all_to_all x2, starting transfers between devices, sent_to_all(): return lax.all_to_all(copies, axis, split_axis=0, concat_axis=0, tiled=True)  10.4 us
    all_to_all x1, starting transfers between devices, per_device(): known = lax.all_to_all(message, TILES, 0, 0, tiled=True)  10.3 us
  transfers between devices with their start and end apart: 4, of which 4 were waited for; matrix products, arithmetic and copies ran while one was open for 3% of the time, Pallas kernels for 2%

profile of v10, /device:TPU:1, one launch (start us, length us, event | category | flops | bytes accessed | tf_op | source)
XLA Modules:
  0.0 184.7 jit_solution(11187787901260035950)
XLA Ops:
  1.3 0.0 copy-start.8
  1.3 6.1 %picked.1 = f32[16,80,128]{2,1,0:T(8,128)} custom-call(s32[1]{0:T(128)} %bitcast.17.count_ref, f32[2,384,512]{2,1,0:T(8,128)} %perturb_ref.3, s32[16,128]{1,0:T(8,128)} %bitcast.21, f32[16,128]{1,0:T(8,128)} %bitcast.22, f32[16,128]{1,0:T(8,128)} %bitcast.23), custom_call_target="tpu_custom_call" | custom-call | tf_op jit(solution)/shard_map/picked/pallas_call | solution.py:111
  7.3 10.3 %all-to-all-start = ((f32[16,80,128]{2,1,0:T(8,128)}), f32[16,80,128]{2,1,0:T(8,128)S(1)}, u32[]{:S(2)}, u32[]{:S(2)}) async-start(f32[16,80,128]{2,1,0:T(8,128)} %picked.1), calls=%async_computation | async-start | bytes 1310720 | tf_op jit(solution)/shard_map/all_to_all | solution.py:392
  17.6 0.0 copy-done.8
  17.6 0.1 power_select_fusion
  17.7 0.1 and_select_fusion
  17.8 2.0 %fusion.56 = (bf16[640,144]{0,1:T(8,128)(2,1)S(1)}, f32[640,144]{0,1:T(8,128)S(1)}) fusion(f32[512]{0:T(512)S(1)} %integer_pow.44, f32[144]{0:T(256)S(1)} %get-tuple-element.25, s32[144]{0:T(256)S(1)} %iota_add_fusion.2, f32[144]{0:T(256)S(1)} %get-tuple-element.24, f32[640]{0:T(1024)S(1)} %get-tuple-element.27, s32[640]{0:T(1024)S(1)} %iota_add_fusion, ...), kind=kOutput, calls=%fused_computation.79 | convolution fusion | flops 569133056 | bytes 564416 | tf_op jit(solution)/shard_map/ab,cb->ac/dot_general | solution.py:400
  19.8 0.0 copy-start.7
  19.9 0.2 copy.18.refs_4_.refs_5_
  20.0 0.2 copy.16
  20.3 0.2 copy-done.7
  20.5 0.1 and_select_fusion.1
  20.6 0.1 power_select_fusion.1
  20.7 1.0 fusion.55
  21.7 0.1 copy.17.refs_2_.refs_3_
  21.8 0.1 copy.14
  22.0 0.1 subtract_convert_fusion.refs_5_.refs_6_
  22.0 15.2 %all-to-all-done.refs_1_ = f32[16,80,128]{2,1,0:T(8,128)S(1)} async-done(((f32[16,80,128]{2,1,0:T(8,128)}), f32[16,80,128]{2,1,0:T(8,128)S(1)}, u32[]{:S(2)}, u32[]{:S(2)}) %all-to-all-start) | async-done | bytes 655392 | tf_op jit(solution)/shard_map/all_to_all | solution.py:392
  37.3 12.9 %sweep_first.1 = (f32[32,16,128]{2,1,0:T(8,128)S(1)}, f32[2,112,144]{2,1,0:T(8,128)}, f32[2,400,640]{2,1,0:T(8,128)}) custom-call(s32[1]{0:T(128)} %bitcast.refs_0_, f32[16,80,128]{2,1,0:T(8,128)S(1)} %all-to-all-done.refs_1_, bf16[112,400]{1,0:T(8,128)(2,1)S(1)} %copy.17.refs_2_.refs_3_, bf16[112,400]{1,0:T(8,128)(2,1)S(1)} %subtract_convert_fusion.1.refs_3_.refs_4_, ...), custom_call_target="tpu_custom_call" | custom-call | tf_op jit(solution)/shard_map/sweep_first/pallas_call | solution.py:279
  50.2 22.6 %all_to_all.40 = f32[32,16,128]{2,1,0:T(8,128)S(1)} all-to-all(f32[32,16,128]{2,1,0:T(8,128)S(1)} %get-tuple-element.12), channel_id=1, replica_groups=mesh['mem_0'=4,'mem_1'=8,'lat_0'=2,'lat_1'=2,'lon'=4] {'mem_0','mem_1'}, dimensions={0} | all-to-all | bytes 524288 | tf_op jit(solution)/shard_map/all_to_all | solution.py:406
  72.8 0.0 copy-start
  72.8 0.0 copy-start.5
  72.9 13.6 %all_to_all.41.refs_2_ = f32[16,16,128]{2,1,0:T(8,128)S(1)} all-to-all(f32[16,16,128]{2,1,0:T(8,128)S(1)} %broadcast_in_dim.14), channel_id=1, replica_groups=mesh['mem_0'=4,'mem_1'=8,'lat_0'=2,'lat_1'=2,'lon'=4] {'lat_0','lat_1','..., dimensions={0} | all-to-all | bytes 262144 | tf_op jit(solution)/shard_map/all_to_all | solution.py:30
  86.4 12.7 %sweep_second.1 = (f32[32,16,128]{2,1,0:T(8,128)}, f32[2,112,144]{2,1,0:T(8,128)}, f32[2,400,640]{2,1,0:T(8,128)}, f32[1,128]{1,0:T(1,128)S(1)}, f32[2,16,128]{2,1,0:T(8,128)S(1)}) custom-call(s32[1]{0:T(128)} %bitcast.refs_0_, f32[16,80,128]{2,1,0:T(8,128)S(1)} %all-to-all-done.refs_1_, f32[16,16,128]{2,1,0:T(8,128)S(1)} %all_to_all.41.refs_2_, ...), custom_call_target="tpu_custom_call" | custom-call | tf_op jit(solution)/shard_map/sweep_second/pallas_call | solution.py:279
  99.1 4.2 %all-to-all-start.3 = ((f32[32,16,128]{2,1,0:T(8,128)}), f32[32,16,128]{2,1,0:T(8,128)S(1)}, u32[]{:S(2)}, u32[]{:S(2)}) async-start(f32[32,16,128]{2,1,0:T(8,128)} %get-tuple-element.14), calls=%async_computation.3 | async-start | bytes 524288 | tf_op jit(solution)/shard_map/all_to_all | solution.py:411
  103.3 0.0 copy-done
  103.4 0.0 copy-done.5
  103.4 0.9 copy-done.6
  104.3 1.7 fields.1.fields_ref
  106.0 1.2 copy-done.1
  107.2 6.8 %all-to-all-done.3 = f32[32,16,128]{2,1,0:T(8,128)S(1)} async-done(((f32[32,16,128]{2,1,0:T(8,128)}), f32[32,16,128]{2,1,0:T(8,128)S(1)}, u32[]{:S(2)}, u32[]{:S(2)}) %all-to-all-start.3) | async-done | bytes 262176 | tf_op jit(solution)/shard_map/all_to_all | solution.py:411
  114.1 12.1 %all_to_all.42.ends_ref = f32[16,2,128]{2,1,0:T(2,128)} all-to-all(f32[16,2,128]{2,1,0:T(2,128)S(1)} %broadcast_in_dim.15), channel_id=1, replica_groups=mesh['mem_0'=4,'mem_1'=8,'lat_0'=2,'lat_1'=2,'lon'=4] {'lat_0','lat_1','..., dimensions={0} | all-to-all | bytes 32768 | tf_op jit(solution)/shard_map/all_to_all | solution.py:30
  126.2 3.8 %join.1 = f32[4,384,128]{2,1,0:T(8,128)} custom-call(f32[16,2,128]{2,1,0:T(2,128)} %all_to_all.42.ends_ref, f32[2,4,384,128]{3,2,1,0:T(8,128)} %copy-done.1), custom_call_target="tpu_custom_call" | custom-call | tf_op jit(solution)/shard_map/join/pallas_call | solution.py:338
  129.9 23.9 %all_to_all.43 = f32[32,48,128]{2,1,0:T(8,128)S(1)} all-to-all(f32[32,48,128]{2,1,0:T(8,128)} %bitcast.19), channel_id=1, replica_groups=mesh['mem_0'=4,'mem_1'=8,'lat_0'=2,'lat_1'=2,'lon'=4] {'mem_0','mem_1'}, dimensions={0} | all-to-all | bytes 1572864 | tf_op jit(solution)/shard_map/all_to_all | solution.py:431
  153.9 0.1 reduce_sum.42
  153.9 0.7 broadcast_in_dim.16
  154.6 6.9 %all-to-all-start.6 = ((f32[8,48,128]{2,1,0:T(8,128)}), f32[8,48,128]{2,1,0:T(8,128)S(1)}, u32[]{:S(2)}, u32[]{:S(2)}) async-start(f32[8,48,128]{2,1,0:T(8,128)} %broadcast_in_dim.16), calls=%async_computation.6 | async-start | bytes 393216 | tf_op jit(solution)/shard_map/all_to_all | solution.py:30
  161.6 0.1 fusion.51
  161.7 0.1 fusion.31.left_ref
  161.8 8.5 %all-to-all-done.6 = f32[8,48,128]{2,1,0:T(8,128)S(1)} async-done(((f32[8,48,128]{2,1,0:T(8,128)}), f32[8,48,128]{2,1,0:T(8,128)S(1)}, u32[]{:S(2)}, u32[]{:S(2)}) %all-to-all-start.6) | async-done | bytes 196640 | tf_op jit(solution)/shard_map/all_to_all | solution.py:30
  170.3 0.9 broadcast_in_dim.17
  171.3 3.5 %all-to-all-start.7 = ((f32[4,384,128]{2,1,0:T(8,128)}), f32[4,384,128]{2,1,0:T(8,128)S(1)}, u32[]{:S(2)}, u32[]{:S(2)}) async-start(f32[4,384,128]{2,1,0:T(8,128)} %broadcast_in_dim.17), calls=%async_computation.7 | async-start | bytes 1572864 | tf_op jit(solution)/shard_map/all_to_all | solution.py:30
  174.8 0.1 fusion.52
  174.9 0.3 fusion.16.right_ref
  175.2 1.6 copy-done.4
  176.8 2.8 %analysis.1 = f32[2,96,128]{2,1,0:T(8,128)} custom-call(f32[1,128]{1,0:T(1,128)S(1)} %get-tuple-element.13.length_ref, f32[16,2,128]{2,1,0:T(2,128)S(1)} %copy-done.2, f32[2,400,640]{2,1,0:T(8,128)S(1)} %copy-done.3, f32[2,400,640]{2,1,0:T(8,128)S(1)} %copy-done.4, f32[96,400]{1,0:T(8,128)S(1)} %fusion.31.left_ref, f32[640,128]{1,0:T(8,128)S(1)} %fusion.16.right_ref), custom_call_target="tpu_custom_call" | custom-call | flops 2000000000 | bytes 5000000 | tf_op jit(solution)/shard_map/analysis/pallas_call | solution.py:435
  179.6 4.2 %all-to-all-done.7 = f32[4,384,128]{2,1,0:T(8,128)S(1)} async-done(((f32[4,384,128]{2,1,0:T(8,128)}), f32[4,384,128]{2,1,0:T(8,128)S(1)}, u32[]{:S(2)}, u32[]{:S(2)}) %all-to-all-start.7) | async-done | bytes 786464 | tf_op jit(solution)/shard_map/all_to_all | solution.py:30
  183.8 0.9 copy.23
  (22 shorter events, 0.2 us)
Async XLA Ops:
  1.3 16.3 %copy-start.8 = (f32[512]{0:T(512)S(1)}, f32[512]{0:T(512)}, u32[]{:S(2)}) copy-start(f32[512]{0:T(512)} %param.9) | copy-start | bytes 6148
  7.3 29.9 %all-to-all-start = ((f32[16,80,128]{2,1,0:T(8,128)}), f32[16,80,128]{2,1,0:T(8,128)S(1)}, u32[]{:S(2)}, u32[]{:S(2)}) async-start(f32[16,80,128]{2,1,0:T(8,128)} %picked.1), calls=%async_computation | async-start | bytes 1310720 | tf_op jit(solution)/shard_map/all_to_all | solution.py:392
  19.8 0.7 copy-start.7
  72.8 30.5 %copy-start = (f32[2,384,512]{2,1,0:T(8,128)S(1)}, f32[2,384,512]{2,1,0:T(8,128)}, u32[]{:S(2)}) copy-start(f32[2,384,512]{2,1,0:T(8,128)} %perturb_ref.3) | copy-start | bytes 4718596
  72.8 30.5 %copy-start.5 = (f32[2,112,144]{2,1,0:T(8,128)S(1)}, f32[2,112,144]{2,1,0:T(8,128)}, u32[]{:S(2)}) copy-start(f32[2,112,144]{2,1,0:T(8,128)} %get-tuple-element.16.coarse_1_ref) | copy-start | bytes 387076
  99.1 14.9 %all-to-all-start.3 = ((f32[32,16,128]{2,1,0:T(8,128)}), f32[32,16,128]{2,1,0:T(8,128)S(1)}, u32[]{:S(2)}, u32[]{:S(2)}) async-start(f32[32,16,128]{2,1,0:T(8,128)} %get-tuple-element.14), calls=%async_computation.3 | async-start | bytes 524288 | tf_op jit(solution)/shard_map/all_to_all | solution.py:411
  103.4 0.9 copy-start.6
  106.0 1.2 copy-start.1
  154.6 15.7 %all-to-all-start.6 = ((f32[8,48,128]{2,1,0:T(8,128)}), f32[8,48,128]{2,1,0:T(8,128)S(1)}, u32[]{:S(2)}, u32[]{:S(2)}) async-start(f32[8,48,128]{2,1,0:T(8,128)} %broadcast_in_dim.16), calls=%async_computation.6 | async-start | bytes 393216 | tf_op jit(solution)/shard_map/all_to_all | solution.py:30
  170.3 4.9 %copy-start.2 = (f32[16,2,128]{2,1,0:T(2,128)S(1)}, f32[16,2,128]{2,1,0:T(2,128)}, u32[]{:S(2)}) copy-start(f32[16,2,128]{2,1,0:T(2,128)} %all_to_all.42.ends_ref) | copy-start | bytes 49156
  170.3 4.9 %copy-start.3 = (f32[2,400,640]{2,1,0:T(8,128)S(1)}, f32[2,400,640]{2,1,0:T(8,128)}, u32[]{:S(2)}) copy-start(f32[2,400,640]{2,1,0:T(8,128)} %get-tuple-element.19.total_1_ref) | copy-start | bytes 6144004
  171.3 12.5 %all-to-all-start.7 = ((f32[4,384,128]{2,1,0:T(8,128)}), f32[4,384,128]{2,1,0:T(8,128)S(1)}, u32[]{:S(2)}, u32[]{:S(2)}) async-start(f32[4,384,128]{2,1,0:T(8,128)} %broadcast_in_dim.17), calls=%async_computation.7 | async-start | bytes 1572864 | tf_op jit(solution)/shard_map/all_to_all | solution.py:30
  175.2 1.6 copy-start.4

commit v11 on v9

--- a/solution.py
+++ b/solution.py
@@ -397,7 +397,7 @@
     ends = sent_to_all(bent, TILES)
 
     field_rows = fine_lat * fine_lon // LANES
-    along_x = lax.axis_size(X)
+    along_x, along_z = lax.axis_size(X), lax.axis_size(Z)
     part_rows, piece_rows = field_rows // along_x, field_rows // groups
     part = (along_x, part_rows, LANES)
     fields = small_call(
@@ -411,8 +411,8 @@
         coarse_2,
     )
     field = small_call(join_kernel, (part,), 10**6, "join", ends, fields)
-    field = lax.all_to_all(field.reshape(groups, piece_rows, LANES), MEM, 0, 0, tiled=True)
-    field = jnp.sum(field, axis=0)
+    field = jnp.sum(lax.all_to_all(field, X, 0, 0, tiled=True), axis=0).reshape(along_z, piece_rows, LANES)
+    field = jnp.sum(lax.all_to_all(field, Z, 0, 0, tiled=True), axis=0)
     everything = sent_to_all(sent_to_all(field, Z).reshape(part_rows, LANES), X)
     whole = pl.BlockSpec(memory_space=pltpu.VMEM)
     analysis = pl.pallas_call(

time: 185 us -> 184 us (level)
  starting transfers between devices: 25.9 us -> 22.3 us
  blocking collectives: 74.3 us -> 77.2 us
    all_to_all x3, starting transfers between devices: 15.6 us -> 12 us  [sent_to_all(): return lax.all_to_all(copies, axis, split_axis=0, concat_axis=0, tiled=True)]
    all_to_all x1 -> x2, blocking collectives: 23.7 us -> 26.6 us  [the longest x1 14.6 us: per_device(): lax.all_to_all(field, X, 0, 0, tiled=True)]
where the time goes in v11:
time: 184 us; the launch traced here: 181 us
  blocking collectives  77.2 us (42%)
  Pallas kernels  35.7 us (19%)
  waiting for transfers between devices  30.6 us (17%)
  starting transfers between devices  22.3 us (12%)
  local copies, waits for them, and re-layouts  9.11 us (5%)
  matrix products  2.98 us (2%)
    all_to_all x2, blocking collectives, per_device(): mine = jnp.sum(lax.all_to_all(part, MEM, 0, 0, tiled=True), axis=0)  37.2 us
    pallas_call x2, Pallas kernels, sweep(): pl.pallas_call(functools.partial(sweep_kernel, first, scale, lon_tiles, m...  24.9 us
    all_to_all x3, waiting for transfers between devices, sent_to_all(): return lax.all_to_all(copies, axis, split_axis=0, concat_axis=0, tiled=True)  15.3 us
    all_to_all x1, waiting for transfers between devices, per_device(): known = lax.all_to_all(message, TILES, 0, 0, tiled=True)  15.2 us
    all_to_all x1, blocking collectives, per_device(): lax.all_to_all(field, X, 0, 0, tiled=True)  14.6 us
    all_to_all x1, blocking collectives, sent_to_all(): return lax.all_to_all(copies, axis, split_axis=0, concat_axis=0, tiled=True)  13.4 us
    all_to_all x3, starting transfers between devices, sent_to_all(): return lax.all_to_all(copies, axis, split_axis=0, concat_axis=0, tiled=True)  12 us
    all_to_all x1, blocking collectives, per_device(): field = jnp.sum(lax.all_to_all(field, Z, 0, 0, tiled=True), axis=0)  12 us
  transfers between devices with their start and end apart: 4, of which 4 were waited for; matrix products, arithmetic and copies ran while one was open for 3% of the time, Pallas kernels for 2%

profile of v11, /device:TPU:1, one launch (start us, length us, event | category | flops | bytes accessed | tf_op | source)
XLA Modules:
  0.0 180.7 jit_solution(13725853927435703762)
XLA Ops:
  1.3 0.0 copy-start.8
  1.3 6.1 %picked.1 = f32[16,80,128]{2,1,0:T(8,128)} custom-call(s32[1]{0:T(128)} %bitcast.17.count_ref, f32[2,384,512]{2,1,0:T(8,128)} %perturb_ref.3, s32[16,128]{1,0:T(8,128)} %bitcast.21, f32[16,128]{1,0:T(8,128)} %bitcast.22, f32[16,128]{1,0:T(8,128)} %bitcast.23), custom_call_target="tpu_custom_call" | custom-call | tf_op jit(solution)/shard_map/picked/pallas_call | solution.py:111
  7.3 10.3 %all-to-all-start = ((f32[16,80,128]{2,1,0:T(8,128)}), f32[16,80,128]{2,1,0:T(8,128)S(1)}, u32[]{:S(2)}, u32[]{:S(2)}) async-start(f32[16,80,128]{2,1,0:T(8,128)} %picked.1), calls=%async_computation | async-start | bytes 1310720 | tf_op jit(solution)/shard_map/all_to_all | solution.py:376
  17.6 0.0 copy-done.8
  17.6 0.1 power_select_fusion
  17.7 0.1 and_select_fusion
  17.8 2.0 %fusion.56 = (bf16[640,144]{0,1:T(8,128)(2,1)S(1)}, f32[640,144]{0,1:T(8,128)S(1)}) fusion(f32[512]{0:T(512)S(1)} %integer_pow.44, f32[144]{0:T(256)S(1)} %get-tuple-element.21, s32[144]{0:T(256)S(1)} %iota_add_fusion.2, f32[144]{0:T(256)S(1)} %get-tuple-element.20, f32[640]{0:T(1024)S(1)} %get-tuple-element.23, s32[640]{0:T(1024)S(1)} %iota_add_fusion, ...), kind=kOutput, calls=%fused_computation.79 | convolution fusion | flops 569133056 | bytes 564416 | tf_op jit(solution)/shard_map/ab,cb->ac/dot_general | solution.py:384
  19.8 0.0 copy-start.7
  19.9 0.2 copy.22.refs_4_.refs_5_
  20.0 0.2 copy.20
  20.3 0.2 copy-done.7
  20.5 0.1 and_select_fusion.1
  20.6 0.1 power_select_fusion.1
  20.7 1.0 fusion.55
  21.7 0.1 copy.21.refs_2_.refs_3_
  21.8 0.1 copy.18
  22.0 0.1 subtract_convert_fusion.refs_5_.refs_6_
  22.0 15.2 %all-to-all-done.refs_1_ = f32[16,80,128]{2,1,0:T(8,128)S(1)} async-done(((f32[16,80,128]{2,1,0:T(8,128)}), f32[16,80,128]{2,1,0:T(8,128)S(1)}, u32[]{:S(2)}, u32[]{:S(2)}) %all-to-all-start) | async-done | bytes 655392 | tf_op jit(solution)/shard_map/all_to_all | solution.py:376
  37.3 12.9 %sweep_first.1 = (f32[32,16,128]{2,1,0:T(8,128)S(1)}, f32[2,112,144]{2,1,0:T(8,128)}, f32[2,400,640]{2,1,0:T(8,128)}) custom-call(s32[1]{0:T(128)} %bitcast.refs_0_, f32[16,80,128]{2,1,0:T(8,128)S(1)} %all-to-all-done.refs_1_, bf16[112,400]{1,0:T(8,128)(2,1)S(1)} %copy.21.refs_2_.refs_3_, bf16[112,400]{1,0:T(8,128)(2,1)S(1)} %subtract_convert_fusion.1.refs_3_.refs_4_, ...), custom_call_target="tpu_custom_call" | custom-call | tf_op jit(solution)/shard_map/sweep_first/pallas_call | solution.py:279
  50.1 22.6 %all_to_all.45 = f32[32,16,128]{2,1,0:T(8,128)S(1)} all-to-all(f32[32,16,128]{2,1,0:T(8,128)S(1)} %get-tuple-element.10), channel_id=1, replica_groups=mesh['mem_0'=4,'mem_1'=8,'lat_0'=2,'lat_1'=2,'lon'=4] {'mem_0','mem_1'}, dimensions={0} | all-to-all | bytes 524288 | tf_op jit(solution)/shard_map/all_to_all | solution.py:390
  72.8 13.4 %all_to_all.46.refs_2_ = f32[16,16,128]{2,1,0:T(8,128)S(1)} all-to-all(f32[16,16,128]{2,1,0:T(8,128)S(1)} %broadcast_in_dim.14), channel_id=1, replica_groups=mesh['mem_0'=4,'mem_1'=8,'lat_0'=2,'lat_1'=2,'lon'=4] {'lat_0','lat_1','..., dimensions={0} | all-to-all | bytes 262144 | tf_op jit(solution)/shard_map/all_to_all | solution.py:30
  86.2 12.0 %sweep_second.1 = (f32[32,16,128]{2,1,0:T(8,128)S(1)}, f32[2,112,144]{2,1,0:T(8,128)}, f32[2,400,640]{2,1,0:T(8,128)}, f32[1,128]{1,0:T(1,128)S(1)}, f32[2,16,128]{2,1,0:T(8,128)S(1)}) custom-call(s32[1]{0:T(128)} %bitcast.refs_0_, f32[16,80,128]{2,1,0:T(8,128)S(1)} %all-to-all-done.refs_1_, f32[16,16,128]{2,1,0:T(8,128)S(1)} %all_to_all.46.refs_2_, ...), custom_call_target="tpu_custom_call" | custom-call | tf_op jit(solution)/shard_map/sweep_second/pallas_call | solution.py:279
  98.2 14.6 %all_to_all.47 = f32[32,16,128]{2,1,0:T(8,128)S(1)} all-to-all(f32[32,16,128]{2,1,0:T(8,128)S(1)} %get-tuple-element.12), channel_id=1, replica_groups=mesh['mem_0'=4,'mem_1'=8,'lat_0'=2,'lat_1'=2,'lon'=4] {'mem_0','mem_1'}, dimensions={0} | all-to-all | bytes 524288 | tf_op jit(solution)/shard_map/all_to_all | solution.py:395
  112.9 0.6 broadcast_in_dim.15
  113.5 5.2 %all-to-all-start.4 = ((f32[16,2,128]{2,1,0:T(2,128)}), f32[16,2,128]{2,1,0:T(2,128)S(1)}, u32[]{:S(2)}, u32[]{:S(2)}) async-start(f32[16,2,128]{2,1,0:T(2,128)} %broadcast_in_dim.15), calls=%async_computation.4 | async-start | bytes 32768 | tf_op jit(solution)/shard_map/all_to_all | solution.py:30
  118.7 0.9 copy-done.6
  119.6 1.7 fields.1.fields_ref
  121.3 1.2 copy-done.1
  122.5 3.5 %all-to-all-done.4.ends_ref = f32[16,2,128]{2,1,0:T(2,128)S(1)} async-done(((f32[16,2,128]{2,1,0:T(2,128)}), f32[16,2,128]{2,1,0:T(2,128)S(1)}, u32[]{:S(2)}, u32[]{:S(2)}) %all-to-all-start.4) | async-done | bytes 16416 | tf_op jit(solution)/shard_map/all_to_all | solution.py:30
  126.0 1.4 copy-done.2
  127.4 0.3 join.1
  127.7 14.6 %all_to_all.48 = f32[4,384,128]{2,1,0:T(8,128)S(1)} all-to-all(f32[4,384,128]{2,1,0:T(8,128)S(1)} %join.1), channel_id=1, replica_groups=mesh['mem_0'=4,'mem_1'=8,'lat_0'=2,'lat_1'=2,'lon'=4] {'mem_0'}, dimensions={0} | all-to-all | bytes 1572864 | tf_op jit(solution)/shard_map/all_to_all | solution.py:414
  142.3 12.0 %all_to_all.49 = f32[8,48,128]{2,1,0:T(8,128)S(1)} all-to-all(f32[8,48,128]{2,1,0:T(8,128)S(1)} %bitcast.19), channel_id=1, replica_groups=mesh['mem_0'=4,'mem_1'=8,'lat_0'=2,'lat_1'=2,'lon'=4] {'mem_1'}, dimensions={0} | all-to-all | bytes 393216 | tf_op jit(solution)/shard_map/all_to_all | solution.py:415
  154.3 0.7 broadcast_in_dim.16
  155.0 3.4 %all-to-all-start.7 = ((f32[8,48,128]{2,1,0:T(8,128)}), f32[8,48,128]{2,1,0:T(8,128)S(1)}, u32[]{:S(2)}, u32[]{:S(2)}) async-start(f32[8,48,128]{2,1,0:T(8,128)} %broadcast_in_dim.16), calls=%async_computation.7 | async-start | bytes 393216 | tf_op jit(solution)/shard_map/all_to_all | solution.py:30
  158.4 0.1 fusion.51
  158.5 0.1 fusion.31.left_ref
  158.7 8.4 %all-to-all-done.7 = f32[8,48,128]{2,1,0:T(8,128)S(1)} async-done(((f32[8,48,128]{2,1,0:T(8,128)}), f32[8,48,128]{2,1,0:T(8,128)S(1)}, u32[]{:S(2)}, u32[]{:S(2)}) %all-to-all-start.7) | async-done | bytes 196640 | tf_op jit(solution)/shard_map/all_to_all | solution.py:30
  167.1 0.9 broadcast_in_dim.17
  168.0 3.5 %all-to-all-start.8 = ((f32[4,384,128]{2,1,0:T(8,128)}), f32[4,384,128]{2,1,0:T(8,128)S(1)}, u32[]{:S(2)}, u32[]{:S(2)}) async-start(f32[4,384,128]{2,1,0:T(8,128)} %broadcast_in_dim.17), calls=%async_computation.8 | async-start | bytes 1572864 | tf_op jit(solution)/shard_map/all_to_all | solution.py:30
  171.5 0.1 fusion.52
  171.6 0.3 fusion.16.right_ref
  171.9 0.0 copy-done.3
  171.9 0.0 copy-start.4
  171.9 1.6 copy-done.4
  173.5 2.8 %analysis.1 = f32[2,96,128]{2,1,0:T(8,128)} custom-call(f32[1,128]{1,0:T(1,128)S(1)} %get-tuple-element.11.length_ref, f32[16,2,128]{2,1,0:T(2,128)S(1)} %all-to-all-done.4.ends_ref, f32[2,400,640]{2,1,0:T(8,128)S(1)} %copy-done.3, f32[2,400,640]{2,1,0:T(8,128)S(1)} %copy-done.4, f32[96,400]{1,0:T(8,128)S(1)} %fusion.31.left_ref, ...), custom_call_target="tpu_custom_call" | custom-call | flops 2000000000 | bytes 5000000 | tf_op jit(solution)/shard_map/analysis/pallas_call | solution.py:418
  176.3 3.5 %all-to-all-done.8 = f32[4,384,128]{2,1,0:T(8,128)S(1)} async-done(((f32[4,384,128]{2,1,0:T(8,128)}), f32[4,384,128]{2,1,0:T(8,128)S(1)}, u32[]{:S(2)}, u32[]{:S(2)}) %all-to-all-start.8) | async-done | bytes 786464 | tf_op jit(solution)/shard_map/all_to_all | solution.py:30
  179.8 0.9 copy.27
  (24 shorter events, 0.2 us)
Async XLA Ops:
  1.3 16.3 %copy-start.8 = (f32[512]{0:T(512)S(1)}, f32[512]{0:T(512)}, u32[]{:S(2)}) copy-start(f32[512]{0:T(512)} %param.9) | copy-start | bytes 6148
  7.3 29.9 %all-to-all-start = ((f32[16,80,128]{2,1,0:T(8,128)}), f32[16,80,128]{2,1,0:T(8,128)S(1)}, u32[]{:S(2)}, u32[]{:S(2)}) async-start(f32[16,80,128]{2,1,0:T(8,128)} %picked.1), calls=%async_computation | async-start | bytes 1310720 | tf_op jit(solution)/shard_map/all_to_all | solution.py:376
  19.8 0.7 copy-start.7
  86.2 32.4 %copy-start = (f32[2,384,512]{2,1,0:T(8,128)S(1)}, f32[2,384,512]{2,1,0:T(8,128)}, u32[]{:S(2)}) copy-start(f32[2,384,512]{2,1,0:T(8,128)} %perturb_ref.3) | copy-start | bytes 4718596
  86.2 32.4 %copy-start.5 = (f32[2,112,144]{2,1,0:T(8,128)S(1)}, f32[2,112,144]{2,1,0:T(8,128)}, u32[]{:S(2)}) copy-start(f32[2,112,144]{2,1,0:T(8,128)} %get-tuple-element.16.coarse_1_ref) | copy-start | bytes 387076
  113.5 12.5 %all-to-all-start.4 = ((f32[16,2,128]{2,1,0:T(2,128)}), f32[16,2,128]{2,1,0:T(2,128)S(1)}, u32[]{:S(2)}, u32[]{:S(2)}) async-start(f32[16,2,128]{2,1,0:T(2,128)} %broadcast_in_dim.15), calls=%async_computation.4 | async-start | bytes 32768 | tf_op jit(solution)/shard_map/all_to_all | solution.py:30
  118.7 0.9 copy-start.6
  121.3 1.2 copy-start.1
  125.9 1.4 copy-start.2
  155.0 12.0 %all-to-all-start.7 = ((f32[8,48,128]{2,1,0:T(8,128)}), f32[8,48,128]{2,1,0:T(8,128)S(1)}, u32[]{:S(2)}, u32[]{:S(2)}) async-start(f32[8,48,128]{2,1,0:T(8,128)} %broadcast_in_dim.16), calls=%async_computation.7 | async-start | bytes 393216 | tf_op jit(solution)/shard_map/all_to_all | solution.py:30
  167.1 4.9 %copy-start.3 = (f32[2,400,640]{2,1,0:T(8,128)S(1)}, f32[2,400,640]{2,1,0:T(8,128)}, u32[]{:S(2)}) copy-start(f32[2,400,640]{2,1,0:T(8,128)} %get-tuple-element.14.total_1_ref) | copy-start | bytes 6144004
  168.0 11.8 %all-to-all-start.8 = ((f32[4,384,128]{2,1,0:T(8,128)}), f32[4,384,128]{2,1,0:T(8,128)S(1)}, u32[]{:S(2)}, u32[]{:S(2)}) async-start(f32[4,384,128]{2,1,0:T(8,128)} %broadcast_in_dim.17), calls=%async_computation.8 | async-start | bytes 1572864 | tf_op jit(solution)/shard_map/all_to_all | solution.py:30
  171.9 1.6 copy-start.4
